TPU v7x, 256 devices: a whole 4x4x8 slice. The times are simulated.
256 devices in a mesh: sta: 32 (over y, z), tpl: 8 (over x, core).
Axes of the slice: x: 4, y: 4, z: 8, core: 2. Of those that a mesh axis runs over, the one named last changes fastest.
Arguments:
- station_data: float32 [3, 512, 3200], P(None, ('sta', 'tpl'))
- channel_mask: int32 [3, 512], P(None, 'sta'), may hold values 0 or 1
- template_waves: bfloat16 [256, 32, 3, 640], P('tpl', 'sta')
- pick_station: int32 [256, 32], P('tpl'), may hold values from 0 to 511, as said below
- pick_lag: int32 [256, 32], P('tpl'), may hold values from 0 to 1024, as said below
Outputs:
- network_stack: float32 [1536, 256], P('sta', 'tpl')
Inputs may be any that keep to these rules, and one draw needn't show every extreme that they name: `pick_station`: the 32 picks of a template lie on distinct stations. Within each aligned block of 32 templates and for each pick index p, at most 4 templates have pick p on one aligned block of 16 stations; for every p this is reached on some block of stations. `pick_lag`: every template has a pick at lag 0 and a pick at lag 1024.
All inputs are finite; a program needn't handle non-finite values. No bound on the sum of `channel_mask` on one device may be relied on, other than what follows from the above.
Results may differ from a plain program's by a relative error of at most 0.0041.
Values may be sent and summed in bfloat16 or wider, within the bound.
No kernel may reach another device: no remote copies, remote signals or barrier semaphores. Data moves between devices by JAX's collectives and lax.ppermute only.
A program may use at most 64 MiB of HBM per device.

v0:
```python
import jax
import jax.numpy as jnp
from jax import lax
from jax.sharding import PartitionSpec as P

NT = 1536
L = 640
LAGS = 1024
BLOCK = 128


epsilon = 1e-05


def window_scales(samples):
    leading = jnp.zeros(samples.shape[:-1] + (1,), jnp.float32)
    sum_one = jnp.concatenate([leading, jnp.cumsum(samples, axis=-1)], axis=-1)
    sum_two = jnp.concatenate([leading, jnp.cumsum(samples * samples, axis=-1)], axis=-1)
    starts = NT + LAGS
    mean_one = (sum_one[..., L : L + starts] - sum_one[..., :starts]) / L
    mean_two = (sum_two[..., L : L + starts] - sum_two[..., :starts]) / L
    return 1.0 / (L * jnp.sqrt(mean_two - mean_one * mean_one + epsilon))


def unit_waves(raw_waves):
    values = raw_waves.astype(jnp.float32)
    centred = values - jnp.mean(values, axis=-1, keepdims=True)
    spread = jnp.sqrt(jnp.mean(centred * centred, axis=-1, keepdims=True) + epsilon)
    return (centred / spread).astype(jnp.bfloat16)


def toeplitz_rows(units):
    batch = units.shape[0]
    row_width = units.shape[1] + BLOCK
    padded = jnp.concatenate([units, jnp.zeros((batch, BLOCK), units.dtype)], axis=1)
    tiled = jnp.tile(padded, (1, BLOCK))
    trimmed = tiled[:, : BLOCK * (row_width - 1)].reshape(batch, BLOCK, row_width - 1)
    return jnp.concatenate([trimmed, jnp.zeros((batch, BLOCK, 1), units.dtype)], axis=2)


def frames_of(windows):
    batch, length = windows.shape
    row_total = (length - L) // BLOCK
    columns = [
        windows[:, BLOCK * offset : BLOCK * offset + row_total * BLOCK].reshape(
            batch, row_total, BLOCK
        )
        for offset in range((L + BLOCK) // BLOCK)
    ]
    return jnp.concatenate(columns, axis=2)


def correlate(windows, units):
    product = jnp.einsum(
        "bim,bjm->bij", frames_of(windows), toeplitz_rows(units), preferred_element_type=jnp.float32
    )
    return product.reshape(windows.shape[0], -1)


def body(station_data, channel_mask, template_waves, pick_station, pick_lag):
    gathered = lax.all_gather(station_data, "tpl", axis=1, tiled=True)
    scales = window_scales(gathered)
    rounded = gathered.astype(jnp.bfloat16)
    group_size = pick_station.shape[0]
    station_count = rounded.shape[1]
    peer_count = lax.axis_size("sta")
    my_index = lax.axis_index("sta")
    capacity = max(2, group_size // 8)
    slot_count = peer_count * capacity
    owners = pick_station // station_count
    landing = (owners == my_index).astype(jnp.int32)
    arrival = jnp.cumsum(landing, axis=0) - 1
    source = lax.broadcasted_iota(jnp.int32, owners.shape, 1)
    slot_grid = jnp.where(landing == 1, source * capacity + arrival, slot_count)
    slot_index = slot_grid.reshape(-1)
    template_ids = lax.broadcasted_iota(jnp.int32, owners.shape, 0).reshape(-1)
    slot_template = (
        jnp.full((slot_count,), -1, jnp.int32).at[slot_index].set(template_ids, mode="drop")
    )
    slot_station = (
        jnp.zeros((slot_count,), jnp.int32)
        .at[slot_index]
        .set((pick_station - my_index * station_count).reshape(-1), mode="drop")
    )
    slot_lag = (
        jnp.zeros((slot_count,), jnp.int32).at[slot_index].set(pick_lag.reshape(-1), mode="drop")
    )
    own_owner = lax.dynamic_index_in_dim(owners, my_index, 1, keepdims=False)
    peers = lax.broadcasted_iota(jnp.int32, (group_size, peer_count), 1)
    hits = (own_owner[:, None] == peers).astype(jnp.int32)
    place = jnp.sum((jnp.cumsum(hits, axis=0) - 1) * hits, axis=1)
    outgoing = (
        jnp.zeros((peer_count, capacity, 3, L), jnp.bfloat16)
        .at[own_owner, place]
        .set(template_waves[:, 0])
    )
    received = lax.all_to_all(outgoing, "sta", split_axis=0, concat_axis=0, tiled=True)
    slot_waves = received.reshape(slot_count, 3, L)
    per_turn = 16
    turn_count = slot_count // per_turn
    units = unit_waves(slot_waves)
    weights = channel_mask.astype(jnp.float32)

    def one_turn(inputs):
        unit_turn, station_turn, lag_turn = inputs

        def take_window(station, lag_here):
            zero_start = jnp.zeros((), jnp.int32)
            window = lax.dynamic_slice(rounded, (zero_start, station, lag_here), (3, 1, NT + L))[
                :, 0
            ]
            scale_rows = lax.dynamic_slice(scales, (zero_start, station, lag_here), (3, 1, NT))[
                :, 0
            ]
            available = lax.dynamic_slice(weights, (zero_start, station), (3, 1))
            return (window, scale_rows * available)

        windows, factors = jax.vmap(take_window)(station_turn, lag_turn)
        correlation = correlate(windows.reshape(-1, NT + L), unit_turn.reshape(-1, L))
        return jnp.sum((correlation * factors.reshape(-1, NT)).reshape(per_turn, 3, NT), axis=1)

    per_slot = lax.map(
        one_turn,
        (
            units.reshape(turn_count, per_turn, 3, L),
            slot_station.reshape(turn_count, per_turn),
            slot_lag.reshape(turn_count, per_turn),
        ),
    ).reshape(slot_count, NT)
    template_cols = lax.broadcasted_iota(jnp.int32, (slot_count, group_size), 1)
    selector = (slot_template[:, None] == template_cols).astype(jnp.float32)
    return lax.psum_scatter(
        jnp.einsum("sn,st->nt", per_slot, selector, precision=lax.Precision.HIGHEST),
        "sta",
        scatter_dimension=0,
        tiled=True,
    )


def solution(mesh):
    in_specs = (
        P(None, ("sta", "tpl"), None),
        P(None, "sta"),
        P("tpl", "sta", None, None),
        P("tpl", None),
        P("tpl", None),
    )
    out_specs = P("sta", "tpl")
    return jax.shard_map(body, mesh=mesh, in_specs=in_specs, out_specs=out_specs, check_vma=False)
```

profile of v0, /device:TPU:2, one launch (start us, length us, event | category | flops | bytes accessed | tf_op | source)
XLA Modules:
  0.0 1406.8 jit_solution(13901518537665854714)
XLA Ops:
  85.9 1094.6 %while.16 = (s32[]{:T(128)}, f32[8,16,1536]{2,1,0:T(8,128)}, s32[8,16]{1,0:T(8,128)S(1)}, s32[8,16]{1,0:T(8,128)S(1)}, bf16[3,16,3200]{2,0,1:T(4,128)(2,1)}, /*i...) while((s32[]{:T(128)}, f32[8,16,1536]{2,1,0:T(8,128)}, ...), condition=%wide.region_14.15_spmd, body=%wide.region_12.14_spmd.sunk | while | flops 113443120 | bytes 85041648 | solution.py:122
  86.2 44.0 %while.17 = (s32[]{:T(128)}, bf16[3,16,3200]{2,0,1:T(4,128)(2,1)}, s32[16,3]{0,1:T(4,128)S(1)}, bf16[16,3,1,2176]{3,1,2,0:T(4,128)(2,1)S(1)}, s32[]{:T(128)}) while((s32[]{:T(128)}, bf16[3,16,3200]{2,0,1:T(4,128)(2,1)}, s32[16,3]{0,1:T(4,128)S(1)}, bf16[16,3,1,2176]{3,1,2,0:T(4,128)(2,1)S(1)}, s32[]{:T(128)}) %tuple.75), condition=%wide.while_cond, body=%wide.while_body.sunk | while | flops 2 | bytes 30581 | solution.py:109
  156.8 23.0 %reshape.371 = bf16[48,128,767]{2,1,0:T(8,128)(2,1)} reshape(bf16[48,98176]{1,0:T(8,128)(2,1)} %slice.155) | data formatting | bytes 18849792 | tf_op jit(solution)/shard_map/while/body/eval_jaxpr/reshape | solution.py:37
  185.0 36.2 %while.18 = (s32[]{:T(128)}, f32[3,16,2560]{2,1,0:T(8,128)S(1)}, s32[16,3]{0,1:T(4,128)S(1)}, f32[16,3,1,1536]{3,0,2,1:T(8,128)S(1)}, s32[]{:T(128)}, /*index=5*/s32[]{:T(128)}) while((s32[]{:T(128)}, f32[3,16,2560]{2,1,0:T(8,128)S(1)}, s32[16,3]{0,1:T(4,128)S(1)}, f32[16,3,1,1536]{3,0,2,1:T(8,128)S(1)}, s32[]{:T(128)}, /*index=5*/s32[]{:T(128)}) %tuple.78), condition=%wide.while_cond.1, body=%wide.while_body.1.sunk | while | flops 2 | bytes 73853 | solution.py:112
  223.0 44.0 %while.17 = (s32[]{:T(128)}, bf16[3,16,3200]{2,0,1:T(4,128)(2,1)}, s32[16,3]{0,1:T(4,128)S(1)}, bf16[16,3,1,2176]{3,1,2,0:T(4,128)(2,1)S(1)}, s32[]{:T(128)}) while((s32[]{:T(128)}, bf16[3,16,3200]{2,0,1:T(4,128)(2,1)}, s32[16,3]{0,1:T(4,128)S(1)}, bf16[16,3,1,2176]{3,1,2,0:T(4,128)(2,1)S(1)}, s32[]{:T(128)}) %tuple.75), condition=%wide.while_cond, body=%wide.while_body.sunk | while | flops 2 | bytes 30581 | solution.py:109
  293.6 23.0 %reshape.371 = bf16[48,128,767]{2,1,0:T(8,128)(2,1)} reshape(bf16[48,98176]{1,0:T(8,128)(2,1)} %slice.155) | data formatting | bytes 18849792 | tf_op jit(solution)/shard_map/while/body/eval_jaxpr/reshape | solution.py:37
  321.8 36.2 %while.18 = (s32[]{:T(128)}, f32[3,16,2560]{2,1,0:T(8,128)S(1)}, s32[16,3]{0,1:T(4,128)S(1)}, f32[16,3,1,1536]{3,0,2,1:T(8,128)S(1)}, s32[]{:T(128)}, /*index=5*/s32[]{:T(128)}) while((s32[]{:T(128)}, f32[3,16,2560]{2,1,0:T(8,128)S(1)}, s32[16,3]{0,1:T(4,128)S(1)}, f32[16,3,1,1536]{3,0,2,1:T(8,128)S(1)}, s32[]{:T(128)}, /*index=5*/s32[]{:T(128)}) %tuple.78), condition=%wide.while_cond.1, body=%wide.while_body.1.sunk | while | flops 2 | bytes 73853 | solution.py:112
  359.8 44.0 %while.17 = (s32[]{:T(128)}, bf16[3,16,3200]{2,0,1:T(4,128)(2,1)}, s32[16,3]{0,1:T(4,128)S(1)}, bf16[16,3,1,2176]{3,1,2,0:T(4,128)(2,1)S(1)}, s32[]{:T(128)}) while((s32[]{:T(128)}, bf16[3,16,3200]{2,0,1:T(4,128)(2,1)}, s32[16,3]{0,1:T(4,128)S(1)}, bf16[16,3,1,2176]{3,1,2,0:T(4,128)(2,1)S(1)}, s32[]{:T(128)}) %tuple.75), condition=%wide.while_cond, body=%wide.while_body.sunk | while | flops 2 | bytes 30581 | solution.py:109
  430.4 23.0 %reshape.371 = bf16[48,128,767]{2,1,0:T(8,128)(2,1)} reshape(bf16[48,98176]{1,0:T(8,128)(2,1)} %slice.155) | data formatting | bytes 18849792 | tf_op jit(solution)/shard_map/while/body/eval_jaxpr/reshape | solution.py:37
  458.6 36.2 %while.18 = (s32[]{:T(128)}, f32[3,16,2560]{2,1,0:T(8,128)S(1)}, s32[16,3]{0,1:T(4,128)S(1)}, f32[16,3,1,1536]{3,0,2,1:T(8,128)S(1)}, s32[]{:T(128)}, /*index=5*/s32[]{:T(128)}) while((s32[]{:T(128)}, f32[3,16,2560]{2,1,0:T(8,128)S(1)}, s32[16,3]{0,1:T(4,128)S(1)}, f32[16,3,1,1536]{3,0,2,1:T(8,128)S(1)}, s32[]{:T(128)}, /*index=5*/s32[]{:T(128)}) %tuple.78), condition=%wide.while_cond.1, body=%wide.while_body.1.sunk | while | flops 2 | bytes 73853 | solution.py:112
  496.5 44.0 %while.17 = (s32[]{:T(128)}, bf16[3,16,3200]{2,0,1:T(4,128)(2,1)}, s32[16,3]{0,1:T(4,128)S(1)}, bf16[16,3,1,2176]{3,1,2,0:T(4,128)(2,1)S(1)}, s32[]{:T(128)}) while((s32[]{:T(128)}, bf16[3,16,3200]{2,0,1:T(4,128)(2,1)}, s32[16,3]{0,1:T(4,128)S(1)}, bf16[16,3,1,2176]{3,1,2,0:T(4,128)(2,1)S(1)}, s32[]{:T(128)}) %tuple.75), condition=%wide.while_cond, body=%wide.while_body.sunk | while | flops 2 | bytes 30581 | solution.py:109
  567.2 23.0 %reshape.371 = bf16[48,128,767]{2,1,0:T(8,128)(2,1)} reshape(bf16[48,98176]{1,0:T(8,128)(2,1)} %slice.155) | data formatting | bytes 18849792 | tf_op jit(solution)/shard_map/while/body/eval_jaxpr/reshape | solution.py:37
  595.4 36.2 %while.18 = (s32[]{:T(128)}, f32[3,16,2560]{2,1,0:T(8,128)S(1)}, s32[16,3]{0,1:T(4,128)S(1)}, f32[16,3,1,1536]{3,0,2,1:T(8,128)S(1)}, s32[]{:T(128)}, /*index=5*/s32[]{:T(128)}) while((s32[]{:T(128)}, f32[3,16,2560]{2,1,0:T(8,128)S(1)}, s32[16,3]{0,1:T(4,128)S(1)}, f32[16,3,1,1536]{3,0,2,1:T(8,128)S(1)}, s32[]{:T(128)}, /*index=5*/s32[]{:T(128)}) %tuple.78), condition=%wide.while_cond.1, body=%wide.while_body.1.sunk | while | flops 2 | bytes 73853 | solution.py:112
  633.4 44.0 %while.17 = (s32[]{:T(128)}, bf16[3,16,3200]{2,0,1:T(4,128)(2,1)}, s32[16,3]{0,1:T(4,128)S(1)}, bf16[16,3,1,2176]{3,1,2,0:T(4,128)(2,1)S(1)}, s32[]{:T(128)}) while((s32[]{:T(128)}, bf16[3,16,3200]{2,0,1:T(4,128)(2,1)}, s32[16,3]{0,1:T(4,128)S(1)}, bf16[16,3,1,2176]{3,1,2,0:T(4,128)(2,1)S(1)}, s32[]{:T(128)}) %tuple.75), condition=%wide.while_cond, body=%wide.while_body.sunk | while | flops 2 | bytes 30581 | solution.py:109
  732.2 36.2 %while.18 = (s32[]{:T(128)}, f32[3,16,2560]{2,1,0:T(8,128)S(1)}, s32[16,3]{0,1:T(4,128)S(1)}, f32[16,3,1,1536]{3,0,2,1:T(8,128)S(1)}, s32[]{:T(128)}, /*index=5*/s32[]{:T(128)}) while((s32[]{:T(128)}, f32[3,16,2560]{2,1,0:T(8,128)S(1)}, s32[16,3]{0,1:T(4,128)S(1)}, f32[16,3,1,1536]{3,0,2,1:T(8,128)S(1)}, s32[]{:T(128)}, /*index=5*/s32[]{:T(128)}) %tuple.78), condition=%wide.while_cond.1, body=%wide.while_body.1.sunk | while | flops 2 | bytes 73853 | solution.py:112
  770.2 44.0 %while.17 = (s32[]{:T(128)}, bf16[3,16,3200]{2,0,1:T(4,128)(2,1)}, s32[16,3]{0,1:T(4,128)S(1)}, bf16[16,3,1,2176]{3,1,2,0:T(4,128)(2,1)S(1)}, s32[]{:T(128)}) while((s32[]{:T(128)}, bf16[3,16,3200]{2,0,1:T(4,128)(2,1)}, s32[16,3]{0,1:T(4,128)S(1)}, bf16[16,3,1,2176]{3,1,2,0:T(4,128)(2,1)S(1)}, s32[]{:T(128)}) %tuple.75), condition=%wide.while_cond, body=%wide.while_body.sunk | while | flops 2 | bytes 30581 | solution.py:109
  840.8 23.0 %reshape.371 = bf16[48,128,767]{2,1,0:T(8,128)(2,1)} reshape(bf16[48,98176]{1,0:T(8,128)(2,1)} %slice.155) | data formatting | bytes 18849792 | tf_op jit(solution)/shard_map/while/body/eval_jaxpr/reshape | solution.py:37
  869.0 36.2 %while.18 = (s32[]{:T(128)}, f32[3,16,2560]{2,1,0:T(8,128)S(1)}, s32[16,3]{0,1:T(4,128)S(1)}, f32[16,3,1,1536]{3,0,2,1:T(8,128)S(1)}, s32[]{:T(128)}, /*index=5*/s32[]{:T(128)}) while((s32[]{:T(128)}, f32[3,16,2560]{2,1,0:T(8,128)S(1)}, s32[16,3]{0,1:T(4,128)S(1)}, f32[16,3,1,1536]{3,0,2,1:T(8,128)S(1)}, s32[]{:T(128)}, /*index=5*/s32[]{:T(128)}) %tuple.78), condition=%wide.while_cond.1, body=%wide.while_body.1.sunk | while | flops 2 | bytes 73853 | solution.py:112
  906.9 44.0 %while.17 = (s32[]{:T(128)}, bf16[3,16,3200]{2,0,1:T(4,128)(2,1)}, s32[16,3]{0,1:T(4,128)S(1)}, bf16[16,3,1,2176]{3,1,2,0:T(4,128)(2,1)S(1)}, s32[]{:T(128)}) while((s32[]{:T(128)}, bf16[3,16,3200]{2,0,1:T(4,128)(2,1)}, s32[16,3]{0,1:T(4,128)S(1)}, bf16[16,3,1,2176]{3,1,2,0:T(4,128)(2,1)S(1)}, s32[]{:T(128)}) %tuple.75), condition=%wide.while_cond, body=%wide.while_body.sunk | while | flops 2 | bytes 30581 | solution.py:109
  977.6 23.0 %reshape.371 = bf16[48,128,767]{2,1,0:T(8,128)(2,1)} reshape(bf16[48,98176]{1,0:T(8,128)(2,1)} %slice.155) | data formatting | bytes 18849792 | tf_op jit(solution)/shard_map/while/body/eval_jaxpr/reshape | solution.py:37
  1005.8 36.2 %while.18 = (s32[]{:T(128)}, f32[3,16,2560]{2,1,0:T(8,128)S(1)}, s32[16,3]{0,1:T(4,128)S(1)}, f32[16,3,1,1536]{3,0,2,1:T(8,128)S(1)}, s32[]{:T(128)}, /*index=5*/s32[]{:T(128)}) while((s32[]{:T(128)}, f32[3,16,2560]{2,1,0:T(8,128)S(1)}, s32[16,3]{0,1:T(4,128)S(1)}, f32[16,3,1,1536]{3,0,2,1:T(8,128)S(1)}, s32[]{:T(128)}, /*index=5*/s32[]{:T(128)}) %tuple.78), condition=%wide.while_cond.1, body=%wide.while_body.1.sunk | while | flops 2 | bytes 73853 | solution.py:112
  1043.8 44.0 %while.17 = (s32[]{:T(128)}, bf16[3,16,3200]{2,0,1:T(4,128)(2,1)}, s32[16,3]{0,1:T(4,128)S(1)}, bf16[16,3,1,2176]{3,1,2,0:T(4,128)(2,1)S(1)}, s32[]{:T(128)}) while((s32[]{:T(128)}, bf16[3,16,3200]{2,0,1:T(4,128)(2,1)}, s32[16,3]{0,1:T(4,128)S(1)}, bf16[16,3,1,2176]{3,1,2,0:T(4,128)(2,1)S(1)}, s32[]{:T(128)}) %tuple.75), condition=%wide.while_cond, body=%wide.while_body.sunk | while | flops 2 | bytes 30581 | solution.py:109
  1142.6 36.2 %while.18 = (s32[]{:T(128)}, f32[3,16,2560]{2,1,0:T(8,128)S(1)}, s32[16,3]{0,1:T(4,128)S(1)}, f32[16,3,1,1536]{3,0,2,1:T(8,128)S(1)}, s32[]{:T(128)}, /*index=5*/s32[]{:T(128)}) while((s32[]{:T(128)}, f32[3,16,2560]{2,1,0:T(8,128)S(1)}, s32[16,3]{0,1:T(4,128)S(1)}, f32[16,3,1,1536]{3,0,2,1:T(8,128)S(1)}, s32[]{:T(128)}, /*index=5*/s32[]{:T(128)}) %tuple.78), condition=%wide.while_cond.1, body=%wide.while_body.1.sunk | while | flops 2 | bytes 73853 | solution.py:112
  1183.4 215.1 %reduce-scatter.4.cloned.1.call-done = f32[48,32]{1,0:T(8,128)} async-done(((f32[1536,32]{1,0:T(8,128)}), f32[48,32]{1,0:T(8,128)}) %reduce-scatter.4.cloned.1.call-update) | async-done | bytes 6160
  (1220 shorter events, 1031.8 us)
Async XLA Ops:
  11.1 12.6 copy-start
  11.1 12.6 copy-start.1
  12.1 71.6 %all-to-all-start = ((bf16[32,4,3,640]{3,1,2,0:T(4,128)(2,1)}), bf16[32,4,3,640]{3,1,2,0:T(4,128)(2,1)S(1)}, u32[]{:S(2)}, u32[]{:S(2)}) async-start(bf16[32,4,3,640]{3,1,2,0:T(4,128)(2,1)} %copy.67), calls=%async_computation | async-start | bytes 983040 | tf_op jit(solution)/shard_map/all_to_all | solution.py:97
  23.6 1374.9 %reduce-scatter.4.cloned.1.call-start = ((), (), s32[]{:S(2)}) async-start(), calls=%async_computation.2 | async-start | bytes 811008
  73.4 0.7 copy-start.2
  73.4 5.2 copy-start.3
Sparse Core Ops, SparseCore 0:
  1183.5 214.9 reduce-scatter.3
where the time goes:
time: 1420 us; the launch traced here: 1410 us
  local copies, waits for them, and re-layouts  1060 us (75%)
  waiting for transfers between devices  215 us (15%)
  matrix products  43.6 us (3%)
  other arithmetic  37 us (3%)
    gather x896, local copies, waits for them, and re-layouts  635 us
    unnamed x2, waiting for transfers between devices  215 us
    reshape x8, local copies, waits for them, and re-layouts, toeplitz_rows(): tiled[:, :BLOCK * (row_width - 1)].reshape(batch, BLOCK, row_width - 1)  184 us
    while x48, local copies, waits for them, and re-layouts  105 us
    slice x8, local copies, waits for them, and re-layouts, toeplitz_rows(): tiled[:, :BLOCK * (row_width - 1)].reshape(batch, BLOCK, row_width - 1)  63.4 us
    dot_general x8, matrix products, correlate(): jnp.einsum('bim,bjm->bij', frames_of(windows), toeplitz_rows(units), pref...  40.7 us
    another operation x8, local copies, waits for them, and re-layouts, toeplitz_rows(): tiled = jnp.tile(padded, (1, BLOCK))  34.2 us
    another operation x6, other arithmetic  29.3 us
  transfers between devices with their start and end apart: 2, of which 1 were waited for; matrix products, arithmetic and copies ran while one was open for 3% of the time, Pallas kernels for 0%

commit v1 on v0

v1 whole, which is shorter than its diff:
```python
import jax
import jax.numpy as jnp
from jax import lax
from jax.experimental import pallas as pl
from jax.experimental.pallas import tpu as pltpu
from jax.sharding import PartitionSpec as P

NT = 1536
L = 640
LAGS = 1024
SAMPLES = 3200
CAP = 4
STEP = 32
LANES = 128
BLOCKS = SAMPLES // STEP
OUT_BLOCKS = NT // STEP
TILES = L // LANES
DEPTH = L + LANES
EPSILON = 1e-05
VALID = 1 << 20


def exclusive_prefix(values):
    groups = values.reshape(STEP // 8, 8, values.shape[-1])
    row = lax.broadcasted_iota(jnp.int32, groups.shape, 1)
    total = groups
    for shift in (1, 2, 4):
        total = total + jnp.where(row >= shift, pltpu.roll(total, shift, 1), 0.0)
    inner = jnp.where(row >= 1, pltpu.roll(total, 1, 1), 0.0)
    pieces = [inner[0]]
    carry = total[0, 7:8]
    for group in range(1, STEP // 8):
        pieces.append(inner[group] + carry)
        carry = carry + total[group, 7:8]
    return jnp.concatenate(pieces, axis=0)


def window_sums(values):
    width = values.shape[-1]
    span = L // STEP
    ahead = pltpu.roll(values, width - span, 1) - values
    two = jnp.sum(values, axis=0, keepdims=True)
    two = two + pltpu.roll(two, width - 1, 1)
    four = two + pltpu.roll(two, width - 2, 1)
    eight = four + pltpu.roll(four, width - 4, 1)
    sixteen = eight + pltpu.roll(eight, width - 8, 1)
    whole = sixteen + pltpu.roll(four, width - 16, 1)
    return whole + exclusive_prefix(ahead)


def kernel(meta_ref, mask_ref, tiles_ref, waves_ref, out_ref,
           frames, scales, units, acc, twice, dense, slots):
    peers = meta_ref.shape[1]

    def list_slot(slot, count):
        slots[count] = slot
        held = meta_ref[slot & (CAP - 1), slot >> 2] >> 20
        return count + held

    count = lax.fori_loop(0, peers * CAP, list_slot, jnp.int32(0))

    @pl.loop(0, peers * CAP // 16)
    def _(chunk):
        rows = pl.ds(pl.multiple_of(chunk * 16, 16), 16)
        for c in range(3):
            values = waves_ref[rows, c * L:(c + 1) * L].astype(jnp.float32)
            centred = values - jnp.mean(values, axis=-1, keepdims=True)
            power = jnp.mean(centred * centred, axis=-1, keepdims=True)
            unit = centred / jnp.sqrt(power + EPSILON)
            unit = unit.astype(jnp.bfloat16).astype(jnp.float32)
            for tile in range(TILES):
                units[c * TILES + tile, rows, :] = unit[:, tile * LANES:(tile + 1) * LANES]

    @pl.loop(0, tiles_ref.shape[0])
    def _(record):
        tile = tiles_ref[record]
        for turn in range(DEPTH // STEP):
            rolled = tile if turn == 0 else pltpu.roll(tile, LANES - turn, 1)
            frames[record, turn * STEP:(turn + 1) * STEP, :] = rolled.astype(jnp.bfloat16)
        mean_one = window_sums(tile) * (1.0 / L)
        mean_two = window_sums(tile * tile) * (1.0 / L)
        within = lax.rem(record, 6)
        station = (record // 6) * 2 + (within & 1)
        weight = mask_ref[within >> 1, station].astype(jnp.float32)
        spread = L * jnp.sqrt(mean_two - mean_one * mean_one + EPSILON)
        scales[record] = weight / spread

    acc[...] = jnp.zeros_like(acc)
    row = lax.broadcasted_iota(jnp.int32, (STEP, LANES), 0)
    lane = lax.broadcasted_iota(jnp.int32, (STEP, LANES), 1)
    own = lane >= row
    lane_used = lane < BLOCKS - L // STEP

    @pl.loop(0, count)
    def _(index):
        slot = slots[index]
        packed = meta_ref[slot & (CAP - 1), slot >> 2]
        template = packed & 31
        station = (packed >> 5) & 15
        lag = (packed >> 9) & 2047
        total = jnp.zeros((STEP, LANES), jnp.float32)
        for c in range(3):
            record = (station >> 1) * 6 + 2 * c + (station & 1)
            before = jnp.zeros((STEP, LANES), jnp.float32)
            columns = []
            for tile in range(TILES):
                wave = units[c * TILES + tile, pl.ds(slot, STEP, stride=0), :]
                spread = pltpu.roll(wave, 0, 1, stride=1, stride_axis=0)
                columns.append(jnp.where(own, spread, before).astype(jnp.bfloat16))
                before = spread
            columns.append(jnp.where(own, 0.0, before).astype(jnp.bfloat16))
            toeplitz = jnp.concatenate(columns, axis=1)
            product = jnp.dot(toeplitz, frames[record], preferred_element_type=jnp.float32)
            total = total + product * scales[record]
        total = jnp.where(lane_used, total, 0.0)
        first = pltpu.roll(total, LANES - (lag >> 5), 1)
        twice[0:STEP, :] = first
        twice[STEP:2 * STEP, :] = pltpu.roll(first, LANES - 1, 1)
        rows = pl.ds(pl.multiple_of(template * STEP, STEP), STEP)
        acc[rows, :] += twice[pl.ds(lag & (STEP - 1), STEP), :]

    for group in range(STEP // 4):
        parts = [acc[pl.ds(4 * group + j, STEP, stride=STEP), :] for j in range(4)]
        turned = jnp.concatenate(parts, axis=0).T
        dense[pl.ds(group, OUT_BLOCKS, stride=8), :] = turned[:OUT_BLOCKS]
    out_ref[...] = dense[...].astype(out_ref.dtype)


def partial_stack(meta, channel_mask, gathered, received):
    group_size = meta.shape[1]
    slot_count = received.shape[0]
    records = gathered.shape[0]
    return pl.pallas_call(
        kernel,
        out_shape=jax.ShapeDtypeStruct((NT * group_size // LANES, LANES), jnp.bfloat16),
        in_specs=[
            pl.BlockSpec(memory_space=pltpu.SMEM),
            pl.BlockSpec(memory_space=pltpu.SMEM),
            pl.BlockSpec(memory_space=pltpu.VMEM),
            pl.BlockSpec(memory_space=pltpu.VMEM),
        ],
        out_specs=pl.BlockSpec(memory_space=pltpu.VMEM),
        scratch_shapes=[
            pltpu.VMEM((records, DEPTH, LANES), jnp.bfloat16),
            pltpu.VMEM((records, STEP, LANES), jnp.float32),
            pltpu.VMEM((3 * TILES, slot_count, LANES), jnp.float32),
            pltpu.VMEM((group_size * STEP, LANES), jnp.float32),
            pltpu.VMEM((2 * STEP, LANES), jnp.float32),
            pltpu.VMEM((NT * group_size // LANES, LANES), jnp.float32),
            pltpu.SMEM((slot_count + 1,), jnp.int32),
        ],
        compiler_params=pltpu.CompilerParams(vmem_limit_bytes=40 * 1024 * 1024),
        name="matched_filter",
    )(meta, channel_mask, gathered, received)


def body(station_data, channel_mask, template_waves, pick_station, pick_lag):
    sta_size = lax.axis_size("sta")
    my_index = lax.axis_index("sta")
    group_size = pick_station.shape[0]
    station_count = channel_mask.shape[1]
    stations_here = station_data.shape[1]
    owners = pick_station // station_count
    order = lax.broadcasted_iota(jnp.int32, (group_size, group_size), 0)
    earlier = lax.broadcasted_iota(jnp.int32, (group_size, group_size), 1) < order

    column = lax.broadcasted_iota(jnp.int32, owners.shape, 1)
    own_owner = jnp.sum(jnp.where(column == my_index, owners, 0), axis=1)
    place = jnp.sum((earlier & (own_owner[:, None] == own_owner[None, :])).astype(jnp.int32), axis=1)
    slot_count = sta_size * CAP
    slot_rows = lax.broadcasted_iota(jnp.int32, (slot_count, group_size), 0)
    select = (slot_rows == (own_owner * CAP + place)[None, :]).astype(jnp.bfloat16)
    waves = template_waves.reshape(group_size, 3 * L)
    outgoing = jnp.dot(select, waves, preferred_element_type=jnp.float32).astype(jnp.bfloat16)
    received = lax.all_to_all(outgoing, "sta", split_axis=0, concat_axis=0, tiled=True)

    tiles = station_data.reshape(3, stations_here, BLOCKS, STEP).transpose(0, 1, 3, 2)
    tiles = jnp.pad(tiles, ((0, 0), (0, 0), (0, 0), (0, LANES - BLOCKS)))
    tiles = tiles.reshape(3 * stations_here, STEP, LANES)
    gathered = lax.all_gather(tiles, "tpl", axis=0, tiled=True)

    landing = owners == my_index
    arrival = jnp.dot(earlier.astype(jnp.bfloat16), landing.astype(jnp.bfloat16),
                      preferred_element_type=jnp.float32).astype(jnp.int32)
    template_ids = lax.broadcasted_iota(jnp.int32, owners.shape, 0)
    packed = VALID + (pick_lag << 9) + ((pick_station - my_index * station_count) << 5) + template_ids
    places = lax.broadcasted_iota(jnp.int32, (CAP,) + owners.shape, 0)
    meta = jnp.sum(jnp.where(landing[None] & (arrival[None] == places), packed[None], 0), axis=1)

    partial_sums = partial_stack(meta, channel_mask, gathered, received)
    sent = partial_sums.reshape(sta_size, -1, LANES)
    arrived = lax.all_to_all(sent, "sta", split_axis=0, concat_axis=0, tiled=True)
    return jnp.sum(arrived.astype(jnp.float32), axis=0).reshape(NT // sta_size, group_size)


def solution(mesh):
    in_specs = (
        P(None, ("sta", "tpl"), None),
        P(None, "sta"),
        P("tpl", "sta", None, None),
        P("tpl", None),
        P("tpl", None),
    )
    return jax.shard_map(body, mesh=mesh, in_specs=in_specs, out_specs=P("sta", "tpl"), check_vma=False)
```

time: 1420 us -> 84.2 us (0.06)
  local copies, waits for them, and re-layouts: 1060 us -> 3.7 us
  waiting for transfers between devices: 215 us -> 1.26 us
  matrix products: 43.6 us -> 0.39 us
  other arithmetic: 37 us -> 1.14 us
  Pallas kernels: 0 us -> 32.2 us
  blocking collectives: 13.6 us -> 33.2 us
    gather x904 -> x0, local copies, waits for them, and re-layouts: 640 us -> none
    unnamed x2 -> x0, waiting for transfers between devices: 215 us -> none
    reshape x79 -> x5, local copies, waits for them, and re-layouts: 192 us -> 1.08 us  [the longest x2 0.76 us: body(): jnp.sum(arrived.astype(jnp.float32), axis=0)]
    while x48 -> x0, local copies, waits for them, and re-layouts: 105 us -> none
    slice x17 -> x0, local copies, waits for them, and re-layouts: 64.4 us -> none  [the longest x8 63.4 us: toeplitz_rows(): tiled[:, :BLOCK * (row_width - 1)].reshape(batch, BLOCK, row_width - 1)]
    dot_general x8 -> x2, matrix products: 40.7 us -> 0.39 us  [the longest x1 0.27 us: body(): jnp.dot(select, waves, preferred_element_type=jnp.float32)]
    another operation x20 -> x0, local copies, waits for them, and re-layouts: 35.1 us -> none  [the longest x8 34.2 us: toeplitz_rows(): tiled = jnp.tile(padded, (1, BLOCK))]
    pallas_call x0 -> x1, Pallas kernels: none -> 32.2 us  [partial_stack(): pl.pallas_call(kernel, out_shape=jax.ShapeDtypeStruct((NT * group_size //...]
  transfers between devices with their start and end apart: 2 -> 1, of which waited for: 1 -> 1; matrix products, arithmetic and copies ran while one was open for 3% -> 1% of each run, Pallas kernels for 0% -> 0%
where the time goes in v1:
time: 84.2 us; the launch traced here: 83.6 us
  blocking collectives  33.2 us (39%)
  Pallas kernels  32.2 us (38%)
  starting transfers between devices  11.6 us (14%)
  local copies, waits for them, and re-layouts  3.7 us (4%)
  waiting for transfers between devices  1.26 us (1%)
  other arithmetic  1.14 us (1%)
    pallas_call x1, Pallas kernels, partial_stack(): pl.pallas_call(kernel, out_shape=jax.ShapeDtypeStruct((NT * group_size //...  32.2 us
    all_to_all x1, blocking collectives, body(): lax.all_to_all(sent, 'sta', split_axis=0, concat_axis=0, tiled=True)  19.7 us
    all_gather x1, blocking collectives, body(): gathered = lax.all_gather(tiles, 'tpl', axis=0, tiled=True)  13.5 us
    all_to_all x1, starting transfers between devices, body(): lax.all_to_all(outgoing, 'sta', split_axis=0, concat_axis=0, tiled=True)  11.6 us
  transfers between devices with their start and end apart: 1, of which 1 were waited for; matrix products, arithmetic and copies ran while one was open for 1% of the time, Pallas kernels for 0%

profile of v1, /device:TPU:2, one launch (start us, length us, event | category | flops | bytes accessed | tf_op | source)
XLA Modules:
  0.0 83.6 jit_solution(16870040526251383658)
XLA Ops:
  0.0 0.9 %select_reduce_fusion.1 = (s32[32]{0:T(128)S(1)}, s32[32,32]{1,0:T(8,128)S(1)}) fusion(pred[32]{0:T(512)(128)(4,1)S(1)} %iota_compare_fusion.5, s32[32,32]{1,0:T(8,128)} %param.8, s32[]{:T(128)S(6)} %mul.13, s32[32,32]{1,0:T(8,128)} %param.9), kind=kLoop, calls=%fused_computation.14 | loop fusion | flops 23520 | bytes 12452 | tf_op jit(solution)/shard_map/reduce_sum | solution.py:168
  0.9 0.2 convert_reduce_fusion.1
  1.1 1.0 %copy.14 = bf16[32,1,3,640]{3,2,0,1:T(4,128)(2,1)S(1)} copy(bf16[32,1,3,640]{3,0,2,1:T(8,128)(2,1)} %param.7) | data formatting | bytes 245760 | tf_op args[2]
  2.1 0.3 convolution_convert_fusion
  2.4 0.9 %all_to_all.10 = bf16[32,4,1920]{2,1,0:T(4,128)(2,1)} reshape(bf16[128,1920]{1,0:T(8,128)(2,1)S(1)} %convolution_convert_fusion) | data formatting | bytes 983040 | tf_op jit(solution)/shard_map/all_to_all | solution.py:175
  3.2 0.0 copy-start.1
  3.2 11.6 %all-to-all-start = ((bf16[32,4,1920]{2,1,0:T(4,128)(2,1)}), bf16[32,4,1920]{2,1,0:T(4,128)(2,1)S(1)}, u32[]{:S(2)}, u32[]{:S(2)}) async-start(bf16[32,4,1920]{2,1,0:T(4,128)(2,1)} %all_to_all.10), calls=%async_computation | async-start | bytes 983040 | tf_op jit(solution)/shard_map/all_to_all | solution.py:175
  14.9 0.0 copy-done.1
  14.9 0.2 reshape.28
  15.1 0.0 copy-start.2
  15.1 0.1 copy.13
  15.2 0.6 copy-done.2
  15.8 0.1 convolution_convert_fusion.1
  16.0 13.5 %all_gather.3.tiles_ref = f32[48,32,128]{2,1,0:T(8,128)S(1)} all-gather(f32[6,32,128]{2,1,0:T(8,128)S(1)} %copy.13), channel_id=1, replica_groups=mesh['sta'=32,'tpl'=8] {'tpl'}, dimensions={0}, use_global_device_ids=true | all-gather | bytes 884736 | tf_op jit(solution)/shard_map/all_gather | solution.py:180
  29.5 0.0 copy-start
  29.5 1.3 %all-to-all-done = bf16[32,4,1920]{2,1,0:T(4,128)(2,1)S(1)} async-done(((bf16[32,4,1920]{2,1,0:T(4,128)(2,1)}), bf16[32,4,1920]{2,1,0:T(4,128)(2,1)S(1)}, u32[]{:S(2)}, u32[]{:S(2)}) %all-to-all-start) | async-done | bytes 491552 | tf_op jit(solution)/shard_map/all_to_all | solution.py:175
  30.8 0.1 all_to_all.12.waves_ref
  30.9 0.0 copy-done
  30.9 32.2 %matched_filter.1 = bf16[384,128]{1,0:T(8,128)(2,1)S(1)} custom-call(s32[4,32]{1,0:T(4,128)S(1)} %select_reduce_fusion.meta_ref, s32[3,16]{1,0:T(4,128)S(1)} %copy-done, f32[48,32,128]{2,1,0:T(8,128)S(1)} %all_gather.3.tiles_ref, bf16[128,1920]{1,0:T(8,128)(2,1)S(1)} %all_to_all.12.waves_ref), custom_call_target="tpu_custom_call" | custom-call | tf_op jit(solution)/shard_map/matched_filter/pallas_call | solution.py:133
  63.1 19.7 %all_to_all.16 = bf16[32,12,128]{2,1,0:T(8,128)(2,1)S(1)} all-to-all(bf16[32,12,128]{2,1,0:T(8,128)(2,1)S(1)} %reshape.31), channel_id=1, replica_groups=mesh['sta'=32,'tpl'=8] {'sta'}, dimensions={0} | all-to-all | bytes 196608 | tf_op jit(solution)/shard_map/all_to_all | solution.py:192
  82.8 0.1 reshape.32
  82.9 0.7 copy.15
  (8 shorter events, 0.2 us)
Async XLA Ops:
  3.2 11.6 %copy-start.1 = (f32[3,2,3200]{2,1,0:T(2,128)S(1)}, f32[3,2,3200]{2,1,0:T(2,128)}, u32[]{:S(2)}) copy-start(f32[3,2,3200]{2,1,0:T(2,128)} %param.5) | copy-start | bytes 230404
  3.2 27.5 %all-to-all-start = ((bf16[32,4,1920]{2,1,0:T(4,128)(2,1)}), bf16[32,4,1920]{2,1,0:T(4,128)(2,1)S(1)}, u32[]{:S(2)}, u32[]{:S(2)}) async-start(bf16[32,4,1920]{2,1,0:T(4,128)(2,1)} %all_to_all.10), calls=%async_computation | async-start | bytes 983040 | tf_op jit(solution)/shard_map/all_to_all | solution.py:175
  15.1 0.7 copy-start.2
  29.5 1.4 %copy-start = (s32[3,16]{1,0:T(4,128)S(1)}, s32[3,16]{1,0:T(4,128)}, u32[]{:S(2)}) copy-start(s32[3,16]{1,0:T(4,128)} %mask_ref.1) | copy-start | bytes 580

commit v2 on v1

--- a/solution.py
+++ b/solution.py
@@ -48,8 +48,9 @@
     return whole + exclusive_prefix(ahead)
 
 
-def kernel(meta_ref, mask_ref, tiles_ref, waves_ref, out_ref,
-           frames, scales, units, acc, twice, dense, slots):
+def kernel(meta_ref, mask_ref, *refs):
+    *tile_refs, waves_ref, out_ref = refs[:-7]
+    (frames, scales, units, acc, twice, dense, slots) = refs[-7:]
     peers = meta_ref.shape[1]
 
     def list_slot(slot, count):
@@ -71,19 +72,22 @@
             for tile in range(TILES):
                 units[c * TILES + tile, rows, :] = unit[:, tile * LANES:(tile + 1) * LANES]
 
-    @pl.loop(0, tiles_ref.shape[0])
-    def _(record):
-        tile = tiles_ref[record]
-        for turn in range(DEPTH // STEP):
-            rolled = tile if turn == 0 else pltpu.roll(tile, LANES - turn, 1)
-            frames[record, turn * STEP:(turn + 1) * STEP, :] = rolled.astype(jnp.bfloat16)
-        mean_one = window_sums(tile) * (1.0 / L)
-        mean_two = window_sums(tile * tile) * (1.0 / L)
-        within = lax.rem(record, 6)
-        station = (record // 6) * 2 + (within & 1)
-        weight = mask_ref[within >> 1, station].astype(jnp.float32)
-        spread = L * jnp.sqrt(mean_two - mean_one * mean_one + EPSILON)
-        scales[record] = weight / spread
+    here = mask_ref[0, 0] >> 1
+    for hop, tile_ref in enumerate(tile_refs):
+        owner = (here - hop) & (len(tile_refs) - 1)
+
+        @pl.loop(0, tile_ref.shape[0])
+        def _(within):
+            record = owner * 6 + within
+            tile = tile_ref[within]
+            for turn in range(DEPTH // STEP):
+                rolled = tile if turn == 0 else pltpu.roll(tile, LANES - turn, 1)
+                frames[record, turn * STEP:(turn + 1) * STEP, :] = rolled.astype(jnp.bfloat16)
+            mean_one = window_sums(tile) * (1.0 / L)
+            mean_two = window_sums(tile * tile) * (1.0 / L)
+            weight = (mask_ref[within >> 1, owner * 2 + (within & 1)] & 1).astype(jnp.float32)
+            spread = L * jnp.sqrt(mean_two - mean_one * mean_one + EPSILON)
+            scales[record] = weight / spread
 
     acc[...] = jnp.zeros_like(acc)
     row = lax.broadcasted_iota(jnp.int32, (STEP, LANES), 0)
@@ -123,22 +127,22 @@
         parts = [acc[pl.ds(4 * group + j, STEP, stride=STEP), :] for j in range(4)]
         turned = jnp.concatenate(parts, axis=0).T
         dense[pl.ds(group, OUT_BLOCKS, stride=8), :] = turned[:OUT_BLOCKS]
-    out_ref[...] = dense[...].astype(out_ref.dtype)
-
-
-def partial_stack(meta, channel_mask, gathered, received):
+    for part in range(out_ref.shape[1] // LANES):
+        rows = dense[pl.ds(part, out_ref.shape[0], stride=3), :]
+        out_ref[:, part * LANES:(part + 1) * LANES] = rows.astype(out_ref.dtype)
+
+
+def partial_stack(meta, mask, tiles, received):
     group_size = meta.shape[1]
     slot_count = received.shape[0]
-    records = gathered.shape[0]
+    records = len(tiles) * tiles[0].shape[0]
     return pl.pallas_call(
         kernel,
-        out_shape=jax.ShapeDtypeStruct((NT * group_size // LANES, LANES), jnp.bfloat16),
+        out_shape=jax.ShapeDtypeStruct((slot_count, NT * group_size // slot_count), jnp.bfloat16),
         in_specs=[
             pl.BlockSpec(memory_space=pltpu.SMEM),
             pl.BlockSpec(memory_space=pltpu.SMEM),
-            pl.BlockSpec(memory_space=pltpu.VMEM),
-            pl.BlockSpec(memory_space=pltpu.VMEM),
-        ],
+        ] + [pl.BlockSpec(memory_space=pltpu.VMEM)] * (len(tiles) + 1),
         out_specs=pl.BlockSpec(memory_space=pltpu.VMEM),
         scratch_shapes=[
             pltpu.VMEM((records, DEPTH, LANES), jnp.bfloat16),
@@ -151,7 +155,7 @@
         ],
         compiler_params=pltpu.CompilerParams(vmem_limit_bytes=40 * 1024 * 1024),
         name="matched_filter",
-    )(meta, channel_mask, gathered, received)
+    )(meta, mask, *tiles, received)
 
 
 def body(station_data, channel_mask, template_waves, pick_station, pick_lag):
@@ -177,7 +181,11 @@
     tiles = station_data.reshape(3, stations_here, BLOCKS, STEP).transpose(0, 1, 3, 2)
     tiles = jnp.pad(tiles, ((0, 0), (0, 0), (0, 0), (0, LANES - BLOCKS)))
     tiles = tiles.reshape(3 * stations_here, STEP, LANES)
-    gathered = lax.all_gather(tiles, "tpl", axis=0, tiled=True)
+    tpl_size = lax.axis_size("tpl")
+    held = [tiles]
+    for hop in range(1, tpl_size):
+        held.append(lax.ppermute(tiles, "tpl", [(i, (i + hop) % tpl_size) for i in range(tpl_size)]))
+    mask = channel_mask + 2 * lax.axis_index("tpl")
 
     landing = owners == my_index
     arrival = jnp.dot(earlier.astype(jnp.bfloat16), landing.astype(jnp.bfloat16),
@@ -187,10 +195,10 @@
     places = lax.broadcasted_iota(jnp.int32, (CAP,) + owners.shape, 0)
     meta = jnp.sum(jnp.where(landing[None] & (arrival[None] == places), packed[None], 0), axis=1)
 
-    partial_sums = partial_stack(meta, channel_mask, gathered, received)
-    sent = partial_sums.reshape(sta_size, -1, LANES)
-    arrived = lax.all_to_all(sent, "sta", split_axis=0, concat_axis=0, tiled=True)
-    return jnp.sum(arrived.astype(jnp.float32), axis=0).reshape(NT // sta_size, group_size)
+    partial_sums = partial_stack(meta, mask, held, received)
+    arrived = lax.all_to_all(partial_sums, "sta", split_axis=0, concat_axis=0, tiled=True)
+    arrived = arrived.reshape(sta_size, CAP, -1).astype(jnp.float32)
+    return jnp.sum(arrived, axis=0).reshape(NT // sta_size, group_size)
 
 
 def solution(mesh):

time: 84.2 us -> 82.8 us (0.983)
  blocking collectives: 33.2 us -> 17.5 us
  starting transfers between devices: 11.6 us -> 19.4 us
  waiting for transfers between devices: 1.26 us -> 7 us
    all_gather x1 -> x0, blocking collectives: 13.5 us -> none  [body(): gathered = lax.all_gather(tiles, 'tpl', axis=0, tiled=True)]
    ppermute x0 -> x7, starting transfers between devices: none -> 7.83 us  [body(): lax.ppermute(tiles, 'tpl', [(i, (i + hop) % tpl_size) for i in range(tpl_...]
    all_to_all x1, waiting for transfers between devices: 1.26 us -> 6.98 us  [body(): lax.all_to_all(outgoing, 'sta', split_axis=0, concat_axis=0, tiled=True)]
    all_to_all x1, blocking collectives: 19.7 us -> 17.5 us  [body(): lax.all_to_all(partial_sums, 'sta', split_axis=0, concat_axis=0, tiled=True)]
    unnamed x8 -> x9, local copies, waits for them, and re-layouts: 1.59 us -> 1.68 us
  transfers between devices with their start and end apart: 1 -> 8, of which waited for: 1 -> 1; matrix products, arithmetic and copies ran while one was open for 1% -> 1% of each run, Pallas kernels for 0% -> 0%
where the time goes in v2:
time: 82.8 us; the launch traced here: 81.5 us
  Pallas kernels  32.2 us (39%)
  starting transfers between devices  19.4 us (23%)
  blocking collectives  17.5 us (21%)
  waiting for transfers between devices  7 us (8%)
  local copies, waits for them, and re-layouts  3.68 us (4%)
  other arithmetic  1.17 us (1%)
    pallas_call x1, Pallas kernels, partial_stack(): pl.pallas_call(kernel, out_shape=jax.ShapeDtypeStruct((slot_count, NT * g...  32.2 us
    all_to_all x1, blocking collectives, body(): lax.all_to_all(partial_sums, 'sta', split_axis=0, concat_axis=0, tiled=True)  17.5 us
    all_to_all x1, starting transfers between devices, body(): lax.all_to_all(outgoing, 'sta', split_axis=0, concat_axis=0, tiled=True)  11.6 us
    ppermute x7, starting transfers between devices, body(): lax.ppermute(tiles, 'tpl', [(i, (i + hop) % tpl_size) for i in range(tpl_...  7.83 us
    all_to_all x1, waiting for transfers between devices, body(): lax.all_to_all(outgoing, 'sta', split_axis=0, concat_axis=0, tiled=True)  6.98 us
    unnamed x9, local copies, waits for them, and re-layouts  1.68 us
  transfers between devices with their start and end apart: 8, of which 1 were waited for; matrix products, arithmetic and copies ran while one was open for 1% of the time, Pallas kernels for 0%

profile of v2, /device:TPU:2, one launch (start us, length us, event | category | flops | bytes accessed | tf_op | source)
XLA Modules:
  0.0 81.5 jit_solution(3559966031133243289)
XLA Ops:
  0.0 0.9 %select_reduce_fusion.1 = (s32[32]{0:T(128)S(1)}, s32[32,32]{1,0:T(8,128)S(1)}) fusion(pred[32]{0:T(512)(128)(4,1)S(1)} %iota_compare_fusion.5, s32[32,32]{1,0:T(8,128)} %param.8, s32[]{:T(128)S(6)} %mul.13, s32[32,32]{1,0:T(8,128)} %param.9), kind=kLoop, calls=%fused_computation.14 | loop fusion | flops 23520 | bytes 12452 | tf_op jit(solution)/shard_map/reduce_sum | solution.py:172
  0.9 0.2 convert_reduce_fusion.1
  1.1 1.0 %copy.11 = bf16[32,1,3,640]{3,2,0,1:T(4,128)(2,1)S(1)} copy(bf16[32,1,3,640]{3,0,2,1:T(8,128)(2,1)} %param.7) | data formatting | bytes 245760 | tf_op args[2]
  2.1 0.3 convolution_convert_fusion
  2.4 0.9 %all_to_all.13 = bf16[32,4,1920]{2,1,0:T(4,128)(2,1)} reshape(bf16[128,1920]{1,0:T(8,128)(2,1)S(1)} %convolution_convert_fusion) | data formatting | bytes 983040 | tf_op jit(solution)/shard_map/all_to_all | solution.py:179
  3.3 11.6 %all-to-all-start = ((bf16[32,4,1920]{2,1,0:T(4,128)(2,1)}), bf16[32,4,1920]{2,1,0:T(4,128)(2,1)S(1)}, u32[]{:S(2)}, u32[]{:S(2)}) async-start(bf16[32,4,1920]{2,1,0:T(4,128)(2,1)} %all_to_all.13), calls=%async_computation | async-start | bytes 983040 | tf_op jit(solution)/shard_map/all_to_all | solution.py:179
  14.9 0.2 reshape.29
  15.1 0.1 copy.13
  15.2 0.0 collective-permute-start
  15.2 1.6 %collective-permute-start.1 = (f32[6,32,128]{2,1,0:T(8,128)S(1)}, f32[6,32,128]{2,1,0:T(8,128)S(1)}, u32[]{:S(2)}, u32[]{:S(2)}) collective-permute-start(f32[6,32,128]{2,1,0:T(8,128)S(1)} %bitcast.9), channel_id=1, source_target_pairs={{0,2},{1,3},{2,4},{3,5},{4,6},{5,7},{6,0},{7,1},{8,10},{9,11},{10,... | collective-permute-start | bytes 294920 | tf_op jit(solution)/shard_map/ppermute | solution.py:187
  16.8 1.0 %collective-permute-start.2 = (f32[6,32,128]{2,1,0:T(8,128)S(1)}, f32[6,32,128]{2,1,0:T(8,128)S(1)}, u32[]{:S(2)}, u32[]{:S(2)}) collective-permute-start(f32[6,32,128]{2,1,0:T(8,128)S(1)} %bitcast.10), channel_id=1, source_target_pairs={{0,3},{1,4},{2,5},{3,6},{4,7},{5,0},{6,1},{7,2},{8,11},{9,12},{10,... | collective-permute-start | bytes 294920 | tf_op jit(solution)/shard_map/ppermute | solution.py:187
  17.8 2.4 %collective-permute-start.3 = (f32[6,32,128]{2,1,0:T(8,128)S(1)}, f32[6,32,128]{2,1,0:T(8,128)S(1)}, u32[]{:S(2)}, u32[]{:S(2)}) collective-permute-start(f32[6,32,128]{2,1,0:T(8,128)S(1)} %bitcast.11), channel_id=1, source_target_pairs={{0,4},{1,5},{2,6},{3,7},{4,0},{5,1},{6,2},{7,3},{8,12},{9,13},{10,... | collective-permute-start | bytes 294920 | tf_op jit(solution)/shard_map/ppermute | solution.py:187
  20.3 0.6 collective-permute-start.4
  20.9 0.0 copy-start.2
  20.9 0.1 convolution_convert_fusion.1
  21.1 0.5 copy-done.2
  21.6 2.2 %collective-permute-start.5 = (f32[6,32,128]{2,1,0:T(8,128)S(1)}, f32[6,32,128]{2,1,0:T(8,128)S(1)}, u32[]{:S(2)}, u32[]{:S(2)}) collective-permute-start(f32[6,32,128]{2,1,0:T(8,128)S(1)} %bitcast.13), channel_id=1, source_target_pairs={{0,6},{1,7},{2,0},{3,1},{4,2},{5,3},{6,4},{7,5},{8,14},{9,15},{10,... | collective-permute-start | bytes 294920 | tf_op jit(solution)/shard_map/ppermute | solution.py:187
  23.8 7.0 %all-to-all-done = bf16[32,4,1920]{2,1,0:T(4,128)(2,1)S(1)} async-done(((bf16[32,4,1920]{2,1,0:T(4,128)(2,1)}), bf16[32,4,1920]{2,1,0:T(4,128)(2,1)S(1)}, u32[]{:S(2)}, u32[]{:S(2)}) %all-to-all-start) | async-done | bytes 491552 | tf_op jit(solution)/shard_map/all_to_all | solution.py:179
  30.8 0.1 all_to_all.15.refs_8_
  31.0 32.2 %matched_filter.1 = bf16[128,384]{1,0:T(8,128)(2,1)S(1)} custom-call(s32[4,32]{1,0:T(4,128)S(1)} %select_reduce_fusion.meta_ref, s32[3,16]{1,0:T(4,128)S(1)} %broadcast_add_fusion.mask_ref, f32[6,32,128]{2,1,0:T(8,128)S(1)} %bitcast.15, f32[6,32,128]{2,1,0:T(8,128)S(1)} %collective-permute-done.refs_1_, f32[6,32,128]{2,1,0:T(8,128)S(1)} %collective-permute-done.1.refs_2_, ...), custom_call_target="tpu_custom_call" | custom-call | tf_op jit(solution)/shard_map/matched_filter/pallas_call | solution.py:139
  63.2 17.5 %all_to_all.20 = bf16[32,4,384]{2,1,0:T(4,128)(2,1)S(1)} all-to-all(bf16[32,4,384]{2,1,0:T(4,128)(2,1)S(1)} %all_to_all.16), channel_id=1, replica_groups=mesh['sta'=32,'tpl'=8] {'sta'}, dimensions={0} | all-to-all | bytes 196608 | tf_op jit(solution)/shard_map/all_to_all | solution.py:199
  80.7 0.1 convert_reduce_fusion
  80.7 0.1 reshape.32
  80.8 0.7 copy.12
  (20 shorter events, 0.2 us)
Async XLA Ops:
  3.3 11.6 %copy-start = (f32[3,2,3200]{2,1,0:T(2,128)S(1)}, f32[3,2,3200]{2,1,0:T(2,128)}, u32[]{:S(2)}) copy-start(f32[3,2,3200]{2,1,0:T(2,128)} %param.5) | copy-start | bytes 230404
  3.3 27.5 %all-to-all-start = ((bf16[32,4,1920]{2,1,0:T(4,128)(2,1)}), bf16[32,4,1920]{2,1,0:T(4,128)(2,1)S(1)}, u32[]{:S(2)}, u32[]{:S(2)}) async-start(bf16[32,4,1920]{2,1,0:T(4,128)(2,1)} %all_to_all.13), calls=%async_computation | async-start | bytes 983040 | tf_op jit(solution)/shard_map/all_to_all | solution.py:179
  15.2 5.7 %copy-start.1 = (s32[32,32]{1,0:T(8,128)S(1)}, s32[32,32]{1,0:T(8,128)}, u32[]{:S(2)}) copy-start(s32[32,32]{1,0:T(8,128)} %param.8) | copy-start | bytes 12292
  15.2 6.4 %collective-permute-start = (f32[6,32,128]{2,1,0:T(8,128)S(1)}, f32[6,32,128]{2,1,0:T(8,128)S(1)}, u32[]{:S(2)}, u32[]{:S(2)}) collective-permute-start(f32[6,32,128]{2,1,0:T(8,128)S(1)} %bitcast.8), channel_id=1, source_target_pairs={{0,1},{1,2},{2,3},{3,4},{4,5},{5,6},{6,7},{7,0},{8,9},{9,10},{10,1... | collective-permute-start | bytes 294920 | tf_op jit(solution)/shard_map/ppermute | solution.py:187
  15.2 8.5 %collective-permute-start.1 = (f32[6,32,128]{2,1,0:T(8,128)S(1)}, f32[6,32,128]{2,1,0:T(8,128)S(1)}, u32[]{:S(2)}, u32[]{:S(2)}) collective-permute-start(f32[6,32,128]{2,1,0:T(8,128)S(1)} %bitcast.9), channel_id=1, source_target_pairs={{0,2},{1,3},{2,4},{3,5},{4,6},{5,7},{6,0},{7,1},{8,10},{9,11},{10,... | collective-permute-start | bytes 294920 | tf_op jit(solution)/shard_map/ppermute | solution.py:187
  16.8 14.1 %collective-permute-start.2 = (f32[6,32,128]{2,1,0:T(8,128)S(1)}, f32[6,32,128]{2,1,0:T(8,128)S(1)}, u32[]{:S(2)}, u32[]{:S(2)}) collective-permute-start(f32[6,32,128]{2,1,0:T(8,128)S(1)} %bitcast.10), channel_id=1, source_target_pairs={{0,3},{1,4},{2,5},{3,6},{4,7},{5,0},{6,1},{7,2},{8,11},{9,12},{10,... | collective-permute-start | bytes 294920 | tf_op jit(solution)/shard_map/ppermute | solution.py:187
  17.8 13.1 %collective-permute-start.3 = (f32[6,32,128]{2,1,0:T(8,128)S(1)}, f32[6,32,128]{2,1,0:T(8,128)S(1)}, u32[]{:S(2)}, u32[]{:S(2)}) collective-permute-start(f32[6,32,128]{2,1,0:T(8,128)S(1)} %bitcast.11), channel_id=1, source_target_pairs={{0,4},{1,5},{2,6},{3,7},{4,0},{5,1},{6,2},{7,3},{8,12},{9,13},{10,... | collective-permute-start | bytes 294920 | tf_op jit(solution)/shard_map/ppermute | solution.py:187
  20.3 10.7 %collective-permute-start.4 = (f32[6,32,128]{2,1,0:T(8,128)S(1)}, f32[6,32,128]{2,1,0:T(8,128)S(1)}, u32[]{:S(2)}, u32[]{:S(2)}) collective-permute-start(f32[6,32,128]{2,1,0:T(8,128)S(1)} %bitcast.12), channel_id=1, source_target_pairs={{0,5},{1,6},{2,7},{3,0},{4,1},{5,2},{6,3},{7,4},{8,13},{9,14},{10,... | collective-permute-start | bytes 294920 | tf_op jit(solution)/shard_map/ppermute | solution.py:187
  20.9 0.7 copy-start.2
  21.6 9.3 %collective-permute-start.5 = (f32[6,32,128]{2,1,0:T(8,128)S(1)}, f32[6,32,128]{2,1,0:T(8,128)S(1)}, u32[]{:S(2)}, u32[]{:S(2)}) collective-permute-start(f32[6,32,128]{2,1,0:T(8,128)S(1)} %bitcast.13), channel_id=1, source_target_pairs={{0,6},{1,7},{2,0},{3,1},{4,2},{5,3},{6,4},{7,5},{8,14},{9,15},{10,... | collective-permute-start | bytes 294920 | tf_op jit(solution)/shard_map/ppermute | solution.py:187
  23.8 7.2 %collective-permute-start.6 = (f32[6,32,128]{2,1,0:T(8,128)S(1)}, f32[6,32,128]{2,1,0:T(8,128)S(1)}, u32[]{:S(2)}, u32[]{:S(2)}) collective-permute-start(f32[6,32,128]{2,1,0:T(8,128)S(1)} %bitcast.14), channel_id=1, source_target_pairs={{0,7},{1,0},{2,1},{3,2},{4,3},{5,4},{6,5},{7,6},{8,15},{9,8},{10,9... | collective-permute-start | bytes 294920 | tf_op jit(solution)/shard_map/ppermute | solution.py:187

commit v3 on v2

v3 whole, which is shorter than its diff:
```python
import jax
import jax.numpy as jnp
from jax import lax
from jax.experimental import pallas as pl
from jax.experimental.pallas import tpu as pltpu
from jax.sharding import PartitionSpec as P

NT = 1536
L = 640
LAGS = 1024
SAMPLES = 3200
CAP = 4
STEP = 32
LANES = 128
BLOCKS = SAMPLES // STEP
OUT_BLOCKS = NT // STEP
TILES = L // LANES
TURNS = 8
UNROLL = 2
STATION_BITS = 4
EPSILON = 1e-05
VALID = 1 << 20


def exclusive_prefix(values):
    lanes = values.shape[-1]
    groups = values.reshape(-1, 8, lanes)
    row = lax.broadcasted_iota(jnp.int32, groups.shape, 1)
    total = groups
    for shift in (1, 2, 4):
        total = total + jnp.where(row >= shift, pltpu.roll(total, shift, 1), 0.0)
    inner = jnp.where(row >= 1, pltpu.roll(total, 1, 1), 0.0).reshape(-1, STEP // 8, 8, lanes)
    last = total.reshape(-1, STEP // 8, 8, lanes)[:, :, 7:8]
    pieces = [inner[:, 0:1]]
    carry = last[:, 0:1]
    for group in range(1, STEP // 8):
        pieces.append(inner[:, group:group + 1] + carry)
        carry = carry + last[:, group:group + 1]
    return jnp.concatenate(pieces, axis=1).reshape(values.shape)


def window_sums(values):
    width = values.shape[-1]
    span = L // STEP
    ahead = pltpu.roll(values, width - span, 1) - values
    two = jnp.sum(values.reshape(-1, STEP, width), axis=1)
    two = two + pltpu.roll(two, width - 1, 1)
    four = two + pltpu.roll(two, width - 2, 1)
    eight = four + pltpu.roll(four, width - 4, 1)
    sixteen = eight + pltpu.roll(eight, width - 8, 1)
    whole = sixteen + pltpu.roll(four, width - 16, 1)
    inner = exclusive_prefix(ahead).reshape(-1, STEP, width)
    return whole[:, None, :] + inner


def select_kernel(index_ref, station_ref, waves_ref, out_ref):
    group_size = station_ref.shape[0]
    square = (group_size, group_size)
    row = lax.broadcasted_iota(jnp.int32, square, 0)
    column = lax.broadcasted_iota(jnp.int32, square, 1)
    owners = station_ref[...] >> STATION_BITS
    down = jnp.sum(jnp.where(column == index_ref[0], owners, 0), axis=1, keepdims=True)
    down = jnp.broadcast_to(down, square)
    across = jnp.sum(jnp.where(row == column, down, 0), axis=0, keepdims=True)
    same = (down == across) & (row < column)
    place = jnp.sum(same.astype(jnp.int32), axis=0, keepdims=True)
    slot = across * CAP + place
    slots = lax.broadcasted_iota(jnp.int32, (out_ref.shape[0], group_size), 0)
    select = (slots == slot).astype(jnp.float32).astype(jnp.bfloat16)
    for c in range(3):
        values = waves_ref[c].astype(jnp.float32)
        centred = values - jnp.mean(values, axis=-1, keepdims=True)
        power = jnp.mean(centred * centred, axis=-1, keepdims=True)
        unit = (centred / jnp.sqrt(power + EPSILON)).astype(jnp.bfloat16)
        picked = jnp.dot(select, unit, preferred_element_type=jnp.float32)
        out_ref[:, c * L:(c + 1) * L] = picked.astype(jnp.bfloat16)


def records_kernel(meta_ref, mask_ref, *refs):
    *tile_refs, frames, scales, slots = refs

    def list_slot(slot, count):
        slots[count] = slot
        held = meta_ref[slot & (CAP - 1), slot >> 2] >> 20
        return count + held

    total = meta_ref.shape[1] * CAP
    count = lax.fori_loop(0, total, list_slot, jnp.int32(0))
    slots[count] = -1
    slots[total + 1] = count

    here = mask_ref[0, 0] >> 1
    for hop, tile_ref in enumerate(tile_refs):
        owner = (here - hop) & (len(tile_refs) - 1)
        size = tile_ref.shape[0]
        first = owner * size
        values = tile_ref[...].reshape(size * STEP, LANES)
        for turn in range(TURNS):
            rolled = values if turn == 0 else pltpu.roll(values, LANES - turn, 1)
            frames[pl.ds(first, size), turn * STEP:(turn + 1) * STEP, :] = (
                rolled.astype(jnp.bfloat16).reshape(size, STEP, LANES)
            )
        mean_one = window_sums(values) * (1.0 / L)
        mean_two = window_sums(values * values) * (1.0 / L)
        spread = L * jnp.sqrt(mean_two - mean_one * mean_one + EPSILON)
        for within in range(size):
            weight = (mask_ref[within >> 1, owner * 2 + (within & 1)] & 1).astype(jnp.float32)
            scales[first + within] = weight / spread[within]


def stack_kernel(meta_ref, slots, frames, scales, waves_ref, out_ref, units, acc, twice, dense):
    slot_count = waves_ref.shape[0]
    count = slots[slot_count + 1]
    for start in range(3 * TILES):
        units[start] = waves_ref[:, start * LANES:(start + 1) * LANES].astype(jnp.float32)
    acc[...] = jnp.zeros_like(acc)
    row = lax.broadcasted_iota(jnp.int32, (STEP, LANES), 0)
    lane = lax.broadcasted_iota(jnp.int32, (STEP, LANES), 1)
    own = lane >= row

    def one_pick(slot, spare):
        held = slot >= 0
        slot = jnp.maximum(slot, 0)
        packed = meta_ref[slot & (CAP - 1), slot >> 2]
        template = jnp.where(held, packed & 31, acc.shape[0] // STEP - 1)
        station = (packed >> 5) & 15
        lag = (packed >> 9) & 2047
        total = jnp.zeros((STEP, LANES), jnp.float32)
        for c in range(3):
            record = (station >> 1) * 6 + 2 * c + (station & 1)
            before = jnp.zeros((STEP, LANES), jnp.float32)
            columns = []
            for tile in range(TILES):
                wave = units[c * TILES + tile, pl.ds(slot, STEP, stride=0), :]
                spread = pltpu.roll(wave, 0, 1, stride=1, stride_axis=0)
                columns.append(jnp.where(own, spread, before).astype(jnp.bfloat16))
                before = spread
            columns.append(jnp.where(own, 0.0, before).astype(jnp.bfloat16))
            left = jnp.concatenate(
                [jnp.concatenate(columns[i:i + 2], axis=1) for i in range(0, TILES + 1, 2)], axis=0
            )
            product = jnp.dot(left, frames[record], preferred_element_type=jnp.float32)
            summed = product[:STEP]
            for part in range(1, (TILES + 1) // 2):
                later = product[part * STEP:(part + 1) * STEP]
                summed = summed + pltpu.roll(later, LANES - TURNS * part, 1)
            total = total + summed * scales[record]
        first = pltpu.roll(total, LANES - (lag >> 5), 1)
        twice[spare, 0:STEP, :] = first
        twice[spare, STEP:2 * STEP, :] = pltpu.roll(first, LANES - 1, 1)
        shifted = twice[spare, pl.ds(lag & (STEP - 1), STEP), :]
        return pl.ds(pl.multiple_of(template * STEP, STEP), STEP), shifted

    @pl.loop(0, (count + UNROLL - 1) // UNROLL)
    def _(index):
        done = [one_pick(slots[index * UNROLL + spare], spare) for spare in range(UNROLL)]
        for rows, shifted in done:
            acc[rows, :] += shifted

    for group in range(STEP // 4):
        parts = [acc[pl.ds(4 * group + j, STEP, stride=STEP), :] for j in range(4)]
        turned = jnp.concatenate(parts, axis=0).T
        dense[pl.ds(group, OUT_BLOCKS, stride=8), :] = turned[:OUT_BLOCKS]
    for part in range(out_ref.shape[1] // LANES):
        rows = dense[pl.ds(part, out_ref.shape[0], stride=3), :]
        out_ref[:, part * LANES:(part + 1) * LANES] = rows.astype(out_ref.dtype)


SMEM = pl.BlockSpec(memory_space=pltpu.SMEM)
VMEM = pl.BlockSpec(memory_space=pltpu.VMEM)


def slot_waves(my_index, pick_station, template_waves, slot_count):
    return pl.pallas_call(
        select_kernel,
        out_shape=jax.ShapeDtypeStruct((slot_count, 3 * L), jnp.bfloat16),
        in_specs=[SMEM, VMEM, VMEM],
        out_specs=VMEM,
        name="select_waves",
    )(my_index.reshape(1), pick_station, template_waves)


def frames_and_scales(meta, mask, tiles):
    records = len(tiles) * tiles[0].shape[0]
    slot_count = meta.size
    return pl.pallas_call(
        records_kernel,
        out_shape=(
            jax.ShapeDtypeStruct((records, TURNS * STEP, LANES), jnp.bfloat16),
            jax.ShapeDtypeStruct((records, STEP, LANES), jnp.float32),
            jax.ShapeDtypeStruct((slot_count + 2,), jnp.int32),
        ),
        in_specs=[SMEM, SMEM] + [VMEM] * len(tiles),
        out_specs=(VMEM, VMEM, SMEM),
        compiler_params=pltpu.CompilerParams(vmem_limit_bytes=16 * 1024 * 1024),
        cost_estimate=pl.CostEstimate(flops=20_000_000, transcendentals=200_000, bytes_accessed=5_000_000),
        name="frames_and_scales",
    )(meta, mask, *tiles)


def partial_stack(meta, slots, frames, scales, received):
    group_size = meta.shape[1]
    slot_count = received.shape[0]
    rows = NT * group_size // LANES
    return pl.pallas_call(
        stack_kernel,
        out_shape=jax.ShapeDtypeStruct((slot_count, rows * LANES // slot_count), jnp.bfloat16),
        in_specs=[SMEM, SMEM, VMEM, VMEM, VMEM],
        out_specs=VMEM,
        scratch_shapes=[
            pltpu.VMEM((3 * TILES, slot_count, LANES), jnp.float32),
            pltpu.VMEM(((group_size + 1) * STEP, LANES), jnp.float32),
            pltpu.VMEM((UNROLL, 2 * STEP, LANES), jnp.float32),
            pltpu.VMEM((rows, LANES), jnp.float32),
        ],
        compiler_params=pltpu.CompilerParams(vmem_limit_bytes=20 * 1024 * 1024),
        cost_estimate=pl.CostEstimate(flops=200_000_000, transcendentals=0, bytes_accessed=8_000_000),
        name="stack_picks",
    )(meta, slots, frames, scales, received)


def body(station_data, channel_mask, template_waves, pick_station, pick_lag):
    sta_size = lax.axis_size("sta")
    tpl_size = lax.axis_size("tpl")
    my_index = lax.axis_index("sta")
    group_size = pick_station.shape[0]
    station_count = channel_mask.shape[1]
    stations_here = station_data.shape[1]

    waves = template_waves.reshape(group_size, 3, L).transpose(1, 0, 2)
    outgoing = slot_waves(my_index, pick_station, waves, sta_size * CAP)
    received = lax.all_to_all(outgoing, "sta", split_axis=0, concat_axis=0, tiled=True)

    tiles = station_data.reshape(3, stations_here, BLOCKS, STEP).transpose(0, 1, 3, 2)
    tiles = jnp.pad(tiles, ((0, 0), (0, 0), (0, 0), (0, LANES - BLOCKS)))
    tiles = tiles.reshape(3 * stations_here, STEP, LANES)
    held = [tiles]
    for hop in range(1, tpl_size):
        held.append(lax.ppermute(tiles, "tpl", [(i, (i + hop) % tpl_size) for i in range(tpl_size)]))
    mask = channel_mask + 2 * lax.axis_index("tpl")

    owners = pick_station // station_count
    order = lax.broadcasted_iota(jnp.int32, (group_size, group_size), 0)
    earlier = lax.broadcasted_iota(jnp.int32, (group_size, group_size), 1) < order
    landing = owners == my_index
    arrival = jnp.dot(earlier.astype(jnp.bfloat16), landing.astype(jnp.bfloat16),
                      preferred_element_type=jnp.float32).astype(jnp.int32)
    template_ids = lax.broadcasted_iota(jnp.int32, owners.shape, 0)
    packed = VALID + (pick_lag << 9) + ((pick_station - my_index * station_count) << 5) + template_ids
    places = lax.broadcasted_iota(jnp.int32, (CAP,) + owners.shape, 0)
    meta = jnp.sum(jnp.where(landing[None] & (arrival[None] == places), packed[None], 0), axis=1)

    frames, scales, slots = frames_and_scales(meta, mask, held)
    partial_sums = partial_stack(meta, slots, frames, scales, received)
    arrived = lax.all_to_all(partial_sums, "sta", split_axis=0, concat_axis=0, tiled=True)
    arrived = arrived.reshape(sta_size, CAP, -1).astype(jnp.float32)
    return jnp.sum(arrived, axis=0).reshape(NT // sta_size, group_size)


def solution(mesh):
    in_specs = (
        P(None, ("sta", "tpl"), None),
        P(None, "sta"),
        P("tpl", "sta", None, None),
        P("tpl", None),
        P("tpl", None),
    )
    return jax.shard_map(body, mesh=mesh, in_specs=in_specs, out_specs=P("sta", "tpl"), check_vma=False)
```

time: 82.8 us -> 74.4 us (0.90)
  the two profiles are of different devices: /device:TPU:2 before, /device:TPU:1 now
where the time goes in v3:
time: 74.4 us; the launch traced here: 73.9 us
  starting transfers between devices  21.9 us (29%)
  blocking collectives  19.3 us (26%)
  Pallas kernels  18 us (24%)
  local copies, waits for them, and re-layouts  12 us (16%)
  waiting for transfers between devices  2.23 us (3%)
    all_to_all x1, blocking collectives, body(): lax.all_to_all(partial_sums, 'sta', split_axis=0, concat_axis=0, tiled=True)  19.3 us
    ppermute x7, starting transfers between devices, body(): lax.ppermute(tiles, 'tpl', [(i, (i + hop) % tpl_size) for i in range(tpl_...  12.3 us
    all_to_all x1, starting transfers between devices, body(): lax.all_to_all(outgoing, 'sta', split_axis=0, concat_axis=0, tiled=True)  9.6 us
    pallas_call x1, Pallas kernels, partial_stack(): pl.pallas_call(stack_kernel, out_shape=jax.ShapeDtypeStruct((slot_count,...  9.16 us
    pallas_call x1, Pallas kernels, frames_and_scales(): pl.pallas_call(records_kernel, out_shape=(jax.ShapeDtypeStruct((records,...  6.64 us
    unnamed x21, local copies, waits for them, and re-layouts  6.25 us
    all_to_all x2, local copies, waits for them, and re-layouts, body(): lax.all_to_all(outgoing, 'sta', split_axis=0, concat_axis=0, tiled=True)  3.87 us
    ppermute x7, waiting for transfers between devices, body(): lax.ppermute(tiles, 'tpl', [(i, (i + hop) % tpl_size) for i in range(tpl_...  2.22 us
  transfers between devices with their start and end apart: 8, of which 1 were waited for; matrix products, arithmetic and copies ran while one was open for 0% of the time, Pallas kernels for 12%

profile of v3, /device:TPU:1, one launch (start us, length us, event | category | flops | bytes accessed | tf_op | source)
XLA Modules:
  0.0 73.9 jit_solution(1595986354883468129)
XLA Ops:
  0.0 1.1 %reshape.24 = f32[3,2,100,32]{3,2,1,0:T(8,128)S(1)} reshape(f32[3,2,3200]{2,1,0:T(2,128)} %param.5) | data formatting | bytes 153600 | tf_op jit(solution)/shard_map/reshape | solution.py:234
  1.3 2.6 %collective-permute-start = (f32[6,32,128]{2,1,0:T(8,128)S(1)}, f32[6,32,128]{2,1,0:T(8,128)S(1)}, u32[]{:S(2)}, u32[]{:S(2)}) collective-permute-start(f32[6,32,128]{2,1,0:T(8,128)S(1)} %bitcast.7), channel_id=1, source_target_pairs={{0,1},{1,2},{2,3},{3,4},{4,5},{5,6},{6,7},{7,0},{8,9},{9,10},{10,1... | collective-permute-start | bytes 294920 | tf_op jit(solution)/shard_map/ppermute | solution.py:239
  3.9 1.2 %collective-permute-start.1 = (f32[6,32,128]{2,1,0:T(8,128)S(1)}, f32[6,32,128]{2,1,0:T(8,128)S(1)}, u32[]{:S(2)}, u32[]{:S(2)}) collective-permute-start(f32[6,32,128]{2,1,0:T(8,128)S(1)} %bitcast.8), channel_id=1, source_target_pairs={{0,2},{1,3},{2,4},{3,5},{4,6},{5,7},{6,0},{7,1},{8,10},{9,11},{10,... | collective-permute-start | bytes 294920 | tf_op jit(solution)/shard_map/ppermute | solution.py:239
  5.1 1.6 %collective-permute-start.2 = (f32[6,32,128]{2,1,0:T(8,128)S(1)}, f32[6,32,128]{2,1,0:T(8,128)S(1)}, u32[]{:S(2)}, u32[]{:S(2)}) collective-permute-start(f32[6,32,128]{2,1,0:T(8,128)S(1)} %bitcast.9), channel_id=1, source_target_pairs={{0,3},{1,4},{2,5},{3,6},{4,7},{5,0},{6,1},{7,2},{8,11},{9,12},{10,... | collective-permute-start | bytes 294920 | tf_op jit(solution)/shard_map/ppermute | solution.py:239
  6.7 1.5 %collective-permute-start.3 = (f32[6,32,128]{2,1,0:T(8,128)S(1)}, f32[6,32,128]{2,1,0:T(8,128)S(1)}, u32[]{:S(2)}, u32[]{:S(2)}) collective-permute-start(f32[6,32,128]{2,1,0:T(8,128)S(1)} %bitcast.10), channel_id=1, source_target_pairs={{0,4},{1,5},{2,6},{3,7},{4,0},{5,1},{6,2},{7,3},{8,12},{9,13},{10,... | collective-permute-start | bytes 294920 | tf_op jit(solution)/shard_map/ppermute | solution.py:239
  8.2 2.6 %collective-permute-start.4 = (f32[6,32,128]{2,1,0:T(8,128)S(1)}, f32[6,32,128]{2,1,0:T(8,128)S(1)}, u32[]{:S(2)}, u32[]{:S(2)}) collective-permute-start(f32[6,32,128]{2,1,0:T(8,128)S(1)} %bitcast.11), channel_id=1, source_target_pairs={{0,5},{1,6},{2,7},{3,0},{4,1},{5,2},{6,3},{7,4},{8,13},{9,14},{10,... | collective-permute-start | bytes 294920 | tf_op jit(solution)/shard_map/ppermute | solution.py:239
  10.9 2.2 %select_waves.1 = bf16[128,1920]{1,0:T(8,128)(2,1)} custom-call(s32[1]{0:T(128)} %bitcast.2.index_ref, s32[32,32]{1,0:T(8,128)} %station_ref.1, bf16[3,32,640]{2,1,0:T(8,128)(2,1)} %bitcast.16), custom_call_target="tpu_custom_call" | custom-call | tf_op jit(solution)/shard_map/select_waves/pallas_call | solution.py:174
  13.0 1.9 %all_to_all.13 = bf16[32,4,1920]{2,1,0:T(4,128)(2,1)} reshape(bf16[128,1920]{1,0:T(8,128)(2,1)} %select_waves.1) | data formatting | bytes 983040 | tf_op jit(solution)/shard_map/all_to_all | solution.py:232
  15.0 9.6 %all-to-all-start = ((bf16[32,4,1920]{2,1,0:T(4,128)(2,1)}), bf16[32,4,1920]{2,1,0:T(4,128)(2,1)}, u32[]{:S(2)}, u32[]{:S(2)}) async-start(bf16[32,4,1920]{2,1,0:T(4,128)(2,1)} %all_to_all.13), calls=%async_computation | async-start | bytes 983040 | tf_op jit(solution)/shard_map/all_to_all | solution.py:232
  24.8 0.7 %collective-permute-start.5 = (f32[6,32,128]{2,1,0:T(8,128)S(1)}, f32[6,32,128]{2,1,0:T(8,128)S(1)}, u32[]{:S(2)}, u32[]{:S(2)}) collective-permute-start(f32[6,32,128]{2,1,0:T(8,128)S(1)} %bitcast.12), channel_id=1, source_target_pairs={{0,6},{1,7},{2,0},{3,1},{4,2},{5,3},{6,4},{7,5},{8,14},{9,15},{10,... | collective-permute-start | bytes 294920 | tf_op jit(solution)/shard_map/ppermute | solution.py:239
  25.5 2.0 %collective-permute-start.6 = (f32[6,32,128]{2,1,0:T(8,128)S(1)}, f32[6,32,128]{2,1,0:T(8,128)S(1)}, u32[]{:S(2)}, u32[]{:S(2)}) collective-permute-start(f32[6,32,128]{2,1,0:T(8,128)S(1)} %bitcast.13), channel_id=1, source_target_pairs={{0,7},{1,0},{2,1},{3,2},{4,3},{5,4},{6,5},{7,6},{8,15},{9,8},{10,9... | collective-permute-start | bytes 294920 | tf_op jit(solution)/shard_map/ppermute | solution.py:239
  27.6 0.6 copy-done.3
  28.2 0.6 copy-done.5
  28.8 2.2 %collective-permute-done.6.refs_7_ = f32[6,32,128]{2,1,0:T(8,128)S(1)} collective-permute-done((f32[6,32,128]{2,1,0:T(8,128)S(1)}, f32[6,32,128]{2,1,0:T(8,128)S(1)}, u32[]{:S(2)}, u32[]{:S(2)}) %collective-permute-start.6) | collective-permute-done | bytes 98336 | tf_op jit(solution)/shard_map/ppermute | solution.py:239
  31.1 0.9 %copy-done.4 = f32[6,32,128]{2,1,0:T(8,128)S(1)} copy-done((f32[6,32,128]{2,1,0:T(8,128)S(1)}, f32[6,32,128]{2,1,0:T(8,128)}, u32[]{:S(2)}) %copy-start.4) | copy-done | bytes 98328
  31.9 0.9 %copy-done.6 = f32[6,32,128]{2,1,0:T(8,128)S(1)} copy-done((f32[6,32,128]{2,1,0:T(8,128)S(1)}, f32[6,32,128]{2,1,0:T(8,128)}, u32[]{:S(2)}) %copy-start.6) | copy-done | bytes 98328
  32.8 6.6 %frames_and_scales.1 = (bf16[48,256,128]{2,1,0:T(8,128)(2,1)S(1)}, f32[48,32,128]{2,1,0:T(8,128)S(1)}, s32[130]{0:T(256)S(1)}) custom-call(s32[4,32]{1,0:T(4,128)S(1)} %select_reduce_fusion.meta_ref, s32[3,16]{1,0:T(4,128)S(1)} %broadcast_add_fusion.mask_ref, f32[6,32,128]{2,1,0:T(8,128)S(1)} %bitcast.14, f32[6,32,128]{2,1,0:T(8,128)S(1)} %collective-permute-done.refs_1_, ...), custom_call_target="tpu_custom_call" | custom-call | flops 20000000 | bytes 5000000 | tf_op jit(solution)/shard_map/frames_and_scales/pallas_call | solution.py:186
  39.5 0.9 %copy-done.1 = f32[48,32,128]{2,1,0:T(8,128)} copy-done((f32[48,32,128]{2,1,0:T(8,128)}, f32[48,32,128]{2,1,0:T(8,128)S(1)}, u32[]{:S(2)}) %copy-start.1) | copy-done | bytes 786456
  40.4 1.9 %all_to_all.15.waves_ref = bf16[128,1920]{1,0:T(8,128)(2,1)} reshape(bf16[32,4,1920]{2,1,0:T(4,128)(2,1)} %all-to-all-done) | data formatting | bytes 983040 | tf_op jit(solution)/shard_map/all_to_all | solution.py:232
  42.3 1.0 %copy-done = bf16[128,1920]{1,0:T(8,128)(2,1)S(1)} copy-done((bf16[128,1920]{1,0:T(8,128)(2,1)S(1)}, bf16[128,1920]{1,0:T(8,128)(2,1)}, u32[]{:S(2)}) %copy-start) | copy-done | bytes 491544
  43.4 1.1 %copy-done.2 = f32[48,32,128]{2,1,0:T(8,128)S(1)} copy-done((f32[48,32,128]{2,1,0:T(8,128)S(1)}, f32[48,32,128]{2,1,0:T(8,128)}, u32[]{:S(2)}) %copy-start.2) | copy-done | bytes 786456
  44.5 9.2 %stack_picks.1 = bf16[128,384]{1,0:T(8,128)(2,1)S(1)} custom-call(s32[4,32]{1,0:T(4,128)S(1)} %select_reduce_fusion.meta_ref, s32[130]{0:T(256)S(1)} %get-tuple-element.8.slots, bf16[48,256,128]{2,1,0:T(8,128)(2,1)S(1)} %get-tuple-element.9.frames, f32[48,32,128]{2,1,0:T(8,128)S(1)} %copy-done.2, bf16[128,1920]{1,0:T(8,128)(2,1)S(1)} %copy-done), custom_call_target="tpu_custom_call" | custom-call | flops 200000000 | bytes 8000000 | tf_op jit(solution)/shard_map/stack_picks/pallas_call | solution.py:205
  53.7 19.3 %all_to_all.20 = bf16[32,4,384]{2,1,0:T(4,128)(2,1)S(1)} all-to-all(bf16[32,4,384]{2,1,0:T(4,128)(2,1)S(1)} %all_to_all.16), channel_id=1, replica_groups=mesh['sta'=32,'tpl'=8] {'sta'}, dimensions={0} | all-to-all | bytes 196608 | tf_op jit(solution)/shard_map/all_to_all | solution.py:255
  73.2 0.7 copy.10
  (30 shorter events, 0.6 us)
Async XLA Ops:
  0.0 24.6 %copy-start.7 = (s32[32,32]{1,0:T(8,128)S(1)}, s32[32,32]{1,0:T(8,128)}, u32[]{:S(2)}) copy-start(s32[32,32]{1,0:T(8,128)} %station_ref.1) | copy-start | bytes 12292
  0.0 24.8 %copy-start.8 = (s32[32,32]{1,0:T(8,128)S(1)}, s32[32,32]{1,0:T(8,128)}, u32[]{:S(2)}) copy-start(s32[32,32]{1,0:T(8,128)} %param.9) | copy-start | bytes 12292
  0.0 24.8 %copy-start.9 = (s32[3,16]{1,0:T(4,128)S(1)}, s32[3,16]{1,0:T(4,128)}, u32[]{:S(2)}) copy-start(s32[3,16]{1,0:T(4,128)} %param.6) | copy-start | bytes 580
  1.3 23.5 %collective-permute-start = (f32[6,32,128]{2,1,0:T(8,128)S(1)}, f32[6,32,128]{2,1,0:T(8,128)S(1)}, u32[]{:S(2)}, u32[]{:S(2)}) collective-permute-start(f32[6,32,128]{2,1,0:T(8,128)S(1)} %bitcast.7), channel_id=1, source_target_pairs={{0,1},{1,2},{2,3},{3,4},{4,5},{5,6},{6,7},{7,0},{8,9},{9,10},{10,1... | collective-permute-start | bytes 294920 | tf_op jit(solution)/shard_map/ppermute | solution.py:239
  3.9 21.7 %collective-permute-start.1 = (f32[6,32,128]{2,1,0:T(8,128)S(1)}, f32[6,32,128]{2,1,0:T(8,128)S(1)}, u32[]{:S(2)}, u32[]{:S(2)}) collective-permute-start(f32[6,32,128]{2,1,0:T(8,128)S(1)} %bitcast.8), channel_id=1, source_target_pairs={{0,2},{1,3},{2,4},{3,5},{4,6},{5,7},{6,0},{7,1},{8,10},{9,11},{10,... | collective-permute-start | bytes 294920 | tf_op jit(solution)/shard_map/ppermute | solution.py:239
  5.1 22.5 %collective-permute-start.2 = (f32[6,32,128]{2,1,0:T(8,128)S(1)}, f32[6,32,128]{2,1,0:T(8,128)S(1)}, u32[]{:S(2)}, u32[]{:S(2)}) collective-permute-start(f32[6,32,128]{2,1,0:T(8,128)S(1)} %bitcast.9), channel_id=1, source_target_pairs={{0,3},{1,4},{2,5},{3,6},{4,7},{5,0},{6,1},{7,2},{8,11},{9,12},{10,... | collective-permute-start | bytes 294920 | tf_op jit(solution)/shard_map/ppermute | solution.py:239
  6.7 20.9 %collective-permute-start.3 = (f32[6,32,128]{2,1,0:T(8,128)S(1)}, f32[6,32,128]{2,1,0:T(8,128)S(1)}, u32[]{:S(2)}, u32[]{:S(2)}) collective-permute-start(f32[6,32,128]{2,1,0:T(8,128)S(1)} %bitcast.10), channel_id=1, source_target_pairs={{0,4},{1,5},{2,6},{3,7},{4,0},{5,1},{6,2},{7,3},{8,12},{9,13},{10,... | collective-permute-start | bytes 294920 | tf_op jit(solution)/shard_map/ppermute | solution.py:239
  8.2 20.0 %collective-permute-start.4 = (f32[6,32,128]{2,1,0:T(8,128)S(1)}, f32[6,32,128]{2,1,0:T(8,128)S(1)}, u32[]{:S(2)}, u32[]{:S(2)}) collective-permute-start(f32[6,32,128]{2,1,0:T(8,128)S(1)} %bitcast.11), channel_id=1, source_target_pairs={{0,5},{1,6},{2,7},{3,0},{4,1},{5,2},{6,3},{7,4},{8,13},{9,14},{10,... | collective-permute-start | bytes 294920 | tf_op jit(solution)/shard_map/ppermute | solution.py:239
  15.0 25.4 %all-to-all-start = ((bf16[32,4,1920]{2,1,0:T(4,128)(2,1)}), bf16[32,4,1920]{2,1,0:T(4,128)(2,1)}, u32[]{:S(2)}, u32[]{:S(2)}) async-start(bf16[32,4,1920]{2,1,0:T(4,128)(2,1)} %all_to_all.13), calls=%async_computation | async-start | bytes 983040 | tf_op jit(solution)/shard_map/all_to_all | solution.py:232
  24.8 4.0 %collective-permute-start.5 = (f32[6,32,128]{2,1,0:T(8,128)S(1)}, f32[6,32,128]{2,1,0:T(8,128)S(1)}, u32[]{:S(2)}, u32[]{:S(2)}) collective-permute-start(f32[6,32,128]{2,1,0:T(8,128)S(1)} %bitcast.12), channel_id=1, source_target_pairs={{0,6},{1,7},{2,0},{3,1},{4,2},{5,3},{6,4},{7,5},{8,14},{9,15},{10,... | collective-permute-start | bytes 294920 | tf_op jit(solution)/shard_map/ppermute | solution.py:239
  25.5 5.5 %collective-permute-start.6 = (f32[6,32,128]{2,1,0:T(8,128)S(1)}, f32[6,32,128]{2,1,0:T(8,128)S(1)}, u32[]{:S(2)}, u32[]{:S(2)}) collective-permute-start(f32[6,32,128]{2,1,0:T(8,128)S(1)} %bitcast.13), channel_id=1, source_target_pairs={{0,7},{1,0},{2,1},{3,2},{4,3},{5,4},{6,5},{7,6},{8,15},{9,8},{10,9... | collective-permute-start | bytes 294920 | tf_op jit(solution)/shard_map/ppermute | solution.py:239
  27.6 0.6 copy-start.3
  28.2 0.6 copy-start.5
  31.0 0.9 %copy-start.4 = (f32[6,32,128]{2,1,0:T(8,128)S(1)}, f32[6,32,128]{2,1,0:T(8,128)}, u32[]{:S(2)}) copy-start(f32[6,32,128]{2,1,0:T(8,128)} %copy-done.3) | copy-start | bytes 294916
  31.9 0.9 %copy-start.6 = (f32[6,32,128]{2,1,0:T(8,128)S(1)}, f32[6,32,128]{2,1,0:T(8,128)}, u32[]{:S(2)}) copy-start(f32[6,32,128]{2,1,0:T(8,128)} %copy-done.5) | copy-start | bytes 294916
  39.5 0.9 %copy-start.1 = (f32[48,32,128]{2,1,0:T(8,128)}, f32[48,32,128]{2,1,0:T(8,128)S(1)}, u32[]{:S(2)}) copy-start(f32[48,32,128]{2,1,0:T(8,128)S(1)} %get-tuple-element.10.scales) | copy-start | bytes 2359300
  42.3 1.0 %copy-start = (bf16[128,1920]{1,0:T(8,128)(2,1)S(1)}, bf16[128,1920]{1,0:T(8,128)(2,1)}, u32[]{:S(2)}) copy-start(bf16[128,1920]{1,0:T(8,128)(2,1)} %all_to_all.15.waves_ref) | copy-start | bytes 1474564
  43.4 1.1 %copy-start.2 = (f32[48,32,128]{2,1,0:T(8,128)S(1)}, f32[48,32,128]{2,1,0:T(8,128)}, u32[]{:S(2)}) copy-start(f32[48,32,128]{2,1,0:T(8,128)} %copy-done.1) | copy-start | bytes 2359300

commit v4 on v3

--- a/solution.py
+++ b/solution.py
@@ -16,7 +16,8 @@
 OUT_BLOCKS = NT // STEP
 TILES = L // LANES
 TURNS = 8
-UNROLL = 2
+UNROLL = 8
+SLOT_ROWS = 64
 STATION_BITS = 4
 EPSILON = 1e-05
 VALID = 1 << 20
@@ -53,7 +54,7 @@
     return whole[:, None, :] + inner
 
 
-def select_kernel(index_ref, station_ref, waves_ref, out_ref):
+def select_kernel(index_ref, station_ref, waves_ref, out_ref, staged):
     group_size = station_ref.shape[0]
     square = (group_size, group_size)
     row = lax.broadcasted_iota(jnp.int32, square, 0)
@@ -65,15 +66,24 @@
     same = (down == across) & (row < column)
     place = jnp.sum(same.astype(jnp.int32), axis=0, keepdims=True)
     slot = across * CAP + place
-    slots = lax.broadcasted_iota(jnp.int32, (out_ref.shape[0], group_size), 0)
-    select = (slots == slot).astype(jnp.float32).astype(jnp.bfloat16)
+    peers = out_ref.shape[0]
+    peer = lax.broadcasted_iota(jnp.int32, (peers, group_size), 0)
+    selects = [(peer * CAP + k == slot).astype(jnp.float32).astype(jnp.bfloat16) for k in range(CAP)]
+    select = jnp.concatenate(selects, axis=0)
     for c in range(3):
         values = waves_ref[c].astype(jnp.float32)
         centred = values - jnp.mean(values, axis=-1, keepdims=True)
         power = jnp.mean(centred * centred, axis=-1, keepdims=True)
         unit = (centred / jnp.sqrt(power + EPSILON)).astype(jnp.bfloat16)
         picked = jnp.dot(select, unit, preferred_element_type=jnp.float32)
-        out_ref[:, c * L:(c + 1) * L] = picked.astype(jnp.bfloat16)
+        for tile in range(TILES):
+            columns = slice(tile * LANES, (tile + 1) * LANES)
+            for k in range(CAP):
+                at = (c * TILES + tile) * CAP + k
+                staged[pl.ds(at, peers, stride=SLOT_ROWS), :] = picked[k * peers:(k + 1) * peers, columns]
+    for at in range(3 * TILES * CAP, SLOT_ROWS):
+        staged[pl.ds(at, peers, stride=SLOT_ROWS), :] = jnp.zeros((peers, LANES), jnp.float32)
+    out_ref[...] = staged[...].astype(jnp.bfloat16).reshape(out_ref.shape)
 
 
 def records_kernel(meta_ref, mask_ref, *refs):
@@ -85,34 +95,35 @@
         return count + held
 
     total = meta_ref.shape[1] * CAP
-    count = lax.fori_loop(0, total, list_slot, jnp.int32(0))
-    slots[count] = -1
-    slots[total + 1] = count
+    count = lax.fori_loop(0, total, list_slot, jnp.int32(0), unroll=16)
+    for spare in range(UNROLL):
+        slots[count + spare] = -1
+    slots[total + UNROLL] = count
 
     here = mask_ref[0, 0] >> 1
-    for hop, tile_ref in enumerate(tile_refs):
-        owner = (here - hop) & (len(tile_refs) - 1)
-        size = tile_ref.shape[0]
-        first = owner * size
-        values = tile_ref[...].reshape(size * STEP, LANES)
-        for turn in range(TURNS):
-            rolled = values if turn == 0 else pltpu.roll(values, LANES - turn, 1)
-            frames[pl.ds(first, size), turn * STEP:(turn + 1) * STEP, :] = (
-                rolled.astype(jnp.bfloat16).reshape(size, STEP, LANES)
-            )
-        mean_one = window_sums(values) * (1.0 / L)
-        mean_two = window_sums(values * values) * (1.0 / L)
-        spread = L * jnp.sqrt(mean_two - mean_one * mean_one + EPSILON)
-        for within in range(size):
-            weight = (mask_ref[within >> 1, owner * 2 + (within & 1)] & 1).astype(jnp.float32)
-            scales[first + within] = weight / spread[within]
+    for core, tile_ref in enumerate(tile_refs):
+        size = 6
+        for hop in range(tile_ref.shape[0] // size):
+            owner = ((here - 2 * hop) & (2 * (tile_ref.shape[0] // size) - 1)) ^ core
+            first = owner * size
+            values = tile_ref[hop * size:(hop + 1) * size].reshape(size * STEP, LANES)
+            for turn in range(TURNS):
+                rolled = values if turn == 0 else pltpu.roll(values, LANES - turn, 1)
+                frames[pl.ds(first, size), turn * STEP:(turn + 1) * STEP, :] = (
+                    rolled.astype(jnp.bfloat16).reshape(size, STEP, LANES)
+                )
+            mean_one = window_sums(values) * (1.0 / L)
+            mean_two = window_sums(values * values) * (1.0 / L)
+            factor = lax.rsqrt(mean_two - mean_one * mean_one + EPSILON)
+            for within in range(size):
+                weight = mask_ref[within >> 1, owner * 2 + (within & 1)] & 1
+                weight = weight.astype(jnp.float32) * (1.0 / L)
+                scales[first + within] = factor[within] * weight
 
 
 def stack_kernel(meta_ref, slots, frames, scales, waves_ref, out_ref, units, acc, twice, dense):
-    slot_count = waves_ref.shape[0]
-    count = slots[slot_count + 1]
-    for start in range(3 * TILES):
-        units[start] = waves_ref[:, start * LANES:(start + 1) * LANES].astype(jnp.float32)
+    count = slots[slots.shape[0] - 1]
+    units[...] = waves_ref[...].reshape(units.shape).astype(jnp.float32)
     acc[...] = jnp.zeros_like(acc)
     row = lax.broadcasted_iota(jnp.int32, (STEP, LANES), 0)
     lane = lax.broadcasted_iota(jnp.int32, (STEP, LANES), 1)
@@ -131,7 +142,8 @@
             before = jnp.zeros((STEP, LANES), jnp.float32)
             columns = []
             for tile in range(TILES):
-                wave = units[c * TILES + tile, pl.ds(slot, STEP, stride=0), :]
+                at = (slot >> 2) * SLOT_ROWS + (c * TILES + tile) * CAP + (slot & (CAP - 1))
+                wave = units[pl.ds(at, STEP, stride=0), :]
                 spread = pltpu.roll(wave, 0, 1, stride=1, stride_axis=0)
                 columns.append(jnp.where(own, spread, before).astype(jnp.bfloat16))
                 before = spread
@@ -170,12 +182,15 @@
 VMEM = pl.BlockSpec(memory_space=pltpu.VMEM)
 
 
-def slot_waves(my_index, pick_station, template_waves, slot_count):
+def slot_waves(my_index, pick_station, template_waves, peers):
     return pl.pallas_call(
         select_kernel,
-        out_shape=jax.ShapeDtypeStruct((slot_count, 3 * L), jnp.bfloat16),
+        out_shape=jax.ShapeDtypeStruct((peers, SLOT_ROWS, LANES), jnp.bfloat16),
         in_specs=[SMEM, VMEM, VMEM],
         out_specs=VMEM,
+        scratch_shapes=[pltpu.VMEM((peers * SLOT_ROWS, LANES), jnp.float32)],
+        compiler_params=pltpu.CompilerParams(vmem_limit_bytes=4 * 1024 * 1024),
+        cost_estimate=pl.CostEstimate(flops=16_000_000, transcendentals=100, bytes_accessed=620_000),
         name="select_waves",
     )(my_index.reshape(1), pick_station, template_waves)
 
@@ -188,11 +203,11 @@
         out_shape=(
             jax.ShapeDtypeStruct((records, TURNS * STEP, LANES), jnp.bfloat16),
             jax.ShapeDtypeStruct((records, STEP, LANES), jnp.float32),
-            jax.ShapeDtypeStruct((slot_count + 2,), jnp.int32),
+            jax.ShapeDtypeStruct((slot_count + UNROLL + 1,), jnp.int32),
         ),
         in_specs=[SMEM, SMEM] + [VMEM] * len(tiles),
         out_specs=(VMEM, VMEM, SMEM),
-        compiler_params=pltpu.CompilerParams(vmem_limit_bytes=16 * 1024 * 1024),
+        compiler_params=pltpu.CompilerParams(vmem_limit_bytes=10 * 1024 * 1024),
         cost_estimate=pl.CostEstimate(flops=20_000_000, transcendentals=200_000, bytes_accessed=5_000_000),
         name="frames_and_scales",
     )(meta, mask, *tiles)
@@ -200,7 +215,7 @@
 
 def partial_stack(meta, slots, frames, scales, received):
     group_size = meta.shape[1]
-    slot_count = received.shape[0]
+    slot_count = received.shape[0] * CAP
     rows = NT * group_size // LANES
     return pl.pallas_call(
         stack_kernel,
@@ -208,12 +223,12 @@
         in_specs=[SMEM, SMEM, VMEM, VMEM, VMEM],
         out_specs=VMEM,
         scratch_shapes=[
-            pltpu.VMEM((3 * TILES, slot_count, LANES), jnp.float32),
+            pltpu.VMEM((received.shape[0] * SLOT_ROWS, LANES), jnp.float32),
             pltpu.VMEM(((group_size + 1) * STEP, LANES), jnp.float32),
             pltpu.VMEM((UNROLL, 2 * STEP, LANES), jnp.float32),
             pltpu.VMEM((rows, LANES), jnp.float32),
         ],
-        compiler_params=pltpu.CompilerParams(vmem_limit_bytes=20 * 1024 * 1024),
+        compiler_params=pltpu.CompilerParams(vmem_limit_bytes=10 * 1024 * 1024),
         cost_estimate=pl.CostEstimate(flops=200_000_000, transcendentals=0, bytes_accessed=8_000_000),
         name="stack_picks",
     )(meta, slots, frames, scales, received)
@@ -228,15 +243,17 @@
     stations_here = station_data.shape[1]
 
     waves = template_waves.reshape(group_size, 3, L).transpose(1, 0, 2)
-    outgoing = slot_waves(my_index, pick_station, waves, sta_size * CAP)
+    outgoing = slot_waves(my_index, pick_station, waves, sta_size)
     received = lax.all_to_all(outgoing, "sta", split_axis=0, concat_axis=0, tiled=True)
 
     tiles = station_data.reshape(3, stations_here, BLOCKS, STEP).transpose(0, 1, 3, 2)
     tiles = jnp.pad(tiles, ((0, 0), (0, 0), (0, 0), (0, LANES - BLOCKS)))
     tiles = tiles.reshape(3 * stations_here, STEP, LANES)
-    held = [tiles]
-    for hop in range(1, tpl_size):
-        held.append(lax.ppermute(tiles, "tpl", [(i, (i + hop) % tpl_size) for i in range(tpl_size)]))
+    row = [tiles]
+    for hop in range(2, tpl_size, 2):
+        row.append(lax.ppermute(tiles, "tpl", [(i, (i + hop) % tpl_size) for i in range(tpl_size)]))
+    row = jnp.concatenate(row, axis=0)
+    held = [row, lax.ppermute(row, "tpl", [(i, i ^ 1) for i in range(tpl_size)])]
     mask = channel_mask + 2 * lax.axis_index("tpl")
 
     owners = pick_station // station_count

time: 74.4 us -> 60.5 us (0.81)
  the two profiles are of different devices: /device:TPU:1 before, /device:TPU:2 now
where the time goes in v4:
time: 60.5 us; the launch traced here: 59.5 us
  starting transfers between devices  16.5 us (27%)
  blocking collectives  15 us (25%)
  Pallas kernels  12.2 us (20%)
  local copies, waits for them, and re-layouts  7.37 us (12%)
  waiting for transfers between devices  6.4 us (11%)
  other arithmetic  1.61 us (3%)
    all_to_all x1, blocking collectives, body(): lax.all_to_all(partial_sums, 'sta', split_axis=0, concat_axis=0, tiled=True)  15 us
    all_to_all x1, starting transfers between devices, body(): lax.all_to_all(outgoing, 'sta', split_axis=0, concat_axis=0, tiled=True)  11.6 us
    pallas_call x1, Pallas kernels, frames_and_scales(): pl.pallas_call(records_kernel, out_shape=(jax.ShapeDtypeStruct((records,...  5.65 us
    unnamed x15, local copies, waits for them, and re-layouts  5.49 us
    all_to_all x1, waiting for transfers between devices, body(): lax.all_to_all(outgoing, 'sta', split_axis=0, concat_axis=0, tiled=True)  4.87 us
    ppermute x3, starting transfers between devices, body(): lax.ppermute(tiles, 'tpl', [(i, (i + hop) % tpl_size) for i in range(tpl_...  4.83 us
    pallas_call x1, Pallas kernels, partial_stack(): pl.pallas_call(stack_kernel, out_shape=jax.ShapeDtypeStruct((slot_count,...  4.78 us
    pallas_call x1, Pallas kernels, slot_waves(): pl.pallas_call(select_kernel, out_shape=jax.ShapeDtypeStruct((peers, SLOT...  1.81 us
  transfers between devices with their start and end apart: 5, of which 2 were waited for; matrix products, arithmetic and copies ran while one was open for 3% of the time, Pallas kernels for 13%

profile of v4, /device:TPU:2, one launch (start us, length us, event | category | flops | bytes accessed | tf_op | source)
XLA Modules:
  0.0 59.5 jit_solution(14100541773717441949)
XLA Ops:
  0.0 1.1 %reshape.22 = f32[3,2,100,32]{3,2,1,0:T(8,128)S(1)} reshape(f32[3,2,3200]{2,1,0:T(2,128)} %param.5) | data formatting | bytes 153600 | tf_op jit(solution)/shard_map/reshape | solution.py:249
  1.1 0.1 copy.11
  1.2 1.6 %collective-permute-start = (f32[6,32,128]{2,1,0:T(8,128)S(1)}, f32[6,32,128]{2,1,0:T(8,128)S(1)}, u32[]{:S(2)}, u32[]{:S(2)}) collective-permute-start(f32[6,32,128]{2,1,0:T(8,128)S(1)} %bitcast.9), channel_id=1, source_target_pairs={{0,2},{1,3},{2,4},{3,5},{4,6},{5,7},{6,0},{7,1},{8,10},{9,11},{10,... | collective-permute-start | bytes 294920 | tf_op jit(solution)/shard_map/ppermute | solution.py:254
  2.8 2.8 %collective-permute-start.1 = (f32[6,32,128]{2,1,0:T(8,128)S(1)}, f32[6,32,128]{2,1,0:T(8,128)S(1)}, u32[]{:S(2)}, u32[]{:S(2)}) collective-permute-start(f32[6,32,128]{2,1,0:T(8,128)S(1)} %bitcast.10), channel_id=1, source_target_pairs={{0,4},{1,5},{2,6},{3,7},{4,0},{5,1},{6,2},{7,3},{8,12},{9,13},{10,... | collective-permute-start | bytes 294920 | tf_op jit(solution)/shard_map/ppermute | solution.py:254
  5.6 0.4 collective-permute-start.2
  6.1 0.7 %copy-done.4 = s32[32,32]{1,0:T(8,128)S(1)} copy-done((s32[32,32]{1,0:T(8,128)S(1)}, s32[32,32]{1,0:T(8,128)}, u32[]{:S(2)}) %copy-start.4) | copy-done | bytes 4120
  6.8 0.9 %copy-done.5 = bf16[32,1,3,640]{3,0,2,1:T(8,128)(2,1)S(1)} copy-done((bf16[32,1,3,640]{3,0,2,1:T(8,128)(2,1)S(1)}, bf16[32,1,3,640]{3,0,2,1:T(8,128)(2,1)}, u32[]{:S(2)}) %copy-start.5) | copy-done | bytes 122904
  7.7 1.8 %select_waves.1 = bf16[32,64,128]{2,1,0:T(8,128)(2,1)} custom-call(s32[1]{0:T(128)} %bitcast.2.index_ref, s32[32,32]{1,0:T(8,128)S(1)} %copy-done.4, bf16[3,32,640]{2,1,0:T(8,128)(2,1)S(1)} %bitcast.7), custom_call_target="tpu_custom_call" | custom-call | flops 16000000 | bytes 620000 | tf_op jit(solution)/shard_map/select_waves/pallas_call | solution.py:186
  9.5 11.6 %all-to-all-start = ((bf16[32,64,128]{2,1,0:T(8,128)(2,1)}), bf16[32,64,128]{2,1,0:T(8,128)(2,1)}, u32[]{:S(2)}, u32[]{:S(2)}) async-start(bf16[32,64,128]{2,1,0:T(8,128)(2,1)} %select_waves.1), calls=%async_computation | async-start | bytes 1048576 | tf_op jit(solution)/shard_map/all_to_all | solution.py:247
  21.1 0.7 %iota_add_fusion = s32[32,32]{1,0:T(8,128)S(1)} fusion(s32[32,32]{1,0:T(8,128)} %station_ref.1, s32[32,32]{1,0:T(8,128)} %param.9, s32[]{:T(128)S(6)} %mul.3), kind=kLoop, calls=%fused_computation.12 | loop fusion | flops 6144 | bytes 12292 | tf_op jit(solution)/shard_map/add | solution.py:266
  21.9 0.7 %fusion.2 = pred[32,32]{1,0:T(8,128)(4,1)S(1)} fusion(s32[32,32]{1,0:T(8,128)} %station_ref.1, s32[]{:T(128)} %axis_index.23), kind=kLoop, calls=%fused_computation.11 | loop fusion | flops 16384 | bytes 5124 | tf_op jit(solution)/shard_map/eq | solution.py:262
  22.7 0.1 collective-permute-start.3
  22.8 0.1 convolution_convert_fusion
  23.0 1.5 %collective-permute-done.3.refs_1_ = f32[24,32,128]{2,1,0:T(8,128)S(1)} collective-permute-done((f32[24,32,128]{2,1,0:T(8,128)S(1)}, f32[24,32,128]{2,1,0:T(8,128)S(1)}, u32[]{:S(2)}, u32[]{:S(2)}) %collective-permute-start.3) | collective-permute-done | bytes 393248 | tf_op jit(solution)/shard_map/ppermute | solution.py:256
  24.5 0.7 %copy-done.2 = f32[24,32,128]{2,1,0:T(8,128)} copy-done((f32[24,32,128]{2,1,0:T(8,128)}, f32[24,32,128]{2,1,0:T(8,128)S(1)}, u32[]{:S(2)}) %copy-start.2) | copy-done | bytes 393240
  25.2 1.0 %copy-done.3 = f32[24,32,128]{2,1,0:T(8,128)S(1)} copy-done((f32[24,32,128]{2,1,0:T(8,128)S(1)}, f32[24,32,128]{2,1,0:T(8,128)}, u32[]{:S(2)}) %copy-start.3) | copy-done | bytes 393240
  26.2 5.7 %frames_and_scales.1 = (bf16[48,256,128]{2,1,0:T(8,128)(2,1)S(1)}, f32[48,32,128]{2,1,0:T(8,128)S(1)}, s32[137]{0:T(256)S(1)}) custom-call(s32[4,32]{1,0:T(4,128)S(1)} %select_reduce_fusion.meta_ref, s32[3,16]{1,0:T(4,128)S(1)} %broadcast_add_fusion.mask_ref, f32[24,32,128]{2,1,0:T(8,128)S(1)} %pad_maximum_fusion.refs_0_, f32[24,32,128]{2,1,0:T(8,128)S(1)} %copy-done.3), custom_call_target="tpu_custom_call" | custom-call | flops 20000000 | bytes 5000000 | tf_op jit(solution)/shard_map/frames_and_scales/pallas_call | solution.py:201
  31.9 0.9 %copy-done = f32[48,32,128]{2,1,0:T(8,128)} copy-done((f32[48,32,128]{2,1,0:T(8,128)}, f32[48,32,128]{2,1,0:T(8,128)S(1)}, u32[]{:S(2)}) %copy-start) | copy-done | bytes 786456
  32.8 4.9 %all-to-all-done.waves_ref = bf16[32,64,128]{2,1,0:T(8,128)(2,1)} async-done(((bf16[32,64,128]{2,1,0:T(8,128)(2,1)}), bf16[32,64,128]{2,1,0:T(8,128)(2,1)}, u32[]{:S(2)}, u32[]{:S(2)}) %all-to-all-start) | async-done | bytes 524320 | tf_op jit(solution)/shard_map/all_to_all | solution.py:247
  37.6 1.1 %copy-done.1 = f32[48,32,128]{2,1,0:T(8,128)S(1)} copy-done((f32[48,32,128]{2,1,0:T(8,128)S(1)}, f32[48,32,128]{2,1,0:T(8,128)}, u32[]{:S(2)}) %copy-start.1) | copy-done | bytes 786456
  38.8 4.8 %stack_picks.1 = bf16[128,384]{1,0:T(8,128)(2,1)S(1)} custom-call(s32[4,32]{1,0:T(4,128)S(1)} %select_reduce_fusion.meta_ref, s32[137]{0:T(256)S(1)} %get-tuple-element.8.slots, bf16[48,256,128]{2,1,0:T(8,128)(2,1)S(1)} %get-tuple-element.9.frames, f32[48,32,128]{2,1,0:T(8,128)S(1)} %copy-done.1, bf16[32,64,128]{2,1,0:T(8,128)(2,1)} %all-to-all-done.waves_ref), custom_call_target="tpu_custom_call" | custom-call | flops 200000000 | bytes 8000000 | tf_op jit(solution)/shard_map/stack_picks/pallas_call | solution.py:220
  43.6 15.0 %all_to_all.14 = bf16[32,4,384]{2,1,0:T(4,128)(2,1)S(1)} all-to-all(bf16[32,4,384]{2,1,0:T(4,128)(2,1)S(1)} %all_to_all.10), channel_id=1, replica_groups=mesh['sta'=32,'tpl'=8] {'sta'}, dimensions={0} | all-to-all | bytes 196608 | tf_op jit(solution)/shard_map/all_to_all | solution.py:272
  58.7 0.1 reshape.26
  58.8 0.7 %copy.10 = f32[48,32]{0,1:T(8,128)} copy(f32[48,32]{1,0:T(8,128)S(1)} %reshape.26) | data formatting | bytes 12288 | tf_op jit(solution)/shard_map/reshape | solution.py:274
  (17 shorter events, 0.2 us)
Async XLA Ops:
  0.0 22.9 %copy-start.6 = (s32[3,16]{1,0:T(4,128)S(1)}, s32[3,16]{1,0:T(4,128)}, u32[]{:S(2)}) copy-start(s32[3,16]{1,0:T(4,128)} %param.6) | copy-start | bytes 580
  1.2 21.4 %collective-permute-start = (f32[6,32,128]{2,1,0:T(8,128)S(1)}, f32[6,32,128]{2,1,0:T(8,128)S(1)}, u32[]{:S(2)}, u32[]{:S(2)}) collective-permute-start(f32[6,32,128]{2,1,0:T(8,128)S(1)} %bitcast.9), channel_id=1, source_target_pairs={{0,2},{1,3},{2,4},{3,5},{4,6},{5,7},{6,0},{7,1},{8,10},{9,11},{10,... | collective-permute-start | bytes 294920 | tf_op jit(solution)/shard_map/ppermute | solution.py:254
  2.8 19.8 %collective-permute-start.1 = (f32[6,32,128]{2,1,0:T(8,128)S(1)}, f32[6,32,128]{2,1,0:T(8,128)S(1)}, u32[]{:S(2)}, u32[]{:S(2)}) collective-permute-start(f32[6,32,128]{2,1,0:T(8,128)S(1)} %bitcast.10), channel_id=1, source_target_pairs={{0,4},{1,5},{2,6},{3,7},{4,0},{5,1},{6,2},{7,3},{8,12},{9,13},{10,... | collective-permute-start | bytes 294920 | tf_op jit(solution)/shard_map/ppermute | solution.py:254
  5.6 17.0 %collective-permute-start.2 = (f32[6,32,128]{2,1,0:T(8,128)S(1)}, f32[6,32,128]{2,1,0:T(8,128)S(1)}, u32[]{:S(2)}, u32[]{:S(2)}) collective-permute-start(f32[6,32,128]{2,1,0:T(8,128)S(1)} %bitcast.11), channel_id=1, source_target_pairs={{0,6},{1,7},{2,0},{3,1},{4,2},{5,3},{6,4},{7,5},{8,14},{9,15},{10,... | collective-permute-start | bytes 294920 | tf_op jit(solution)/shard_map/ppermute | solution.py:254
  6.1 0.7 %copy-start.4 = (s32[32,32]{1,0:T(8,128)S(1)}, s32[32,32]{1,0:T(8,128)}, u32[]{:S(2)}) copy-start(s32[32,32]{1,0:T(8,128)} %station_ref.1) | copy-start | bytes 12292
  6.8 0.9 %copy-start.5 = (bf16[32,1,3,640]{3,0,2,1:T(8,128)(2,1)S(1)}, bf16[32,1,3,640]{3,0,2,1:T(8,128)(2,1)}, u32[]{:S(2)}) copy-start(bf16[32,1,3,640]{3,0,2,1:T(8,128)(2,1)} %param.7) | copy-start | bytes 368644
  9.5 28.1 %all-to-all-start = ((bf16[32,64,128]{2,1,0:T(8,128)(2,1)}), bf16[32,64,128]{2,1,0:T(8,128)(2,1)}, u32[]{:S(2)}, u32[]{:S(2)}) async-start(bf16[32,64,128]{2,1,0:T(8,128)(2,1)} %select_waves.1), calls=%async_computation | async-start | bytes 1048576 | tf_op jit(solution)/shard_map/all_to_all | solution.py:247
  22.7 1.8 %collective-permute-start.3 = (f32[24,32,128]{2,1,0:T(8,128)S(1)}, f32[24,32,128]{2,1,0:T(8,128)S(1)}, u32[]{:S(2)}, u32[]{:S(2)}) collective-permute-start(f32[24,32,128]{2,1,0:T(8,128)S(1)} %pad_maximum_fusion.refs_0_), channel_id=1, source_target_pairs={{0,1},{1,0},{2,3},{3,2},{4,5},{5,4},{6,7},{7,6},{8,9},{9,8},{10,11... | collective-permute-start | bytes 1179656 | tf_op jit(solution)/shard_map/ppermute | solution.py:256
  24.5 0.7 %copy-start.2 = (f32[24,32,128]{2,1,0:T(8,128)}, f32[24,32,128]{2,1,0:T(8,128)S(1)}, u32[]{:S(2)}) copy-start(f32[24,32,128]{2,1,0:T(8,128)S(1)} %collective-permute-done.3.refs_1_) | copy-start | bytes 1179652
  25.2 1.0 %copy-start.3 = (f32[24,32,128]{2,1,0:T(8,128)S(1)}, f32[24,32,128]{2,1,0:T(8,128)}, u32[]{:S(2)}) copy-start(f32[24,32,128]{2,1,0:T(8,128)} %copy-done.2) | copy-start | bytes 1179652
  31.9 0.9 %copy-start = (f32[48,32,128]{2,1,0:T(8,128)}, f32[48,32,128]{2,1,0:T(8,128)S(1)}, u32[]{:S(2)}) copy-start(f32[48,32,128]{2,1,0:T(8,128)S(1)} %get-tuple-element.10.scales) | copy-start | bytes 2359300
  37.6 1.1 %copy-start.1 = (f32[48,32,128]{2,1,0:T(8,128)S(1)}, f32[48,32,128]{2,1,0:T(8,128)}, u32[]{:S(2)}) copy-start(f32[48,32,128]{2,1,0:T(8,128)} %copy-done) | copy-start | bytes 2359300

commit v5 on v4

v5 whole, which is shorter than its diff:
```python
import jax
import jax.numpy as jnp
from jax import lax
from jax.experimental import pallas as pl
from jax.experimental.pallas import tpu as pltpu
from jax.sharding import PartitionSpec as P

NT = 1536
L = 640
LAGS = 1024
SAMPLES = 3200
CAP = 4
STEP = 32
LANES = 128
BLOCKS = SAMPLES // STEP
OUT_BLOCKS = NT // STEP
TILES = L // LANES
TURNS = 8
UNROLL = 8
SLOT_ROWS = 64
RECORDS = 6
STATION_BITS = 4
EPSILON = 1e-05
VALID = 1 << 20


def exclusive_prefix(values):
    lanes = values.shape[-1]
    groups = values.reshape(-1, 8, lanes)
    row = lax.broadcasted_iota(jnp.int32, groups.shape, 1)
    total = groups
    for shift in (1, 2, 4):
        total = total + jnp.where(row >= shift, pltpu.roll(total, shift, 1), 0.0)
    inner = jnp.where(row >= 1, pltpu.roll(total, 1, 1), 0.0).reshape(-1, STEP // 8, 8, lanes)
    last = total.reshape(-1, STEP // 8, 8, lanes)[:, :, 7:8]
    pieces = [inner[:, 0:1]]
    carry = last[:, 0:1]
    for group in range(1, STEP // 8):
        pieces.append(inner[:, group:group + 1] + carry)
        carry = carry + last[:, group:group + 1]
    return jnp.concatenate(pieces, axis=1).reshape(values.shape)


def window_sums(values):
    width = values.shape[-1]
    span = L // STEP
    ahead = pltpu.roll(values, width - span, 1) - values
    two = jnp.sum(values.reshape(-1, STEP, width), axis=1)
    two = two + pltpu.roll(two, width - 1, 1)
    four = two + pltpu.roll(two, width - 2, 1)
    eight = four + pltpu.roll(four, width - 4, 1)
    sixteen = eight + pltpu.roll(eight, width - 8, 1)
    whole = sixteen + pltpu.roll(four, width - 16, 1)
    inner = exclusive_prefix(ahead).reshape(-1, STEP, width)
    return whole[:, None, :] + inner


def scales_kernel(index_ref, mask_hbm, tiles_ref, out_ref, mask_ref, sem):
    copy = pltpu.make_async_copy(mask_hbm, mask_ref, sem)
    copy.start()
    size = tiles_ref.shape[0]
    here = index_ref[1]
    values = tiles_ref[...].reshape(size * STEP, LANES)
    mean_one = window_sums(values) * (1.0 / L)
    mean_two = window_sums(values * values) * (1.0 / L)
    factor = lax.rsqrt(mean_two - mean_one * mean_one + EPSILON)
    out_ref[0:size] = tiles_ref[...]
    copy.wait()
    for record in range(size):
        weight = mask_ref[record >> 1, here * 2 + (record & 1)].astype(jnp.float32) * (1.0 / L)
        out_ref[size + record] = factor[record] * weight


def select_kernel(index_ref, station_hbm, lag_hbm, waves_hbm, out_ref, meta_ref,
                  station_ref, lag_ref, waves_ref, staged, sems):
    copies = [
        pltpu.make_async_copy(station_hbm, station_ref, sems.at[0]),
        pltpu.make_async_copy(lag_hbm, lag_ref, sems.at[1]),
        pltpu.make_async_copy(waves_hbm, waves_ref, sems.at[2]),
    ]
    for copy in copies:
        copy.start()
    peers = out_ref.shape[0]
    group_size = station_ref.shape[0]
    square = (group_size, group_size)
    row = lax.broadcasted_iota(jnp.int32, square, 0)
    column = lax.broadcasted_iota(jnp.int32, square, 1)
    for at in range(3 * TILES * CAP, SLOT_ROWS):
        staged[pl.ds(at, peers, stride=SLOT_ROWS), :] = jnp.zeros((peers, LANES), jnp.float32)
    copies[0].wait()
    stations = station_ref[...]
    owners = stations >> STATION_BITS
    down = jnp.sum(jnp.where(column == index_ref[0], owners, 0), axis=1, keepdims=True)
    down = jnp.broadcast_to(down, square)
    across = jnp.sum(jnp.where(row == column, down, 0), axis=0, keepdims=True)
    same = (down == across) & (row < column)
    place = jnp.sum(same.astype(jnp.int32), axis=0, keepdims=True)
    slot = across * CAP + place
    peer = lax.broadcasted_iota(jnp.int32, (peers, group_size), 0)
    selects = [(peer * CAP + k == slot).astype(jnp.float32).astype(jnp.bfloat16) for k in range(CAP)]
    select = jnp.concatenate(selects, axis=0)

    copies[1].wait()
    landing = owners == index_ref[0]
    earlier = (column < row).astype(jnp.float32).astype(jnp.bfloat16)
    arrival = jnp.dot(earlier, landing.astype(jnp.float32).astype(jnp.bfloat16), preferred_element_type=jnp.float32)
    packed = VALID + (lag_ref[...] << 9) + ((stations & (2**STATION_BITS - 1)) << 5) + row
    for k in range(CAP):
        held = landing & (arrival.astype(jnp.int32) == k)
        meta_ref[k:k + 1, :] = jnp.sum(jnp.where(held, packed, 0), axis=0, keepdims=True)

    copies[2].wait()
    for c in range(3):
        values = waves_ref[c].astype(jnp.float32)
        centred = values - jnp.mean(values, axis=-1, keepdims=True)
        power = jnp.mean(centred * centred, axis=-1, keepdims=True)
        unit = (centred / jnp.sqrt(power + EPSILON)).astype(jnp.bfloat16)
        picked = jnp.dot(select, unit, preferred_element_type=jnp.float32)
        for tile in range(TILES):
            columns = slice(tile * LANES, (tile + 1) * LANES)
            for k in range(CAP):
                at = (c * TILES + tile) * CAP + k
                staged[pl.ds(at, peers, stride=SLOT_ROWS), :] = picked[k * peers:(k + 1) * peers, columns]
    out_ref[...] = staged[...].astype(jnp.bfloat16).reshape(out_ref.shape)


def owner_of(here, core, hop, hops):
    return ((here - 2 * hop) & (2 * hops - 1)) ^ core


def stack_kernel(meta_ref, index_ref, near_ref, far_ref, waves_hbm, out_ref,
                 waves_ref, tiles, scales, frames, units, acc, twice, dense, slots, sems):
    here = index_ref[1]
    hops = near_ref.shape[0] // (2 * RECORDS)
    waves_copy = pltpu.make_async_copy(waves_hbm, waves_ref, sems.at[2])
    row_copies = [pltpu.make_async_copy(row_ref, tiles.at[core], sems.at[core])
                  for core, row_ref in enumerate((near_ref, far_ref))]
    for copy in row_copies + [waves_copy]:
        copy.start()

    def list_slot(slot, count):
        slots[count] = slot
        held = meta_ref[slot & (CAP - 1), slot >> 2] >> 20
        return count + held

    count = lax.fori_loop(0, meta_ref.shape[1] * CAP, list_slot, jnp.int32(0), unroll=16)
    for spare in range(UNROLL):
        slots[count + spare] = -1
    acc[...] = jnp.zeros_like(acc)

    for core, copy in enumerate(row_copies):
        copy.wait()
        for hop in range(hops):
            first = owner_of(here, core, hop, hops) * RECORDS
            at = 2 * RECORDS * hop
            values = tiles[core, at:at + RECORDS].reshape(RECORDS * STEP, LANES).astype(jnp.bfloat16)
            for turn in range(TURNS):
                rolled = values if turn == 0 else pltpu.roll(values, LANES - turn, 1)
                frames[pl.ds(first, RECORDS), turn * STEP:(turn + 1) * STEP, :] = (
                    rolled.reshape(RECORDS, STEP, LANES)
                )
            scales[pl.ds(first, RECORDS)] = tiles[core, at + RECORDS:at + 2 * RECORDS]
    waves_copy.wait()
    units[...] = waves_ref[...].reshape(units.shape).astype(jnp.float32)
    row = lax.broadcasted_iota(jnp.int32, (STEP, LANES), 0)
    lane = lax.broadcasted_iota(jnp.int32, (STEP, LANES), 1)
    own = lane >= row

    def one_pick(slot, spare):
        held = slot >= 0
        slot = jnp.maximum(slot, 0)
        packed = meta_ref[slot & (CAP - 1), slot >> 2]
        template = jnp.where(held, packed & 31, acc.shape[0] // STEP - 1)
        station = (packed >> 5) & 15
        lag = (packed >> 9) & 2047
        total = jnp.zeros((STEP, LANES), jnp.float32)
        for c in range(3):
            record = (station >> 1) * RECORDS + 2 * c + (station & 1)
            before = jnp.zeros((STEP, LANES), jnp.float32)
            columns = []
            for tile in range(TILES):
                at = (slot >> 2) * SLOT_ROWS + (c * TILES + tile) * CAP + (slot & (CAP - 1))
                wave = units[pl.ds(at, STEP, stride=0), :]
                spread = pltpu.roll(wave, 0, 1, stride=1, stride_axis=0)
                columns.append(jnp.where(own, spread, before).astype(jnp.bfloat16))
                before = spread
            columns.append(jnp.where(own, 0.0, before).astype(jnp.bfloat16))
            left = jnp.concatenate(
                [jnp.concatenate(columns[i:i + 2], axis=1) for i in range(0, TILES + 1, 2)], axis=0
            )
            product = jnp.dot(left, frames[record], preferred_element_type=jnp.float32)
            summed = product[:STEP]
            for part in range(1, (TILES + 1) // 2):
                later = product[part * STEP:(part + 1) * STEP]
                summed = summed + pltpu.roll(later, LANES - TURNS * part, 1)
            total = total + summed * scales[record]
        first = pltpu.roll(total, LANES - (lag >> 5), 1)
        twice[spare, 0:STEP, :] = first
        twice[spare, STEP:2 * STEP, :] = pltpu.roll(first, LANES - 1, 1)
        shifted = twice[spare, pl.ds(lag & (STEP - 1), STEP), :]
        return pl.ds(pl.multiple_of(template * STEP, STEP), STEP), shifted

    @pl.loop(0, (count + UNROLL - 1) // UNROLL)
    def _(index):
        done = [one_pick(slots[index * UNROLL + spare], spare) for spare in range(UNROLL)]
        for rows, shifted in done:
            acc[rows, :] += shifted

    for group in range(STEP // 4):
        parts = [acc[pl.ds(4 * group + j, STEP, stride=STEP), :] for j in range(4)]
        turned = jnp.concatenate(parts, axis=0).T
        dense[pl.ds(group, OUT_BLOCKS, stride=8), :] = turned[:OUT_BLOCKS]
    for part in range(out_ref.shape[1] // LANES):
        rows = dense[pl.ds(part, out_ref.shape[0], stride=3), :]
        out_ref[:, part * LANES:(part + 1) * LANES] = rows.astype(out_ref.dtype)


SMEM = pl.BlockSpec(memory_space=pltpu.SMEM)
VMEM = pl.BlockSpec(memory_space=pltpu.VMEM)
ANY = pl.BlockSpec(memory_space=pl.ANY)
HBM = pl.BlockSpec(memory_space=pltpu.HBM)


def with_scales(index, channel_mask, tiles):
    return pl.pallas_call(
        scales_kernel,
        out_shape=jax.ShapeDtypeStruct((2 * tiles.shape[0], STEP, LANES), jnp.float32),
        in_specs=[SMEM, HBM, VMEM],
        out_specs=VMEM,
        scratch_shapes=[pltpu.SMEM(channel_mask.shape, jnp.int32), pltpu.SemaphoreType.DMA],
        compiler_params=pltpu.CompilerParams(vmem_limit_bytes=4 * 1024 * 1024),
        cost_estimate=pl.CostEstimate(flops=2_000_000, transcendentals=25_000, bytes_accessed=300_000),
        name="record_scales",
    )(index, channel_mask, tiles)


def slot_waves(index, pick_station, pick_lag, template_waves, peers):
    group_size = pick_station.shape[0]
    return pl.pallas_call(
        select_kernel,
        out_shape=(
            jax.ShapeDtypeStruct((peers, SLOT_ROWS, LANES), jnp.bfloat16),
            jax.ShapeDtypeStruct((CAP, peers), jnp.int32),
        ),
        in_specs=[SMEM, HBM, HBM, HBM],
        out_specs=(VMEM, VMEM),
        scratch_shapes=[
            pltpu.VMEM((group_size, peers), jnp.int32),
            pltpu.VMEM((group_size, peers), jnp.int32),
            pltpu.VMEM(template_waves.shape, jnp.bfloat16),
            pltpu.VMEM((peers * SLOT_ROWS, LANES), jnp.float32),
            pltpu.SemaphoreType.DMA((3,)),
        ],
        compiler_params=pltpu.CompilerParams(vmem_limit_bytes=6 * 1024 * 1024),
        cost_estimate=pl.CostEstimate(flops=16_000_000, transcendentals=100, bytes_accessed=620_000),
        name="select_waves",
    )(index, pick_station, pick_lag, template_waves)


def partial_stack(meta, index, rows, received):
    group_size = meta.shape[1]
    peers = received.shape[0]
    slot_count = peers * CAP
    lines = NT * group_size // LANES
    records = rows[0].shape[0]
    return pl.pallas_call(
        stack_kernel,
        out_shape=jax.ShapeDtypeStruct((slot_count, lines * LANES // slot_count), jnp.bfloat16),
        in_specs=[SMEM, SMEM, ANY, ANY, ANY],
        out_specs=VMEM,
        scratch_shapes=[
            pltpu.VMEM(received.shape, jnp.bfloat16),
            pltpu.VMEM((2, records, STEP, LANES), jnp.float32),
            pltpu.VMEM((records, STEP, LANES), jnp.float32),
            pltpu.VMEM((records, TURNS * STEP, LANES), jnp.bfloat16),
            pltpu.VMEM((peers * SLOT_ROWS, LANES), jnp.float32),
            pltpu.VMEM(((group_size + 1) * STEP, LANES), jnp.float32),
            pltpu.VMEM((UNROLL, 2 * STEP, LANES), jnp.float32),
            pltpu.VMEM((lines, LANES), jnp.float32),
            pltpu.SMEM((slot_count + UNROLL,), jnp.int32),
            pltpu.SemaphoreType.DMA((3,)),
        ],
        compiler_params=pltpu.CompilerParams(vmem_limit_bytes=16 * 1024 * 1024),
        cost_estimate=pl.CostEstimate(flops=200_000_000, transcendentals=0, bytes_accessed=8_000_000),
        name="stack_picks",
    )(meta, index, *rows, received)


def body(station_data, channel_mask, template_waves, pick_station, pick_lag):
    sta_size = lax.axis_size("sta")
    tpl_size = lax.axis_size("tpl")
    group_size = pick_station.shape[0]
    stations_here = station_data.shape[1]
    index = jnp.stack([lax.axis_index("sta"), lax.axis_index("tpl")]).astype(jnp.int32)

    tiles = station_data.reshape(3, stations_here, BLOCKS, STEP).transpose(0, 1, 3, 2)
    tiles = jnp.pad(tiles, ((0, 0), (0, 0), (0, 0), (0, LANES - BLOCKS)))
    own = with_scales(index, channel_mask, tiles.reshape(3 * stations_here, STEP, LANES))
    row = [own]
    for hop in range(2, tpl_size, 2):
        row.append(lax.ppermute(own, "tpl", [(i, (i + hop) % tpl_size) for i in range(tpl_size)]))
    row = jnp.concatenate(row, axis=0)
    rows = [row, lax.ppermute(row, "tpl", [(i, i ^ 1) for i in range(tpl_size)])]

    waves = template_waves.reshape(group_size, 3, L).transpose(1, 0, 2)
    outgoing, meta = slot_waves(index, pick_station, pick_lag, waves, sta_size)
    received = lax.all_to_all(outgoing, "sta", split_axis=0, concat_axis=0, tiled=True)

    partial_sums = partial_stack(meta, index, rows, received)
    arrived = lax.all_to_all(partial_sums, "sta", split_axis=0, concat_axis=0, tiled=True)
    arrived = arrived.reshape(sta_size, CAP, -1).astype(jnp.float32)
    return jnp.sum(arrived, axis=0).reshape(NT // sta_size, group_size)


def solution(mesh):
    in_specs = (
        P(None, ("sta", "tpl"), None),
        P(None, "sta"),
        P("tpl", "sta", None, None),
        P("tpl", None),
        P("tpl", None),
    )
    return jax.shard_map(body, mesh=mesh, in_specs=in_specs, out_specs=P("sta", "tpl"), check_vma=False)
```

time: 60.5 us -> 61 us (level); the launches traced: 59.5 us -> 60.7 us
  waiting for transfers between devices: 6.4 us -> 16.3 us
  local copies, waits for them, and re-layouts: 7.37 us -> 2.65 us
  Pallas kernels: 12.2 us -> 9.86 us
  other arithmetic: 1.61 us -> 0.21 us
    all_to_all x1, waiting for transfers between devices: 4.87 us -> 14.1 us  [body(): lax.all_to_all(outgoing, 'sta', split_axis=0, concat_axis=0, tiled=True)]
    unnamed x15 -> x9, local copies, waits for them, and re-layouts: 5.49 us -> 0.8 us
    pallas_call x2, Pallas kernels: 7.47 us -> 4.05 us  [the longest x1 2.93 us: slot_waves(): pl.pallas_call(select_kernel, out_shape=(jax.ShapeDtypeStruct((peers, SLO...]
    pallas_call x1, Pallas kernels: 4.78 us -> 5.81 us  [partial_stack(): pl.pallas_call(stack_kernel, out_shape=jax.ShapeDtypeStruct((slot_count,...]
    add x2 -> x0, other arithmetic: 0.75 us -> none  [the longest x1 0.75 us: body(): VALID + (pick_lag << 9) + (pick_station - my_index * station_count << 5)]
    ppermute x1, waiting for transfers between devices: 1.53 us -> 2.27 us  [body(): lax.ppermute(row, 'tpl', [(i, i ^ 1) for i in range(tpl_size)])]
    eq x1 -> x0, other arithmetic: 0.73 us -> none  [body(): landing = owners == my_index]
  transfers between devices with their start and end apart: 5 -> 5, of which waited for: 2 -> 2; matrix products, arithmetic and copies ran while one was open for 3% -> 0% of each run, Pallas kernels for 13% -> 5%
where the time goes in v5:
time: 61 us; the launch traced here: 60.7 us
  starting transfers between devices  16.4 us (27%)
  waiting for transfers between devices  16.3 us (27%)
  blocking collectives  15.1 us (25%)
  Pallas kernels  9.86 us (16%)
  local copies, waits for them, and re-layouts  2.65 us (4%)
    all_to_all x1, blocking collectives, body(): lax.all_to_all(partial_sums, 'sta', split_axis=0, concat_axis=0, tiled=True)  15.1 us
    all_to_all x1, waiting for transfers between devices, body(): lax.all_to_all(outgoing, 'sta', split_axis=0, concat_axis=0, tiled=True)  14.1 us
    all_to_all x1, starting transfers between devices, body(): lax.all_to_all(outgoing, 'sta', split_axis=0, concat_axis=0, tiled=True)  11.5 us
    pallas_call x1, Pallas kernels, partial_stack(): pl.pallas_call(stack_kernel, out_shape=jax.ShapeDtypeStruct((slot_count,...  5.81 us
    ppermute x3, starting transfers between devices, body(): lax.ppermute(own, 'tpl', [(i, (i + hop) % tpl_size) for i in range(tpl_si...  4.83 us
    pallas_call x1, Pallas kernels, slot_waves(): pl.pallas_call(select_kernel, out_shape=(jax.ShapeDtypeStruct((peers, SLO...  2.93 us
    ppermute x1, waiting for transfers between devices, body(): lax.ppermute(row, 'tpl', [(i, i ^ 1) for i in range(tpl_size)])  2.27 us
  transfers between devices with their start and end apart: 5, of which 2 were waited for; matrix products, arithmetic and copies ran while one was open for 0% of the time, Pallas kernels for 5%

profile of v5, /device:TPU:2, one launch (start us, length us, event | category | flops | bytes accessed | tf_op | source)
XLA Modules:
  0.0 60.7 jit_solution(17597159699293699822)
XLA Ops:
  0.0 1.0 %reshape.17 = f32[3,2,100,32]{3,2,1,0:T(8,128)S(1)} reshape(f32[3,2,3200]{2,1,0:T(2,128)} %param.5) | data formatting | bytes 153600 | tf_op jit(solution)/shard_map/reshape | solution.py:296
  1.1 0.1 copy.9
  1.2 0.1 pad_add_fusion.index_ref
  1.3 0.7 %copy-done.3 = s32[3,16]{1,0:T(4,128)S(1)} copy-done((s32[3,16]{1,0:T(4,128)S(1)}, s32[3,16]{1,0:T(4,128)}, u32[]{:S(2)}) %copy-start.3) | copy-done | bytes 216
  2.0 1.1 %record_scales.1 = f32[12,32,128]{2,1,0:T(8,128)S(1)} custom-call(s32[2]{0:T(128)S(1)} %pad_add_fusion.index_ref, s32[3,16]{1,0:T(4,128)S(1)} %copy-done.3, f32[6,32,128]{2,1,0:T(8,128)S(1)} %bitcast.7), custom_call_target="tpu_custom_call" | custom-call | flops 2000000 | bytes 300000 | tf_op jit(solution)/shard_map/record_scales/pallas_call | solution.py:225
  3.1 2.3 %collective-permute-start.2 = (f32[12,32,128]{2,1,0:T(8,128)S(1)}, f32[12,32,128]{2,1,0:T(8,128)S(1)}, u32[]{:S(2)}, u32[]{:S(2)}) collective-permute-start(f32[12,32,128]{2,1,0:T(8,128)S(1)} %record_scales.1), channel_id=1, source_target_pairs={{0,6},{1,7},{2,0},{3,1},{4,2},{5,3},{6,4},{7,5},{8,14},{9,15},{10,... | collective-permute-start | bytes 589832 | tf_op jit(solution)/shard_map/ppermute | solution.py:301
  5.4 0.7 %collective-permute-start.1 = (f32[12,32,128]{2,1,0:T(8,128)S(1)}, f32[12,32,128]{2,1,0:T(8,128)S(1)}, u32[]{:S(2)}, u32[]{:S(2)}) collective-permute-start(f32[12,32,128]{2,1,0:T(8,128)S(1)} %record_scales.1), channel_id=1, source_target_pairs={{0,4},{1,5},{2,6},{3,7},{4,0},{5,1},{6,2},{7,3},{8,12},{9,13},{10,... | collective-permute-start | bytes 589832 | tf_op jit(solution)/shard_map/ppermute | solution.py:301
  6.1 1.8 %collective-permute-start = (f32[12,32,128]{2,1,0:T(8,128)S(1)}, f32[12,32,128]{2,1,0:T(8,128)S(1)}, u32[]{:S(2)}, u32[]{:S(2)}) collective-permute-start(f32[12,32,128]{2,1,0:T(8,128)S(1)} %record_scales.1), channel_id=1, source_target_pairs={{0,2},{1,3},{2,4},{3,5},{4,6},{5,7},{6,0},{7,1},{8,10},{9,11},{10,... | collective-permute-start | bytes 589832 | tf_op jit(solution)/shard_map/ppermute | solution.py:301
  7.9 0.0 copy-done
  7.9 0.0 copy-done.1
  7.9 2.9 %select_waves.1 = (bf16[32,64,128]{2,1,0:T(8,128)(2,1)}, s32[4,32]{1,0:T(4,128)S(1)}) custom-call(s32[2]{0:T(128)S(1)} %pad_add_fusion.index_ref, s32[32,32]{1,0:T(8,128)S(1)} %copy-done.1, s32[32,32]{1,0:T(8,128)S(1)} %copy-done.2, bf16[3,32,640]{2,1,0:T(8,128)(2,1)S(1)} %bitcast.8), custom_call_target="tpu_custom_call" | custom-call | flops 16000000 | bytes 620000 | tf_op jit(solution)/shard_map/select_waves/pallas_call | solution.py:239
  10.9 11.5 %all-to-all-start = ((bf16[32,64,128]{2,1,0:T(8,128)(2,1)}), bf16[32,64,128]{2,1,0:T(8,128)(2,1)S(1)}, u32[]{:S(2)}, u32[]{:S(2)}) async-start(bf16[32,64,128]{2,1,0:T(8,128)(2,1)} %get-tuple-element.8), calls=%async_computation | async-start | bytes 1048576 | tf_op jit(solution)/shard_map/all_to_all | solution.py:307
  22.4 0.0 collective-permute-done.2
  22.4 0.0 collective-permute-done.1
  22.4 0.0 collective-permute-done
  22.4 0.1 pad_maximum_fusion.near_ref
  22.5 0.1 collective-permute-start.3
  22.6 2.3 %collective-permute-done.3.far_ref = f32[48,32,128]{2,1,0:T(8,128)S(1)} collective-permute-done((f32[48,32,128]{2,1,0:T(8,128)S(1)}, f32[48,32,128]{2,1,0:T(8,128)S(1)}, u32[]{:S(2)}, u32[]{:S(2)}) %collective-permute-start.3) | collective-permute-done | bytes 786464 | tf_op jit(solution)/shard_map/ppermute | solution.py:303
  24.8 14.1 %all-to-all-done.waves_hbm = bf16[32,64,128]{2,1,0:T(8,128)(2,1)S(1)} async-done(((bf16[32,64,128]{2,1,0:T(8,128)(2,1)}), bf16[32,64,128]{2,1,0:T(8,128)(2,1)S(1)}, u32[]{:S(2)}, u32[]{:S(2)}) %all-to-all-start) | async-done | bytes 524320 | tf_op jit(solution)/shard_map/all_to_all | solution.py:307
  38.9 5.8 %stack_picks.1 = bf16[128,384]{1,0:T(8,128)(2,1)S(1)} custom-call(s32[4,32]{1,0:T(4,128)S(1)} %get-tuple-element.7.meta_ref, s32[2]{0:T(128)S(1)} %pad_add_fusion.index_ref, f32[48,32,128]{2,1,0:T(8,128)S(1)} %pad_maximum_fusion.near_ref, f32[48,32,128]{2,1,0:T(8,128)S(1)} %collective-permute-done.3.far_ref, bf16[32,64,128]{2,1,0:T(8,128)(2,1)S(1)} %all-to-all-done.waves_hbm), custom_call_target="tpu_custom_call" | custom-call | flops 200000000 | bytes 8000000 | tf_op jit(solution)/shard_map/stack_picks/pallas_call | solution.py:266
  44.7 15.1 %all_to_all.14 = bf16[32,4,384]{2,1,0:T(4,128)(2,1)S(1)} all-to-all(bf16[32,4,384]{2,1,0:T(4,128)(2,1)S(1)} %all_to_all.10), channel_id=1, replica_groups=mesh['sta'=32,'tpl'=8] {'sta'}, dimensions={0} | all-to-all | bytes 196608 | tf_op jit(solution)/shard_map/all_to_all | solution.py:310
  59.9 0.1 convert_reduce_fusion
  60.0 0.1 reshape.19
  60.0 0.7 %copy.8 = f32[48,32]{0,1:T(8,128)} copy(f32[48,32]{1,0:T(8,128)S(1)} %reshape.19) | data formatting | bytes 12288 | tf_op jit(solution)/shard_map/reshape | solution.py:312
  (7 shorter events, 0.1 us)
Async XLA Ops:
  1.3 0.7 %copy-start.3 = (s32[3,16]{1,0:T(4,128)S(1)}, s32[3,16]{1,0:T(4,128)}, u32[]{:S(2)}) copy-start(s32[3,16]{1,0:T(4,128)} %mask_hbm.1) | copy-start | bytes 580
  2.0 6.0 %copy-start = (bf16[32,1,3,640]{3,0,2,1:T(8,128)(2,1)S(1)}, bf16[32,1,3,640]{3,0,2,1:T(8,128)(2,1)}, u32[]{:S(2)}) copy-start(bf16[32,1,3,640]{3,0,2,1:T(8,128)(2,1)} %param.7) | copy-start | bytes 368644
  2.0 6.0 %copy-start.1 = (s32[32,32]{1,0:T(8,128)S(1)}, s32[32,32]{1,0:T(8,128)}, u32[]{:S(2)}) copy-start(s32[32,32]{1,0:T(8,128)} %station_hbm.1) | copy-start | bytes 12292
  2.0 6.0 %copy-start.2 = (s32[32,32]{1,0:T(8,128)S(1)}, s32[32,32]{1,0:T(8,128)}, u32[]{:S(2)}) copy-start(s32[32,32]{1,0:T(8,128)} %lag_hbm.1) | copy-start | bytes 12292
  3.1 19.3 %collective-permute-start.2 = (f32[12,32,128]{2,1,0:T(8,128)S(1)}, f32[12,32,128]{2,1,0:T(8,128)S(1)}, u32[]{:S(2)}, u32[]{:S(2)}) collective-permute-start(f32[12,32,128]{2,1,0:T(8,128)S(1)} %record_scales.1), channel_id=1, source_target_pairs={{0,6},{1,7},{2,0},{3,1},{4,2},{5,3},{6,4},{7,5},{8,14},{9,15},{10,... | collective-permute-start | bytes 589832 | tf_op jit(solution)/shard_map/ppermute | solution.py:301
  5.4 16.9 %collective-permute-start.1 = (f32[12,32,128]{2,1,0:T(8,128)S(1)}, f32[12,32,128]{2,1,0:T(8,128)S(1)}, u32[]{:S(2)}, u32[]{:S(2)}) collective-permute-start(f32[12,32,128]{2,1,0:T(8,128)S(1)} %record_scales.1), channel_id=1, source_target_pairs={{0,4},{1,5},{2,6},{3,7},{4,0},{5,1},{6,2},{7,3},{8,12},{9,13},{10,... | collective-permute-start | bytes 589832 | tf_op jit(solution)/shard_map/ppermute | solution.py:301
  6.1 16.3 %collective-permute-start = (f32[12,32,128]{2,1,0:T(8,128)S(1)}, f32[12,32,128]{2,1,0:T(8,128)S(1)}, u32[]{:S(2)}, u32[]{:S(2)}) collective-permute-start(f32[12,32,128]{2,1,0:T(8,128)S(1)} %record_scales.1), channel_id=1, source_target_pairs={{0,2},{1,3},{2,4},{3,5},{4,6},{5,7},{6,0},{7,1},{8,10},{9,11},{10,... | collective-permute-start | bytes 589832 | tf_op jit(solution)/shard_map/ppermute | solution.py:301
  10.9 28.0 %all-to-all-start = ((bf16[32,64,128]{2,1,0:T(8,128)(2,1)}), bf16[32,64,128]{2,1,0:T(8,128)(2,1)S(1)}, u32[]{:S(2)}, u32[]{:S(2)}) async-start(bf16[32,64,128]{2,1,0:T(8,128)(2,1)} %get-tuple-element.8), calls=%async_computation | async-start | bytes 1048576 | tf_op jit(solution)/shard_map/all_to_all | solution.py:307
  22.5 2.4 %collective-permute-start.3 = (f32[48,32,128]{2,1,0:T(8,128)S(1)}, f32[48,32,128]{2,1,0:T(8,128)S(1)}, u32[]{:S(2)}, u32[]{:S(2)}) collective-permute-start(f32[48,32,128]{2,1,0:T(8,128)S(1)} %pad_maximum_fusion.near_ref), channel_id=1, source_target_pairs={{0,1},{1,0},{2,3},{3,2},{4,5},{5,4},{6,7},{7,6},{8,9},{9,8},{10,11... | collective-permute-start | bytes 2359304 | tf_op jit(solution)/shard_map/ppermute | solution.py:303

commit v6 on v5

--- a/solution.py
+++ b/solution.py
@@ -128,13 +128,13 @@
     return ((here - 2 * hop) & (2 * hops - 1)) ^ core
 
 
-def stack_kernel(meta_ref, index_ref, near_ref, far_ref, waves_hbm, out_ref,
-                 waves_ref, tiles, scales, frames, units, acc, twice, dense, slots, sems):
+def stack_kernel(meta_ref, index_ref, *refs):
+    *row_refs, waves_hbm, out_ref = refs[:-10]
+    waves_ref, tiles, scales, frames, units, acc, twice, dense, slots, sems = refs[-10:]
     here = index_ref[1]
-    hops = near_ref.shape[0] // (2 * RECORDS)
-    waves_copy = pltpu.make_async_copy(waves_hbm, waves_ref, sems.at[2])
-    row_copies = [pltpu.make_async_copy(row_ref, tiles.at[core], sems.at[core])
-                  for core, row_ref in enumerate((near_ref, far_ref))]
+    hops = len(row_refs) // 2
+    waves_copy = pltpu.make_async_copy(waves_hbm, waves_ref, sems.at[len(row_refs)])
+    row_copies = [pltpu.make_async_copy(row_ref, tiles.at[at], sems.at[at]) for at, row_ref in enumerate(row_refs)]
     for copy in row_copies + [waves_copy]:
         copy.start()
 
@@ -148,18 +148,14 @@
         slots[count + spare] = -1
     acc[...] = jnp.zeros_like(acc)
 
-    for core, copy in enumerate(row_copies):
+    for at, copy in enumerate(row_copies):
         copy.wait()
-        for hop in range(hops):
-            first = owner_of(here, core, hop, hops) * RECORDS
-            at = 2 * RECORDS * hop
-            values = tiles[core, at:at + RECORDS].reshape(RECORDS * STEP, LANES).astype(jnp.bfloat16)
-            for turn in range(TURNS):
-                rolled = values if turn == 0 else pltpu.roll(values, LANES - turn, 1)
-                frames[pl.ds(first, RECORDS), turn * STEP:(turn + 1) * STEP, :] = (
-                    rolled.reshape(RECORDS, STEP, LANES)
-                )
-            scales[pl.ds(first, RECORDS)] = tiles[core, at + RECORDS:at + 2 * RECORDS]
+        first = owner_of(here, at // hops, at % hops, hops) * RECORDS
+        values = tiles[at, :RECORDS].reshape(RECORDS * STEP, LANES).astype(jnp.bfloat16)
+        for turn in range(TURNS):
+            rolled = values if turn == 0 else pltpu.roll(values, LANES - turn, 1)
+            frames[pl.ds(first, RECORDS), turn * STEP:(turn + 1) * STEP, :] = rolled.reshape(RECORDS, STEP, LANES)
+        scales[pl.ds(first, RECORDS)] = tiles[at, RECORDS:]
     waves_copy.wait()
     units[...] = waves_ref[...].reshape(units.shape).astype(jnp.float32)
     row = lax.broadcasted_iota(jnp.int32, (STEP, LANES), 0)
@@ -262,15 +258,15 @@
     peers = received.shape[0]
     slot_count = peers * CAP
     lines = NT * group_size // LANES
-    records = rows[0].shape[0]
+    records = len(rows) * RECORDS
     return pl.pallas_call(
         stack_kernel,
         out_shape=jax.ShapeDtypeStruct((slot_count, lines * LANES // slot_count), jnp.bfloat16),
-        in_specs=[SMEM, SMEM, ANY, ANY, ANY],
+        in_specs=[SMEM, SMEM] + [ANY] * (len(rows) + 1),
         out_specs=VMEM,
         scratch_shapes=[
             pltpu.VMEM(received.shape, jnp.bfloat16),
-            pltpu.VMEM((2, records, STEP, LANES), jnp.float32),
+            pltpu.VMEM((len(rows), 2 * RECORDS, STEP, LANES), jnp.float32),
             pltpu.VMEM((records, STEP, LANES), jnp.float32),
             pltpu.VMEM((records, TURNS * STEP, LANES), jnp.bfloat16),
             pltpu.VMEM((peers * SLOT_ROWS, LANES), jnp.float32),
@@ -278,7 +274,7 @@
             pltpu.VMEM((UNROLL, 2 * STEP, LANES), jnp.float32),
             pltpu.VMEM((lines, LANES), jnp.float32),
             pltpu.SMEM((slot_count + UNROLL,), jnp.int32),
-            pltpu.SemaphoreType.DMA((3,)),
+            pltpu.SemaphoreType.DMA((len(rows) + 1,)),
         ],
         compiler_params=pltpu.CompilerParams(vmem_limit_bytes=16 * 1024 * 1024),
         cost_estimate=pl.CostEstimate(flops=200_000_000, transcendentals=0, bytes_accessed=8_000_000),
@@ -293,18 +289,18 @@
     stations_here = station_data.shape[1]
     index = jnp.stack([lax.axis_index("sta"), lax.axis_index("tpl")]).astype(jnp.int32)
 
+    waves = template_waves.reshape(group_size, 3, L).transpose(1, 0, 2)
+    outgoing, meta = slot_waves(index, pick_station, pick_lag, waves, sta_size)
+    received = lax.all_to_all(outgoing, "sta", split_axis=0, concat_axis=0, tiled=True)
+
     tiles = station_data.reshape(3, stations_here, BLOCKS, STEP).transpose(0, 1, 3, 2)
     tiles = jnp.pad(tiles, ((0, 0), (0, 0), (0, 0), (0, LANES - BLOCKS)))
     own = with_scales(index, channel_mask, tiles.reshape(3 * stations_here, STEP, LANES))
-    row = [own]
+    swap = [(i, i ^ 1) for i in range(tpl_size)]
+    near = [own]
     for hop in range(2, tpl_size, 2):
-        row.append(lax.ppermute(own, "tpl", [(i, (i + hop) % tpl_size) for i in range(tpl_size)]))
-    row = jnp.concatenate(row, axis=0)
-    rows = [row, lax.ppermute(row, "tpl", [(i, i ^ 1) for i in range(tpl_size)])]
-
-    waves = template_waves.reshape(group_size, 3, L).transpose(1, 0, 2)
-    outgoing, meta = slot_waves(index, pick_station, pick_lag, waves, sta_size)
-    received = lax.all_to_all(outgoing, "sta", split_axis=0, concat_axis=0, tiled=True)
+        near.append(lax.ppermute(own, "tpl", [(i, (i + hop) % tpl_size) for i in range(tpl_size)]))
+    rows = near + [lax.ppermute(row, "tpl", swap) for row in near]
 
     partial_sums = partial_stack(meta, index, rows, received)
     arrived = lax.all_to_all(partial_sums, "sta", split_axis=0, concat_axis=0, tiled=True)

time: 61 us -> 63.8 us (1.046)
  the two profiles are of different devices: /device:TPU:2 before, /device:TPU:1 now
where the time goes in v6:
time: 63.8 us; the launch traced here: 63.4 us
  starting transfers between devices  24.7 us (39%)
  blocking collectives  18.1 us (28%)
  Pallas kernels  12.2 us (19%)
  waiting for transfers between devices  4.1 us (6%)
  local copies, waits for them, and re-layouts  4.04 us (6%)
    all_to_all x1, blocking collectives, body(): lax.all_to_all(partial_sums, 'sta', split_axis=0, concat_axis=0, tiled=True)  18.1 us
    all_to_all x1, starting transfers between devices, body(): lax.all_to_all(outgoing, 'sta', split_axis=0, concat_axis=0, tiled=True)  12.2 us
    ppermute x4, starting transfers between devices, body(): rows = near + [lax.ppermute(row, 'tpl', swap) for row in near]  8.87 us
    pallas_call x1, Pallas kernels, partial_stack(): pl.pallas_call(stack_kernel, out_shape=jax.ShapeDtypeStruct((slot_count,...  8.17 us
    ppermute x3, starting transfers between devices, body(): lax.ppermute(own, 'tpl', [(i, (i + hop) % tpl_size) for i in range(tpl_si...  3.68 us
    unnamed x11, local copies, waits for them, and re-layouts  3.05 us
    ppermute x3, waiting for transfers between devices, body(): lax.ppermute(own, 'tpl', [(i, (i + hop) % tpl_size) for i in range(tpl_si...  3.03 us
    pallas_call x1, Pallas kernels, slot_waves(): pl.pallas_call(select_kernel, out_shape=(jax.ShapeDtypeStruct((peers, SLO...  2.93 us
  transfers between devices with their start and end apart: 8, of which 3 were waited for; matrix products, arithmetic and copies ran while one was open for 0% of the time, Pallas kernels for 2%

profile of v6, /device:TPU:1, one launch (start us, length us, event | category | flops | bytes accessed | tf_op | source)
XLA Modules:
  0.0 63.4 jit_solution(11800823937793047603)
XLA Ops:
  0.0 0.1 pad_add_fusion.index_ref
  0.1 0.6 %copy-done.1 = s32[32,32]{1,0:T(8,128)S(1)} copy-done((s32[32,32]{1,0:T(8,128)S(1)}, s32[32,32]{1,0:T(8,128)}, u32[]{:S(2)}) %copy-start.1) | copy-done | bytes 4120
  0.7 0.9 %copy-done = bf16[32,1,3,640]{3,0,2,1:T(8,128)(2,1)S(1)} copy-done((bf16[32,1,3,640]{3,0,2,1:T(8,128)(2,1)S(1)}, bf16[32,1,3,640]{3,0,2,1:T(8,128)(2,1)}, u32[]{:S(2)}) %copy-start) | copy-done | bytes 122904
  1.6 0.7 %copy-done.2 = s32[32,32]{1,0:T(8,128)S(1)} copy-done((s32[32,32]{1,0:T(8,128)S(1)}, s32[32,32]{1,0:T(8,128)}, u32[]{:S(2)}) %copy-start.2) | copy-done | bytes 4120
  2.3 2.9 %select_waves.1 = (bf16[32,64,128]{2,1,0:T(8,128)(2,1)}, s32[4,32]{1,0:T(4,128)S(1)}) custom-call(s32[2]{0:T(128)S(1)} %pad_add_fusion.index_ref, s32[32,32]{1,0:T(8,128)S(1)} %copy-done.1, s32[32,32]{1,0:T(8,128)S(1)} %copy-done.2, bf16[3,32,640]{2,1,0:T(8,128)(2,1)S(1)} %bitcast.8), custom_call_target="tpu_custom_call" | custom-call | flops 16000000 | bytes 620000 | tf_op jit(solution)/shard_map/select_waves/pallas_call | solution.py:235
  5.3 12.2 %all-to-all-start = ((bf16[32,64,128]{2,1,0:T(8,128)(2,1)}), bf16[32,64,128]{2,1,0:T(8,128)(2,1)S(1)}, u32[]{:S(2)}, u32[]{:S(2)}) async-start(bf16[32,64,128]{2,1,0:T(8,128)(2,1)} %get-tuple-element.8), calls=%async_computation | async-start | bytes 1048576 | tf_op jit(solution)/shard_map/all_to_all | solution.py:294
  17.5 0.2 reshape.17
  17.7 0.1 copy.9
  17.8 0.7 %copy-done.3 = s32[3,16]{1,0:T(4,128)S(1)} copy-done((s32[3,16]{1,0:T(4,128)S(1)}, s32[3,16]{1,0:T(4,128)}, u32[]{:S(2)}) %copy-start.3) | copy-done | bytes 216
  18.5 1.1 %record_scales.1.refs_0_ = f32[12,32,128]{2,1,0:T(8,128)S(1)} custom-call(s32[2]{0:T(128)S(1)} %pad_add_fusion.index_ref, s32[3,16]{1,0:T(4,128)S(1)} %copy-done.3, f32[6,32,128]{2,1,0:T(8,128)S(1)} %bitcast.7), custom_call_target="tpu_custom_call" | custom-call | flops 2000000 | bytes 300000 | tf_op jit(solution)/shard_map/record_scales/pallas_call | solution.py:221
  19.6 2.6 %collective-permute-start.2 = (f32[12,32,128]{2,1,0:T(8,128)S(1)}, f32[12,32,128]{2,1,0:T(8,128)S(1)}, u32[]{:S(2)}, u32[]{:S(2)}) collective-permute-start(f32[12,32,128]{2,1,0:T(8,128)S(1)} %record_scales.1.refs_0_), channel_id=1, source_target_pairs={{0,6},{1,7},{2,0},{3,1},{4,2},{5,3},{6,4},{7,5},{8,14},{9,15},{10,... | collective-permute-start | bytes 589832 | tf_op jit(solution)/shard_map/ppermute | solution.py:302
  22.2 0.5 collective-permute-start.1
  22.7 0.6 collective-permute-start
  23.3 1.8 %collective-permute-start.3 = (f32[12,32,128]{2,1,0:T(8,128)S(1)}, f32[12,32,128]{2,1,0:T(8,128)S(1)}, u32[]{:S(2)}, u32[]{:S(2)}) collective-permute-start(f32[12,32,128]{2,1,0:T(8,128)S(1)} %record_scales.1.refs_0_), channel_id=1, source_target_pairs={{0,1},{1,0},{2,3},{3,2},{4,5},{5,4},{6,7},{7,6},{8,9},{9,8},{10,11... | collective-permute-start | bytes 589832 | tf_op jit(solution)/shard_map/ppermute | solution.py:303
  25.1 1.1 %collective-permute-done.2.refs_3_ = f32[12,32,128]{2,1,0:T(8,128)S(1)} collective-permute-done((f32[12,32,128]{2,1,0:T(8,128)S(1)}, f32[12,32,128]{2,1,0:T(8,128)S(1)}, u32[]{:S(2)}, u32[]{:S(2)}) %collective-permute-start.2) | collective-permute-done | bytes 196640 | tf_op jit(solution)/shard_map/ppermute | solution.py:302
  26.2 5.3 %collective-permute-start.6 = (f32[12,32,128]{2,1,0:T(8,128)S(1)}, f32[12,32,128]{2,1,0:T(8,128)S(1)}, u32[]{:S(2)}, u32[]{:S(2)}) collective-permute-start(f32[12,32,128]{2,1,0:T(8,128)S(1)} %collective-permute-done.2.refs_3_), channel_id=1, source_target_pairs={{0,1},{1,0},{2,3},{3,2},{4,5},{5,4},{6,7},{7,6},{8,9},{9,8},{10,11... | collective-permute-start | bytes 589832 | tf_op jit(solution)/shard_map/ppermute | solution.py:303
  31.5 1.3 %collective-permute-start.5 = (f32[12,32,128]{2,1,0:T(8,128)S(1)}, f32[12,32,128]{2,1,0:T(8,128)S(1)}, u32[]{:S(2)}, u32[]{:S(2)}) collective-permute-start(f32[12,32,128]{2,1,0:T(8,128)S(1)} %collective-permute-done.1.refs_2_), channel_id=1, source_target_pairs={{0,1},{1,0},{2,3},{3,2},{4,5},{5,4},{6,7},{7,6},{8,9},{9,8},{10,11... | collective-permute-start | bytes 589832 | tf_op jit(solution)/shard_map/ppermute | solution.py:303
  32.8 1.9 %collective-permute-done.refs_1_ = f32[12,32,128]{2,1,0:T(8,128)S(1)} collective-permute-done((f32[12,32,128]{2,1,0:T(8,128)S(1)}, f32[12,32,128]{2,1,0:T(8,128)S(1)}, u32[]{:S(2)}, u32[]{:S(2)}) %collective-permute-start) | collective-permute-done | bytes 196640 | tf_op jit(solution)/shard_map/ppermute | solution.py:302
  34.7 0.5 collective-permute-start.4
  35.2 1.1 %collective-permute-done.4.refs_5_ = f32[12,32,128]{2,1,0:T(8,128)S(1)} collective-permute-done((f32[12,32,128]{2,1,0:T(8,128)S(1)}, f32[12,32,128]{2,1,0:T(8,128)S(1)}, u32[]{:S(2)}, u32[]{:S(2)}) %collective-permute-start.4) | collective-permute-done | bytes 196640 | tf_op jit(solution)/shard_map/ppermute | solution.py:303
  36.3 8.2 %stack_picks.1 = bf16[128,384]{1,0:T(8,128)(2,1)S(1)} custom-call(s32[4,32]{1,0:T(4,128)S(1)} %get-tuple-element.7.meta_ref, s32[2]{0:T(128)S(1)} %pad_add_fusion.index_ref, f32[12,32,128]{2,1,0:T(8,128)S(1)} %record_scales.1.refs_0_, f32[12,32,128]{2,1,0:T(8,128)S(1)} %collective-permute-done.refs_1_, f32[12,32,128]{2,1,0:T(8,128)S(1)} %collective-permute-done.1.refs_2_, ...), custom_call_target="tpu_custom_call" | custom-call | flops 200000000 | bytes 8000000 | tf_op jit(solution)/shard_map/stack_picks/pallas_call | solution.py:262
  44.5 18.1 %all_to_all.14 = bf16[32,4,384]{2,1,0:T(4,128)(2,1)S(1)} all-to-all(bf16[32,4,384]{2,1,0:T(4,128)(2,1)S(1)} %all_to_all.10), channel_id=1, replica_groups=mesh['sta'=32,'tpl'=8] {'sta'}, dimensions={0} | all-to-all | bytes 196608 | tf_op jit(solution)/shard_map/all_to_all | solution.py:306
  62.6 0.1 reshape.19
  62.7 0.7 %copy.8 = f32[48,32]{0,1:T(8,128)} copy(f32[48,32]{1,0:T(8,128)S(1)} %reshape.19) | data formatting | bytes 12288 | tf_op jit(solution)/shard_map/reshape | solution.py:308
  (14 shorter events, 0.1 us)
Async XLA Ops:
  0.0 0.7 %copy-start.1 = (s32[32,32]{1,0:T(8,128)S(1)}, s32[32,32]{1,0:T(8,128)}, u32[]{:S(2)}) copy-start(s32[32,32]{1,0:T(8,128)} %station_hbm.1) | copy-start | bytes 12292
  0.7 0.9 %copy-start = (bf16[32,1,3,640]{3,0,2,1:T(8,128)(2,1)S(1)}, bf16[32,1,3,640]{3,0,2,1:T(8,128)(2,1)}, u32[]{:S(2)}) copy-start(bf16[32,1,3,640]{3,0,2,1:T(8,128)(2,1)} %param.7) | copy-start | bytes 368644
  1.6 0.7 %copy-start.2 = (s32[32,32]{1,0:T(8,128)S(1)}, s32[32,32]{1,0:T(8,128)}, u32[]{:S(2)}) copy-start(s32[32,32]{1,0:T(8,128)} %lag_hbm.1) | copy-start | bytes 12292
  5.3 12.2 %copy-start.4 = (f32[3,2,3200]{2,1,0:T(2,128)S(1)}, f32[3,2,3200]{2,1,0:T(2,128)}, u32[]{:S(2)}) copy-start(f32[3,2,3200]{2,1,0:T(2,128)} %param.5) | copy-start | bytes 230404
  5.3 31.0 %all-to-all-start = ((bf16[32,64,128]{2,1,0:T(8,128)(2,1)}), bf16[32,64,128]{2,1,0:T(8,128)(2,1)S(1)}, u32[]{:S(2)}, u32[]{:S(2)}) async-start(bf16[32,64,128]{2,1,0:T(8,128)(2,1)} %get-tuple-element.8), calls=%async_computation | async-start | bytes 1048576 | tf_op jit(solution)/shard_map/all_to_all | solution.py:294
  17.8 0.7 %copy-start.3 = (s32[3,16]{1,0:T(4,128)S(1)}, s32[3,16]{1,0:T(4,128)}, u32[]{:S(2)}) copy-start(s32[3,16]{1,0:T(4,128)} %mask_hbm.1) | copy-start | bytes 580
  19.6 6.6 %collective-permute-start.2 = (f32[12,32,128]{2,1,0:T(8,128)S(1)}, f32[12,32,128]{2,1,0:T(8,128)S(1)}, u32[]{:S(2)}, u32[]{:S(2)}) collective-permute-start(f32[12,32,128]{2,1,0:T(8,128)S(1)} %record_scales.1.refs_0_), channel_id=1, source_target_pairs={{0,6},{1,7},{2,0},{3,1},{4,2},{5,3},{6,4},{7,5},{8,14},{9,15},{10,... | collective-permute-start | bytes 589832 | tf_op jit(solution)/shard_map/ppermute | solution.py:302
  22.2 9.4 %collective-permute-start.1 = (f32[12,32,128]{2,1,0:T(8,128)S(1)}, f32[12,32,128]{2,1,0:T(8,128)S(1)}, u32[]{:S(2)}, u32[]{:S(2)}) collective-permute-start(f32[12,32,128]{2,1,0:T(8,128)S(1)} %record_scales.1.refs_0_), channel_id=1, source_target_pairs={{0,4},{1,5},{2,6},{3,7},{4,0},{5,1},{6,2},{7,3},{8,12},{9,13},{10,... | collective-permute-start | bytes 589832 | tf_op jit(solution)/shard_map/ppermute | solution.py:302
  22.7 12.0 %collective-permute-start = (f32[12,32,128]{2,1,0:T(8,128)S(1)}, f32[12,32,128]{2,1,0:T(8,128)S(1)}, u32[]{:S(2)}, u32[]{:S(2)}) collective-permute-start(f32[12,32,128]{2,1,0:T(8,128)S(1)} %record_scales.1.refs_0_), channel_id=1, source_target_pairs={{0,2},{1,3},{2,4},{3,5},{4,6},{5,7},{6,0},{7,1},{8,10},{9,11},{10,... | collective-permute-start | bytes 589832 | tf_op jit(solution)/shard_map/ppermute | solution.py:302
  23.3 11.9 %collective-permute-start.3 = (f32[12,32,128]{2,1,0:T(8,128)S(1)}, f32[12,32,128]{2,1,0:T(8,128)S(1)}, u32[]{:S(2)}, u32[]{:S(2)}) collective-permute-start(f32[12,32,128]{2,1,0:T(8,128)S(1)} %record_scales.1.refs_0_), channel_id=1, source_target_pairs={{0,1},{1,0},{2,3},{3,2},{4,5},{5,4},{6,7},{7,6},{8,9},{9,8},{10,11... | collective-permute-start | bytes 589832 | tf_op jit(solution)/shard_map/ppermute | solution.py:303
  26.2 9.0 %collective-permute-start.6 = (f32[12,32,128]{2,1,0:T(8,128)S(1)}, f32[12,32,128]{2,1,0:T(8,128)S(1)}, u32[]{:S(2)}, u32[]{:S(2)}) collective-permute-start(f32[12,32,128]{2,1,0:T(8,128)S(1)} %collective-permute-done.2.refs_3_), channel_id=1, source_target_pairs={{0,1},{1,0},{2,3},{3,2},{4,5},{5,4},{6,7},{7,6},{8,9},{9,8},{10,11... | collective-permute-start | bytes 589832 | tf_op jit(solution)/shard_map/ppermute | solution.py:303
  31.5 3.7 %collective-permute-start.5 = (f32[12,32,128]{2,1,0:T(8,128)S(1)}, f32[12,32,128]{2,1,0:T(8,128)S(1)}, u32[]{:S(2)}, u32[]{:S(2)}) collective-permute-start(f32[12,32,128]{2,1,0:T(8,128)S(1)} %collective-permute-done.1.refs_2_), channel_id=1, source_target_pairs={{0,1},{1,0},{2,3},{3,2},{4,5},{5,4},{6,7},{7,6},{8,9},{9,8},{10,11... | collective-permute-start | bytes 589832 | tf_op jit(solution)/shard_map/ppermute | solution.py:303
  34.7 1.6 %collective-permute-start.4 = (f32[12,32,128]{2,1,0:T(8,128)S(1)}, f32[12,32,128]{2,1,0:T(8,128)S(1)}, u32[]{:S(2)}, u32[]{:S(2)}) collective-permute-start(f32[12,32,128]{2,1,0:T(8,128)S(1)} %collective-permute-done.refs_1_), channel_id=1, source_target_pairs={{0,1},{1,0},{2,3},{3,2},{4,5},{5,4},{6,7},{7,6},{8,9},{9,8},{10,11... | collective-permute-start | bytes 589832 | tf_op jit(solution)/shard_map/ppermute | solution.py:303

commit v7 on v5

--- a/solution.py
+++ b/solution.py
@@ -64,11 +64,14 @@
     mean_one = window_sums(values) * (1.0 / L)
     mean_two = window_sums(values * values) * (1.0 / L)
     factor = lax.rsqrt(mean_two - mean_one * mean_one + EPSILON)
-    out_ref[0:size] = tiles_ref[...]
+    out_ref[0:size] = tiles_ref[...].astype(jnp.bfloat16)
     copy.wait()
     for record in range(size):
         weight = mask_ref[record >> 1, here * 2 + (record & 1)].astype(jnp.float32) * (1.0 / L)
-        out_ref[size + record] = factor[record] * weight
+        scale = factor[record] * weight
+        coarse = scale.astype(jnp.bfloat16)
+        out_ref[size + record] = coarse
+        out_ref[2 * size + record] = (scale - coarse.astype(jnp.float32)).astype(jnp.bfloat16)
 
 
 def select_kernel(index_ref, station_hbm, lag_hbm, waves_hbm, out_ref, meta_ref,
@@ -131,7 +134,7 @@
 def stack_kernel(meta_ref, index_ref, near_ref, far_ref, waves_hbm, out_ref,
                  waves_ref, tiles, scales, frames, units, acc, twice, dense, slots, sems):
     here = index_ref[1]
-    hops = near_ref.shape[0] // (2 * RECORDS)
+    hops = near_ref.shape[0] // (3 * RECORDS)
     waves_copy = pltpu.make_async_copy(waves_hbm, waves_ref, sems.at[2])
     row_copies = [pltpu.make_async_copy(row_ref, tiles.at[core], sems.at[core])
                   for core, row_ref in enumerate((near_ref, far_ref))]
@@ -152,14 +155,16 @@
         copy.wait()
         for hop in range(hops):
             first = owner_of(here, core, hop, hops) * RECORDS
-            at = 2 * RECORDS * hop
-            values = tiles[core, at:at + RECORDS].reshape(RECORDS * STEP, LANES).astype(jnp.bfloat16)
+            at = 3 * RECORDS * hop
+            values = tiles[core, at:at + RECORDS].reshape(RECORDS * STEP, LANES)
             for turn in range(TURNS):
                 rolled = values if turn == 0 else pltpu.roll(values, LANES - turn, 1)
                 frames[pl.ds(first, RECORDS), turn * STEP:(turn + 1) * STEP, :] = (
                     rolled.reshape(RECORDS, STEP, LANES)
                 )
-            scales[pl.ds(first, RECORDS)] = tiles[core, at + RECORDS:at + 2 * RECORDS]
+            coarse = tiles[core, at + RECORDS:at + 2 * RECORDS].astype(jnp.float32)
+            fine = tiles[core, at + 2 * RECORDS:at + 3 * RECORDS].astype(jnp.float32)
+            scales[pl.ds(first, RECORDS)] = coarse + fine
     waves_copy.wait()
     units[...] = waves_ref[...].reshape(units.shape).astype(jnp.float32)
     row = lax.broadcasted_iota(jnp.int32, (STEP, LANES), 0)
@@ -224,7 +229,7 @@
 def with_scales(index, channel_mask, tiles):
     return pl.pallas_call(
         scales_kernel,
-        out_shape=jax.ShapeDtypeStruct((2 * tiles.shape[0], STEP, LANES), jnp.float32),
+        out_shape=jax.ShapeDtypeStruct((3 * tiles.shape[0], STEP, LANES), jnp.bfloat16),
         in_specs=[SMEM, HBM, VMEM],
         out_specs=VMEM,
         scratch_shapes=[pltpu.SMEM(channel_mask.shape, jnp.int32), pltpu.SemaphoreType.DMA],
@@ -262,7 +267,7 @@
     peers = received.shape[0]
     slot_count = peers * CAP
     lines = NT * group_size // LANES
-    records = rows[0].shape[0]
+    records = 2 * rows[0].shape[0] // 3
     return pl.pallas_call(
         stack_kernel,
         out_shape=jax.ShapeDtypeStruct((slot_count, lines * LANES // slot_count), jnp.bfloat16),
@@ -270,7 +275,7 @@
         out_specs=VMEM,
         scratch_shapes=[
             pltpu.VMEM(received.shape, jnp.bfloat16),
-            pltpu.VMEM((2, records, STEP, LANES), jnp.float32),
+            pltpu.VMEM((2,) + rows[0].shape, jnp.bfloat16),
             pltpu.VMEM((records, STEP, LANES), jnp.float32),
             pltpu.VMEM((records, TURNS * STEP, LANES), jnp.bfloat16),
             pltpu.VMEM((peers * SLOT_ROWS, LANES), jnp.float32),
@@ -293,6 +298,10 @@
     stations_here = station_data.shape[1]
     index = jnp.stack([lax.axis_index("sta"), lax.axis_index("tpl")]).astype(jnp.int32)
 
+    waves = template_waves.reshape(group_size, 3, L).transpose(1, 0, 2)
+    outgoing, meta = slot_waves(index, pick_station, pick_lag, waves, sta_size)
+    received = lax.all_to_all(outgoing, "sta", split_axis=0, concat_axis=0, tiled=True)
+
     tiles = station_data.reshape(3, stations_here, BLOCKS, STEP).transpose(0, 1, 3, 2)
     tiles = jnp.pad(tiles, ((0, 0), (0, 0), (0, 0), (0, LANES - BLOCKS)))
     own = with_scales(index, channel_mask, tiles.reshape(3 * stations_here, STEP, LANES))
@@ -301,10 +310,6 @@
         row.append(lax.ppermute(own, "tpl", [(i, (i + hop) % tpl_size) for i in range(tpl_size)]))
     row = jnp.concatenate(row, axis=0)
     rows = [row, lax.ppermute(row, "tpl", [(i, i ^ 1) for i in range(tpl_size)])]
-
-    waves = template_waves.reshape(group_size, 3, L).transpose(1, 0, 2)
-    outgoing, meta = slot_waves(index, pick_station, pick_lag, waves, sta_size)
-    received = lax.all_to_all(outgoing, "sta", split_axis=0, concat_axis=0, tiled=True)
 
     partial_sums = partial_stack(meta, index, rows, received)
     arrived = lax.all_to_all(partial_sums, "sta", split_axis=0, concat_axis=0, tiled=True)

time: 61 us -> 60.2 us (0.987)
  the two profiles are of different devices: /device:TPU:2 before, /device:TPU:1 now
where the time goes in v7:
time: 60.2 us; the launch traced here: 59.8 us
  blocking collectives  18 us (30%)
  starting transfers between devices  16.8 us (28%)
  waiting for transfers between devices  10.6 us (18%)
  Pallas kernels  9.99 us (17%)
  local copies, waits for them, and re-layouts  4.04 us (7%)
    all_to_all x1, blocking collectives, body(): lax.all_to_all(partial_sums, 'sta', split_axis=0, concat_axis=0, tiled=True)  18 us
    all_to_all x1, starting transfers between devices, body(): lax.all_to_all(outgoing, 'sta', split_axis=0, concat_axis=0, tiled=True)  12.2 us
    ppermute x3, waiting for transfers between devices, body(): lax.ppermute(own, 'tpl', [(i, (i + hop) % tpl_size) for i in range(tpl_si...  8.94 us
    pallas_call x1, Pallas kernels, partial_stack(): pl.pallas_call(stack_kernel, out_shape=jax.ShapeDtypeStruct((slot_count,...  5.94 us
    ppermute x3, starting transfers between devices, body(): lax.ppermute(own, 'tpl', [(i, (i + hop) % tpl_size) for i in range(tpl_si...  3.68 us
    unnamed x11, local copies, waits for them, and re-layouts  3.05 us
    pallas_call x1, Pallas kernels, slot_waves(): pl.pallas_call(select_kernel, out_shape=(jax.ShapeDtypeStruct((peers, SLO...  2.92 us
    ppermute x1, waiting for transfers between devices, body(): lax.ppermute(row, 'tpl', [(i, i ^ 1) for i in range(tpl_size)])  1.63 us
  transfers between devices with their start and end apart: 5, of which 4 were waited for; matrix products, arithmetic and copies ran while one was open for 1% of the time, Pallas kernels for 2%

profile of v7, /device:TPU:1, one launch (start us, length us, event | category | flops | bytes accessed | tf_op | source)
XLA Modules:
  0.0 59.8 jit_solution(5559113890038071580)
XLA Ops:
  0.0 0.1 pad_add_fusion.index_ref
  0.1 0.6 %copy-done.1 = s32[32,32]{1,0:T(8,128)S(1)} copy-done((s32[32,32]{1,0:T(8,128)S(1)}, s32[32,32]{1,0:T(8,128)}, u32[]{:S(2)}) %copy-start.1) | copy-done | bytes 4120
  0.7 0.9 %copy-done = bf16[32,1,3,640]{3,0,2,1:T(8,128)(2,1)S(1)} copy-done((bf16[32,1,3,640]{3,0,2,1:T(8,128)(2,1)S(1)}, bf16[32,1,3,640]{3,0,2,1:T(8,128)(2,1)}, u32[]{:S(2)}) %copy-start) | copy-done | bytes 122904
  1.6 0.7 %copy-done.2 = s32[32,32]{1,0:T(8,128)S(1)} copy-done((s32[32,32]{1,0:T(8,128)S(1)}, s32[32,32]{1,0:T(8,128)}, u32[]{:S(2)}) %copy-start.2) | copy-done | bytes 4120
  2.3 2.9 %select_waves.1 = (bf16[32,64,128]{2,1,0:T(8,128)(2,1)}, s32[4,32]{1,0:T(4,128)S(1)}) custom-call(s32[2]{0:T(128)S(1)} %pad_add_fusion.index_ref, s32[32,32]{1,0:T(8,128)S(1)} %copy-done.1, s32[32,32]{1,0:T(8,128)S(1)} %copy-done.2, bf16[3,32,640]{2,1,0:T(8,128)(2,1)S(1)} %bitcast.8), custom_call_target="tpu_custom_call" | custom-call | flops 16000000 | bytes 620000 | tf_op jit(solution)/shard_map/select_waves/pallas_call | solution.py:244
  5.3 12.2 %all-to-all-start = ((bf16[32,64,128]{2,1,0:T(8,128)(2,1)}), bf16[32,64,128]{2,1,0:T(8,128)(2,1)S(1)}, u32[]{:S(2)}, u32[]{:S(2)}) async-start(bf16[32,64,128]{2,1,0:T(8,128)(2,1)} %get-tuple-element.8), calls=%async_computation | async-start | bytes 1048576 | tf_op jit(solution)/shard_map/all_to_all | solution.py:303
  17.5 0.2 reshape.17
  17.7 0.1 copy.9
  17.8 0.7 %copy-done.3 = s32[3,16]{1,0:T(4,128)S(1)} copy-done((s32[3,16]{1,0:T(4,128)S(1)}, s32[3,16]{1,0:T(4,128)}, u32[]{:S(2)}) %copy-start.3) | copy-done | bytes 216
  18.5 1.1 %record_scales.1 = bf16[18,32,128]{2,1,0:T(8,128)(2,1)S(1)} custom-call(s32[2]{0:T(128)S(1)} %pad_add_fusion.index_ref, s32[3,16]{1,0:T(4,128)S(1)} %copy-done.3, f32[6,32,128]{2,1,0:T(8,128)S(1)} %bitcast.7), custom_call_target="tpu_custom_call" | custom-call | flops 2000000 | bytes 300000 | tf_op jit(solution)/shard_map/record_scales/pallas_call | solution.py:230
  19.6 2.6 %collective-permute-start.2 = (bf16[18,32,128]{2,1,0:T(8,128)(2,1)S(1)}, bf16[18,32,128]{2,1,0:T(8,128)(2,1)S(1)}, u32[]{:S(2)}, u32[]{:S(2)}) collective-permute-start(bf16[18,32,128]{2,1,0:T(8,128)(2,1)S(1)} %record_scales.1), channel_id=1, source_target_pairs={{0,6},{1,7},{2,0},{3,1},{4,2},{5,3},{6,4},{7,5},{8,14},{9,15},{10,... | collective-permute-start | bytes 442376 | tf_op jit(solution)/shard_map/ppermute | solution.py:310
  22.2 0.5 collective-permute-start.1
  22.7 0.6 %collective-permute-start = (bf16[18,32,128]{2,1,0:T(8,128)(2,1)S(1)}, bf16[18,32,128]{2,1,0:T(8,128)(2,1)S(1)}, u32[]{:S(2)}, u32[]{:S(2)}) collective-permute-start(bf16[18,32,128]{2,1,0:T(8,128)(2,1)S(1)} %record_scales.1), channel_id=1, source_target_pairs={{0,2},{1,3},{2,4},{3,5},{4,6},{5,7},{6,0},{7,1},{8,10},{9,11},{10,... | collective-permute-start | bytes 442376 | tf_op jit(solution)/shard_map/ppermute | solution.py:310
  23.3 2.1 %collective-permute-done.2 = bf16[18,32,128]{2,1,0:T(8,128)(2,1)S(1)} collective-permute-done((bf16[18,32,128]{2,1,0:T(8,128)(2,1)S(1)}, bf16[18,32,128]{2,1,0:T(8,128)(2,1)S(1)}, u32[]{:S(2)}, u32[]{:S(2)}) %collective-permute-start.2) | collective-permute-done | bytes 147488 | tf_op jit(solution)/shard_map/ppermute | solution.py:310
  25.4 2.6 %collective-permute-done.1 = bf16[18,32,128]{2,1,0:T(8,128)(2,1)S(1)} collective-permute-done((bf16[18,32,128]{2,1,0:T(8,128)(2,1)S(1)}, bf16[18,32,128]{2,1,0:T(8,128)(2,1)S(1)}, u32[]{:S(2)}, u32[]{:S(2)}) %collective-permute-start.1) | collective-permute-done | bytes 147488 | tf_op jit(solution)/shard_map/ppermute | solution.py:310
  28.0 4.3 %collective-permute-done = bf16[18,32,128]{2,1,0:T(8,128)(2,1)S(1)} collective-permute-done((bf16[18,32,128]{2,1,0:T(8,128)(2,1)S(1)}, bf16[18,32,128]{2,1,0:T(8,128)(2,1)S(1)}, u32[]{:S(2)}, u32[]{:S(2)}) %collective-permute-start) | collective-permute-done | bytes 147488 | tf_op jit(solution)/shard_map/ppermute | solution.py:310
  32.2 0.1 pad_maximum_fusion.near_ref
  32.3 0.9 %collective-permute-start.3 = (bf16[72,32,128]{2,1,0:T(8,128)(2,1)S(1)}, bf16[72,32,128]{2,1,0:T(8,128)(2,1)S(1)}, u32[]{:S(2)}, u32[]{:S(2)}) collective-permute-start(bf16[72,32,128]{2,1,0:T(8,128)(2,1)S(1)} %pad_maximum_fusion.near_ref), channel_id=1, source_target_pairs={{0,1},{1,0},{2,3},{3,2},{4,5},{5,4},{6,7},{7,6},{8,9},{9,8},{10,11... | collective-permute-start | bytes 1769480 | tf_op jit(solution)/shard_map/ppermute | solution.py:312
  33.3 1.6 %collective-permute-done.3.far_ref = bf16[72,32,128]{2,1,0:T(8,128)(2,1)S(1)} collective-permute-done((bf16[72,32,128]{2,1,0:T(8,128)(2,1)S(1)}, bf16[72,32,128]{2,1,0:T(8,128)(2,1)S(1)}, u32[]{:S(2)}, u32[]{:S(2)}) %collective-permute-start.3) | collective-permute-done | bytes 589856 | tf_op jit(solution)/shard_map/ppermute | solution.py:312
  34.9 5.9 %stack_picks.1 = bf16[128,384]{1,0:T(8,128)(2,1)S(1)} custom-call(s32[4,32]{1,0:T(4,128)S(1)} %get-tuple-element.7.meta_ref, s32[2]{0:T(128)S(1)} %pad_add_fusion.index_ref, bf16[72,32,128]{2,1,0:T(8,128)(2,1)S(1)} %pad_maximum_fusion.near_ref, bf16[72,32,128]{2,1,0:T(8,128)(2,1)S(1)} %collective-permute-done.3.far_ref, ...), custom_call_target="tpu_custom_call" | custom-call | flops 200000000 | bytes 8000000 | tf_op jit(solution)/shard_map/stack_picks/pallas_call | solution.py:271
  40.9 18.0 %all_to_all.14 = bf16[32,4,384]{2,1,0:T(4,128)(2,1)S(1)} all-to-all(bf16[32,4,384]{2,1,0:T(4,128)(2,1)S(1)} %all_to_all.10), channel_id=1, replica_groups=mesh['sta'=32,'tpl'=8] {'sta'}, dimensions={0} | all-to-all | bytes 196608 | tf_op jit(solution)/shard_map/all_to_all | solution.py:315
  58.9 0.1 convert_reduce_fusion
  59.0 0.1 reshape.19
  59.1 0.7 %copy.8 = f32[48,32]{0,1:T(8,128)} copy(f32[48,32]{1,0:T(8,128)S(1)} %reshape.19) | data formatting | bytes 12288 | tf_op jit(solution)/shard_map/reshape | solution.py:317
  (9 shorter events, 0.1 us)
Async XLA Ops:
  0.0 0.7 %copy-start.1 = (s32[32,32]{1,0:T(8,128)S(1)}, s32[32,32]{1,0:T(8,128)}, u32[]{:S(2)}) copy-start(s32[32,32]{1,0:T(8,128)} %station_hbm.1) | copy-start | bytes 12292
  0.7 0.9 %copy-start = (bf16[32,1,3,640]{3,0,2,1:T(8,128)(2,1)S(1)}, bf16[32,1,3,640]{3,0,2,1:T(8,128)(2,1)}, u32[]{:S(2)}) copy-start(bf16[32,1,3,640]{3,0,2,1:T(8,128)(2,1)} %param.7) | copy-start | bytes 368644
  1.6 0.7 %copy-start.2 = (s32[32,32]{1,0:T(8,128)S(1)}, s32[32,32]{1,0:T(8,128)}, u32[]{:S(2)}) copy-start(s32[32,32]{1,0:T(8,128)} %lag_hbm.1) | copy-start | bytes 12292
  5.3 12.2 %copy-start.4 = (f32[3,2,3200]{2,1,0:T(2,128)S(1)}, f32[3,2,3200]{2,1,0:T(2,128)}, u32[]{:S(2)}) copy-start(f32[3,2,3200]{2,1,0:T(2,128)} %param.5) | copy-start | bytes 230404
  5.3 29.6 %all-to-all-start = ((bf16[32,64,128]{2,1,0:T(8,128)(2,1)}), bf16[32,64,128]{2,1,0:T(8,128)(2,1)S(1)}, u32[]{:S(2)}, u32[]{:S(2)}) async-start(bf16[32,64,128]{2,1,0:T(8,128)(2,1)} %get-tuple-element.8), calls=%async_computation | async-start | bytes 1048576 | tf_op jit(solution)/shard_map/all_to_all | solution.py:303
  17.8 0.7 %copy-start.3 = (s32[3,16]{1,0:T(4,128)S(1)}, s32[3,16]{1,0:T(4,128)}, u32[]{:S(2)}) copy-start(s32[3,16]{1,0:T(4,128)} %mask_hbm.1) | copy-start | bytes 580
  19.6 5.8 %collective-permute-start.2 = (bf16[18,32,128]{2,1,0:T(8,128)(2,1)S(1)}, bf16[18,32,128]{2,1,0:T(8,128)(2,1)S(1)}, u32[]{:S(2)}, u32[]{:S(2)}) collective-permute-start(bf16[18,32,128]{2,1,0:T(8,128)(2,1)S(1)} %record_scales.1), channel_id=1, source_target_pairs={{0,6},{1,7},{2,0},{3,1},{4,2},{5,3},{6,4},{7,5},{8,14},{9,15},{10,... | collective-permute-start | bytes 442376 | tf_op jit(solution)/shard_map/ppermute | solution.py:310
  22.2 5.8 %collective-permute-start.1 = (bf16[18,32,128]{2,1,0:T(8,128)(2,1)S(1)}, bf16[18,32,128]{2,1,0:T(8,128)(2,1)S(1)}, u32[]{:S(2)}, u32[]{:S(2)}) collective-permute-start(bf16[18,32,128]{2,1,0:T(8,128)(2,1)S(1)} %record_scales.1), channel_id=1, source_target_pairs={{0,4},{1,5},{2,6},{3,7},{4,0},{5,1},{6,2},{7,3},{8,12},{9,13},{10,... | collective-permute-start | bytes 442376 | tf_op jit(solution)/shard_map/ppermute | solution.py:310
  22.7 9.5 %collective-permute-start = (bf16[18,32,128]{2,1,0:T(8,128)(2,1)S(1)}, bf16[18,32,128]{2,1,0:T(8,128)(2,1)S(1)}, u32[]{:S(2)}, u32[]{:S(2)}) collective-permute-start(bf16[18,32,128]{2,1,0:T(8,128)(2,1)S(1)} %record_scales.1), channel_id=1, source_target_pairs={{0,2},{1,3},{2,4},{3,5},{4,6},{5,7},{6,0},{7,1},{8,10},{9,11},{10,... | collective-permute-start | bytes 442376 | tf_op jit(solution)/shard_map/ppermute | solution.py:310
  32.3 2.6 %collective-permute-start.3 = (bf16[72,32,128]{2,1,0:T(8,128)(2,1)S(1)}, bf16[72,32,128]{2,1,0:T(8,128)(2,1)S(1)}, u32[]{:S(2)}, u32[]{:S(2)}) collective-permute-start(bf16[72,32,128]{2,1,0:T(8,128)(2,1)S(1)} %pad_maximum_fusion.near_ref), channel_id=1, source_target_pairs={{0,1},{1,0},{2,3},{3,2},{4,5},{5,4},{6,7},{7,6},{8,9},{9,8},{10,11... | collective-permute-start | bytes 1769480 | tf_op jit(solution)/shard_map/ppermute | solution.py:312

commit v8 on v4

v8 whole, which is shorter than its diff:
```python
import jax
import jax.numpy as jnp
from jax import lax
from jax.experimental import pallas as pl
from jax.experimental.pallas import tpu as pltpu
from jax.sharding import PartitionSpec as P

NT = 1536
L = 640
LAGS = 1024
SAMPLES = 3200
CAP = 4
STEP = 32
LANES = 128
BLOCKS = SAMPLES // STEP
OUT_BLOCKS = NT // STEP
TILES = L // LANES
TURNS = 8
UNROLL = 8
SLOT_ROWS = 64
RECORDS = 6
STATION_BITS = 4
EPSILON = 1e-05
VALID = 1 << 27


def exclusive_prefix(values):
    lanes = values.shape[-1]
    groups = values.reshape(-1, 8, lanes)
    row = lax.broadcasted_iota(jnp.int32, groups.shape, 1)
    total = groups
    for shift in (1, 2, 4):
        total = total + jnp.where(row >= shift, pltpu.roll(total, shift, 1), 0.0)
    inner = jnp.where(row >= 1, pltpu.roll(total, 1, 1), 0.0).reshape(-1, STEP // 8, 8, lanes)
    last = total.reshape(-1, STEP // 8, 8, lanes)[:, :, 7:8]
    pieces = [inner[:, 0:1]]
    carry = last[:, 0:1]
    for group in range(1, STEP // 8):
        pieces.append(inner[:, group:group + 1] + carry)
        carry = carry + last[:, group:group + 1]
    return jnp.concatenate(pieces, axis=1).reshape(values.shape)


def window_sums(values):
    width = values.shape[-1]
    span = L // STEP
    ahead = pltpu.roll(values, width - span, 1) - values
    two = jnp.sum(values.reshape(-1, STEP, width), axis=1)
    two = two + pltpu.roll(two, width - 1, 1)
    four = two + pltpu.roll(two, width - 2, 1)
    eight = four + pltpu.roll(four, width - 4, 1)
    sixteen = eight + pltpu.roll(eight, width - 8, 1)
    whole = sixteen + pltpu.roll(four, width - 16, 1)
    inner = exclusive_prefix(ahead).reshape(-1, STEP, width)
    return whole[:, None, :] + inner


def select_kernel(index_ref, station_ref, waves_ref, out_ref, staged):
    group_size = station_ref.shape[0]
    square = (group_size, group_size)
    row = lax.broadcasted_iota(jnp.int32, square, 0)
    column = lax.broadcasted_iota(jnp.int32, square, 1)
    owners = station_ref[...] >> STATION_BITS
    down = jnp.sum(jnp.where(column == index_ref[0], owners, 0), axis=1, keepdims=True)
    down = jnp.broadcast_to(down, square)
    across = jnp.sum(jnp.where(row == column, down, 0), axis=0, keepdims=True)
    same = (down == across) & (row < column)
    place = jnp.sum(same.astype(jnp.int32), axis=0, keepdims=True)
    slot = across * CAP + place
    peers = out_ref.shape[0]
    peer = lax.broadcasted_iota(jnp.int32, (peers, group_size), 0)
    selects = [(peer * CAP + k == slot).astype(jnp.float32).astype(jnp.bfloat16) for k in range(CAP)]
    select = jnp.concatenate(selects, axis=0)
    for c in range(3):
        values = waves_ref[c].astype(jnp.float32)
        centred = values - jnp.mean(values, axis=-1, keepdims=True)
        power = jnp.mean(centred * centred, axis=-1, keepdims=True)
        unit = (centred / jnp.sqrt(power + EPSILON)).astype(jnp.bfloat16)
        picked = jnp.dot(select, unit, preferred_element_type=jnp.float32)
        for tile in range(TILES):
            columns = slice(tile * LANES, (tile + 1) * LANES)
            for k in range(CAP):
                at = (c * TILES + tile) * CAP + k
                staged[pl.ds(at, peers, stride=SLOT_ROWS), :] = picked[k * peers:(k + 1) * peers, columns]
    for at in range(3 * TILES * CAP, SLOT_ROWS):
        staged[pl.ds(at, peers, stride=SLOT_ROWS), :] = jnp.zeros((peers, LANES), jnp.float32)
    out_ref[...] = staged[...].astype(jnp.bfloat16).reshape(out_ref.shape)


def owner_of(here, core, hop, hops):
    return ((here - 2 * hop) & (2 * hops - 1)) ^ core


def scales_kernel(index_ref, mask_hbm, station_ref, lag_ref, near_ref, far_ref, scales, entries,
                  meta_vmem, meta, mask_ref, sems):
    mask_copy = pltpu.make_async_copy(mask_hbm, mask_ref, sems.at[0])
    mask_copy.start()
    square = station_ref.shape
    row = lax.broadcasted_iota(jnp.int32, square, 0)
    column = lax.broadcasted_iota(jnp.int32, square, 1)
    stations = station_ref[...]
    landing = (stations >> STATION_BITS) == index_ref[0]
    earlier = (column < row).astype(jnp.float32).astype(jnp.bfloat16)
    arrival = jnp.dot(earlier, landing.astype(jnp.float32).astype(jnp.bfloat16), preferred_element_type=jnp.float32)
    local = stations & (2**STATION_BITS - 1)
    packed = VALID + (column << 22) + (lag_ref[...] << 9) + (local << 5) + row
    for k in range(CAP):
        held = landing & (arrival.astype(jnp.int32) == k)
        meta_vmem[k:k + 1, :] = jnp.sum(jnp.where(held, packed, 0), axis=0, keepdims=True)
    meta_copy = pltpu.make_async_copy(meta_vmem, meta, sems.at[1])
    meta_copy.start()

    here = index_ref[1]
    hops = near_ref.shape[0] // RECORDS
    mask_copy.wait()
    for core, tile_ref in enumerate((near_ref, far_ref)):
        for hop in range(hops):
            owner = owner_of(here, core, hop, hops)
            values = tile_ref[hop * RECORDS:(hop + 1) * RECORDS].reshape(RECORDS * STEP, LANES)
            mean_one = window_sums(values) * (1.0 / L)
            mean_two = window_sums(values * values) * (1.0 / L)
            factor = lax.rsqrt(mean_two - mean_one * mean_one + EPSILON)
            for record in range(RECORDS):
                weight = mask_ref[record >> 1, owner * 2 + (record & 1)].astype(jnp.float32) * (1.0 / L)
                scales[owner * RECORDS + record] = factor[record] * weight

    meta_copy.wait()

    def list_slot(slot, count):
        packed = meta[slot & (CAP - 1), slot >> 2]
        entries[count] = packed + ((slot & (CAP - 1)) << 20)
        return count + (packed >> 27)

    total = meta.shape[1] * CAP
    count = lax.fori_loop(0, total, list_slot, jnp.int32(0), unroll=16)
    for spare in range(UNROLL):
        entries[count + spare] = -1
    entries[total + UNROLL] = count


def stack_kernel(entries, index_ref, near_ref, far_ref, scales_hbm, waves_hbm, out_ref,
                 waves_ref, tiles, scales, frames, units, acc, twice, dense, sems):
    here = index_ref[1]
    hops = near_ref.shape[0] // RECORDS
    row_copies = [pltpu.make_async_copy(row_ref, tiles.at[core], sems.at[core])
                  for core, row_ref in enumerate((near_ref, far_ref))]
    waves_copy = pltpu.make_async_copy(waves_hbm, waves_ref, sems.at[2])
    scales_copy = pltpu.make_async_copy(scales_hbm, scales, sems.at[3])
    for copy in row_copies + [waves_copy, scales_copy]:
        copy.start()
    count = entries[entries.shape[0] - 1]
    acc[...] = jnp.zeros_like(acc)

    for core, copy in enumerate(row_copies):
        copy.wait()
        for hop in range(hops):
            first = owner_of(here, core, hop, hops) * RECORDS
            at = RECORDS * hop
            values = tiles[core, at:at + RECORDS].reshape(RECORDS * STEP, LANES).astype(jnp.bfloat16)
            for turn in range(TURNS):
                rolled = values if turn == 0 else pltpu.roll(values, LANES - turn, 1)
                frames[pl.ds(first, RECORDS), turn * STEP:(turn + 1) * STEP, :] = (
                    rolled.reshape(RECORDS, STEP, LANES)
                )
    waves_copy.wait()
    units[...] = waves_ref[...].reshape(units.shape).astype(jnp.float32)
    scales_copy.wait()
    row = lax.broadcasted_iota(jnp.int32, (STEP, LANES), 0)
    lane = lax.broadcasted_iota(jnp.int32, (STEP, LANES), 1)
    own = lane >= row

    def one_pick(entry, spare):
        held = entry >= 0
        packed = jnp.maximum(entry, 0)
        template = jnp.where(held, packed & 31, acc.shape[0] // STEP - 1)
        first_row = ((packed >> 22) & 31) * SLOT_ROWS + ((packed >> 20) & (CAP - 1))
        station = (packed >> 5) & 15
        lag = (packed >> 9) & 2047
        total = jnp.zeros((STEP, LANES), jnp.float32)
        for c in range(3):
            record = (station >> 1) * RECORDS + 2 * c + (station & 1)
            before = jnp.zeros((STEP, LANES), jnp.float32)
            columns = []
            for tile in range(TILES):
                at = first_row + (c * TILES + tile) * CAP
                wave = units[pl.ds(at, STEP, stride=0), :]
                spread = pltpu.roll(wave, 0, 1, stride=1, stride_axis=0)
                columns.append(jnp.where(own, spread, before).astype(jnp.bfloat16))
                before = spread
            columns.append(jnp.where(own, 0.0, before).astype(jnp.bfloat16))
            left = jnp.concatenate(
                [jnp.concatenate(columns[i:i + 2], axis=1) for i in range(0, TILES + 1, 2)], axis=0
            )
            product = jnp.dot(left, frames[record], preferred_element_type=jnp.float32)
            summed = product[:STEP]
            for part in range(1, (TILES + 1) // 2):
                later = product[part * STEP:(part + 1) * STEP]
                summed = summed + pltpu.roll(later, LANES - TURNS * part, 1)
            total = total + summed * scales[record]
        first = pltpu.roll(total, LANES - (lag >> 5), 1)
        twice[spare, 0:STEP, :] = first
        twice[spare, STEP:2 * STEP, :] = pltpu.roll(first, LANES - 1, 1)
        shifted = twice[spare, pl.ds(lag & (STEP - 1), STEP), :]
        return pl.ds(pl.multiple_of(template * STEP, STEP), STEP), shifted

    @pl.loop(0, (count + UNROLL - 1) // UNROLL)
    def _(index):
        done = [one_pick(entries[index * UNROLL + spare], spare) for spare in range(UNROLL)]
        for rows, shifted in done:
            acc[rows, :] += shifted

    for group in range(STEP // 4):
        parts = [acc[pl.ds(4 * group + j, STEP, stride=STEP), :] for j in range(4)]
        turned = jnp.concatenate(parts, axis=0).T
        dense[pl.ds(group, OUT_BLOCKS, stride=8), :] = turned[:OUT_BLOCKS]
    for part in range(out_ref.shape[1] // LANES):
        rows = dense[pl.ds(part, out_ref.shape[0], stride=3), :]
        out_ref[:, part * LANES:(part + 1) * LANES] = rows.astype(out_ref.dtype)


SMEM = pl.BlockSpec(memory_space=pltpu.SMEM)
VMEM = pl.BlockSpec(memory_space=pltpu.VMEM)
ANY = pl.BlockSpec(memory_space=pl.ANY)
HBM = pl.BlockSpec(memory_space=pltpu.HBM)


def slot_waves(index, pick_station, template_waves, peers):
    return pl.pallas_call(
        select_kernel,
        out_shape=jax.ShapeDtypeStruct((peers, SLOT_ROWS, LANES), jnp.bfloat16),
        in_specs=[SMEM, VMEM, VMEM],
        out_specs=VMEM,
        scratch_shapes=[pltpu.VMEM((peers * SLOT_ROWS, LANES), jnp.float32)],
        compiler_params=pltpu.CompilerParams(vmem_limit_bytes=4 * 1024 * 1024),
        cost_estimate=pl.CostEstimate(flops=16_000_000, transcendentals=100, bytes_accessed=620_000),
        name="select_waves",
    )(index, pick_station, template_waves)


def scales_and_entries(index, channel_mask, pick_station, pick_lag, rows):
    slot_count = pick_station.shape[1] * CAP
    return pl.pallas_call(
        scales_kernel,
        out_shape=(
            jax.ShapeDtypeStruct((2 * rows[0].shape[0], STEP, LANES), jnp.float32),
            jax.ShapeDtypeStruct((slot_count + UNROLL + 1,), jnp.int32),
        ),
        in_specs=[SMEM, HBM, VMEM, VMEM, VMEM, VMEM],
        out_specs=(VMEM, SMEM),
        scratch_shapes=[
            pltpu.VMEM((CAP, pick_station.shape[1]), jnp.int32),
            pltpu.SMEM((CAP, pick_station.shape[1]), jnp.int32),
            pltpu.SMEM(channel_mask.shape, jnp.int32),
            pltpu.SemaphoreType.DMA((2,)),
        ],
        compiler_params=pltpu.CompilerParams(vmem_limit_bytes=8 * 1024 * 1024),
        cost_estimate=pl.CostEstimate(flops=6000_000_000, transcendentals=200_000, bytes_accessed=2_000_000),
        name="record_scales",
    )(index, channel_mask, pick_station, pick_lag, *rows)


def partial_stack(entries, index, rows, scales, received, group_size):
    peers = received.shape[0]
    slot_count = peers * CAP
    lines = NT * group_size // LANES
    records = scales.shape[0]
    return pl.pallas_call(
        stack_kernel,
        out_shape=jax.ShapeDtypeStruct((slot_count, lines * LANES // slot_count), jnp.bfloat16),
        in_specs=[SMEM, SMEM, ANY, ANY, ANY, ANY],
        out_specs=VMEM,
        scratch_shapes=[
            pltpu.VMEM(received.shape, jnp.bfloat16),
            pltpu.VMEM((2,) + rows[0].shape, jnp.float32),
            pltpu.VMEM(scales.shape, jnp.float32),
            pltpu.VMEM((records, TURNS * STEP, LANES), jnp.bfloat16),
            pltpu.VMEM((peers * SLOT_ROWS, LANES), jnp.float32),
            pltpu.VMEM(((group_size + 1) * STEP, LANES), jnp.float32),
            pltpu.VMEM((UNROLL, 2 * STEP, LANES), jnp.float32),
            pltpu.VMEM((lines, LANES), jnp.float32),
            pltpu.SemaphoreType.DMA((4,)),
        ],
        compiler_params=pltpu.CompilerParams(vmem_limit_bytes=16 * 1024 * 1024),
        cost_estimate=pl.CostEstimate(flops=200_000_000, transcendentals=0, bytes_accessed=8_000_000),
        name="stack_picks",
    )(entries, index, *rows, scales, received)


def body(station_data, channel_mask, template_waves, pick_station, pick_lag):
    sta_size = lax.axis_size("sta")
    tpl_size = lax.axis_size("tpl")
    group_size = pick_station.shape[0]
    stations_here = station_data.shape[1]
    index = jnp.stack([lax.axis_index("sta"), lax.axis_index("tpl")]).astype(jnp.int32)

    tiles = station_data.reshape(3, stations_here, BLOCKS, STEP).transpose(0, 1, 3, 2)
    tiles = jnp.pad(tiles, ((0, 0), (0, 0), (0, 0), (0, LANES - BLOCKS)))
    own = tiles.reshape(3 * stations_here, STEP, LANES)
    near = [own]
    for hop in range(2, tpl_size, 2):
        near.append(lax.ppermute(own, "tpl", [(i, (i + hop) % tpl_size) for i in range(tpl_size)]))
    near = jnp.concatenate(near, axis=0)
    rows = [near, lax.ppermute(near, "tpl", [(i, i ^ 1) for i in range(tpl_size)])]

    waves = template_waves.reshape(group_size, 3, L).transpose(1, 0, 2)
    outgoing = slot_waves(index, pick_station, waves, sta_size)
    received = lax.all_to_all(outgoing, "sta", split_axis=0, concat_axis=0, tiled=True)

    scales, entries = scales_and_entries(index, channel_mask, pick_station, pick_lag, rows)
    partial_sums = partial_stack(entries, index, rows, scales, received, group_size)
    arrived = lax.all_to_all(partial_sums, "sta", split_axis=0, concat_axis=0, tiled=True)
    arrived = arrived.reshape(sta_size, CAP, -1).astype(jnp.float32)
    return jnp.sum(arrived, axis=0).reshape(NT // sta_size, group_size)


def solution(mesh):
    in_specs = (
        P(None, ("sta", "tpl"), None),
        P(None, "sta"),
        P("tpl", "sta", None, None),
        P("tpl", None),
        P("tpl", None),
    )
    return jax.shard_map(body, mesh=mesh, in_specs=in_specs, out_specs=P("sta", "tpl"), check_vma=False)
```

time: 60.5 us -> 58.5 us (0.967); the launches traced: 59.5 us -> 58.2 us
  waiting for transfers between devices: 6.4 us -> 12 us
  local copies, waits for them, and re-layouts: 7.37 us -> 2.01 us
  other arithmetic: 1.61 us -> 0.17 us
    all_to_all x1, waiting for transfers between devices: 4.87 us -> 10.3 us  [body(): lax.all_to_all(outgoing, 'sta', split_axis=0, concat_axis=0, tiled=True)]
    unnamed x15 -> x9, local copies, waits for them, and re-layouts: 5.49 us -> 0.14 us
    pallas_call x1, Pallas kernels: 5.65 us -> 4.36 us  [scales_and_entries(): pl.pallas_call(scales_kernel, out_shape=(jax.ShapeDtypeStruct((2 * rows[0...]
    pallas_call x1, Pallas kernels: 4.78 us -> 5.67 us  [partial_stack(): pl.pallas_call(stack_kernel, out_shape=jax.ShapeDtypeStruct((slot_count,...]
    add x2 -> x0, other arithmetic: 0.75 us -> none  [the longest x1 0.75 us: body(): VALID + (pick_lag << 9) + (pick_station - my_index * station_count << 5)]
    eq x1 -> x0, other arithmetic: 0.73 us -> none  [body(): landing = owners == my_index]
  transfers between devices with their start and end apart: 5 -> 5, of which waited for: 2 -> 2; matrix products, arithmetic and copies ran while one was open for 3% -> 0% of each run, Pallas kernels for 13% -> 12%
where the time goes in v8:
time: 58.5 us; the launch traced here: 58.2 us
  starting transfers between devices  16.4 us (28%)
  blocking collectives  15.1 us (26%)
  Pallas kernels  12.4 us (21%)
  waiting for transfers between devices  12 us (21%)
  local copies, waits for them, and re-layouts  2.01 us (3%)
    all_to_all x1, blocking collectives, body(): lax.all_to_all(partial_sums, 'sta', split_axis=0, concat_axis=0, tiled=True)  15.1 us
    all_to_all x1, starting transfers between devices, body(): lax.all_to_all(outgoing, 'sta', split_axis=0, concat_axis=0, tiled=True)  11.5 us
    all_to_all x1, waiting for transfers between devices, body(): lax.all_to_all(outgoing, 'sta', split_axis=0, concat_axis=0, tiled=True)  10.3 us
    pallas_call x1, Pallas kernels, partial_stack(): pl.pallas_call(stack_kernel, out_shape=jax.ShapeDtypeStruct((slot_count,...  5.67 us
    ppermute x3, starting transfers between devices, body(): lax.ppermute(own, 'tpl', [(i, (i + hop) % tpl_size) for i in range(tpl_si...  4.83 us
    pallas_call x1, Pallas kernels, scales_and_entries(): pl.pallas_call(scales_kernel, out_shape=(jax.ShapeDtypeStruct((2 * rows[0...  4.36 us
    pallas_call x1, Pallas kernels, slot_waves(): pl.pallas_call(select_kernel, out_shape=jax.ShapeDtypeStruct((peers, SLOT...  2.37 us
    ppermute x1, waiting for transfers between devices, body(): lax.ppermute(near, 'tpl', [(i, i ^ 1) for i in range(tpl_size)])  1.71 us
  transfers between devices with their start and end apart: 5, of which 2 were waited for; matrix products, arithmetic and copies ran while one was open for 0% of the time, Pallas kernels for 12%

profile of v8, /device:TPU:2, one launch (start us, length us, event | category | flops | bytes accessed | tf_op | source)
XLA Modules:
  0.0 58.2 jit_solution(8447210776338558300)
XLA Ops:
  0.0 1.0 %reshape.16 = f32[3,2,100,32]{3,2,1,0:T(8,128)S(1)} reshape(f32[3,2,3200]{2,1,0:T(2,128)} %param.5) | data formatting | bytes 153600 | tf_op jit(solution)/shard_map/reshape | solution.py:296
  1.1 0.1 copy.9
  1.2 0.0 copy-start.1
  1.2 2.3 %collective-permute-start.2 = (f32[6,32,128]{2,1,0:T(8,128)S(1)}, f32[6,32,128]{2,1,0:T(8,128)S(1)}, u32[]{:S(2)}, u32[]{:S(2)}) collective-permute-start(f32[6,32,128]{2,1,0:T(8,128)S(1)} %bitcast.9), channel_id=1, source_target_pairs={{0,6},{1,7},{2,0},{3,1},{4,2},{5,3},{6,4},{7,5},{8,14},{9,15},{10,... | collective-permute-start | bytes 294920 | tf_op jit(solution)/shard_map/ppermute | solution.py:301
  3.6 0.7 %collective-permute-start.1 = (f32[6,32,128]{2,1,0:T(8,128)S(1)}, f32[6,32,128]{2,1,0:T(8,128)S(1)}, u32[]{:S(2)}, u32[]{:S(2)}) collective-permute-start(f32[6,32,128]{2,1,0:T(8,128)S(1)} %bitcast.10), channel_id=1, source_target_pairs={{0,4},{1,5},{2,6},{3,7},{4,0},{5,1},{6,2},{7,3},{8,12},{9,13},{10,... | collective-permute-start | bytes 294920 | tf_op jit(solution)/shard_map/ppermute | solution.py:301
  4.3 1.8 %collective-permute-start = (f32[6,32,128]{2,1,0:T(8,128)S(1)}, f32[6,32,128]{2,1,0:T(8,128)S(1)}, u32[]{:S(2)}, u32[]{:S(2)}) collective-permute-start(f32[6,32,128]{2,1,0:T(8,128)S(1)} %bitcast.11), channel_id=1, source_target_pairs={{0,2},{1,3},{2,4},{3,5},{4,6},{5,7},{6,0},{7,1},{8,10},{9,11},{10,... | collective-permute-start | bytes 294920 | tf_op jit(solution)/shard_map/ppermute | solution.py:301
  6.1 0.1 pad_add_fusion.index_ref
  6.1 0.0 copy-done
  6.1 2.4 %select_waves.1 = bf16[32,64,128]{2,1,0:T(8,128)(2,1)} custom-call(s32[2]{0:T(128)S(1)} %pad_add_fusion.index_ref, s32[32,32]{1,0:T(8,128)S(1)} %copy-done.1, bf16[3,32,640]{2,1,0:T(8,128)(2,1)S(1)} %bitcast.7), custom_call_target="tpu_custom_call" | custom-call | flops 16000000 | bytes 620000 | tf_op jit(solution)/shard_map/select_waves/pallas_call | solution.py:228
  8.5 11.5 %all-to-all-start = ((bf16[32,64,128]{2,1,0:T(8,128)(2,1)}), bf16[32,64,128]{2,1,0:T(8,128)(2,1)S(1)}, u32[]{:S(2)}, u32[]{:S(2)}) async-start(bf16[32,64,128]{2,1,0:T(8,128)(2,1)} %select_waves.1), calls=%async_computation | async-start | bytes 1048576 | tf_op jit(solution)/shard_map/all_to_all | solution.py:307
  20.0 0.0 copy-start.2
  20.0 0.0 copy-start.3
  20.0 0.0 collective-permute-done.2
  20.0 0.0 collective-permute-done.1
  20.0 0.0 collective-permute-done
  20.1 0.1 collective-permute-start.3
  20.2 1.7 %collective-permute-done.3.far_ref = f32[24,32,128]{2,1,0:T(8,128)S(1)} collective-permute-done((f32[24,32,128]{2,1,0:T(8,128)S(1)}, f32[24,32,128]{2,1,0:T(8,128)S(1)}, u32[]{:S(2)}, u32[]{:S(2)}) %collective-permute-start.3) | collective-permute-done | bytes 393248 | tf_op jit(solution)/shard_map/ppermute | solution.py:303
  21.9 4.4 %record_scales.1 = (f32[48,32,128]{2,1,0:T(8,128)S(1)}, s32[137]{0:T(256)S(1)}) custom-call(s32[2]{0:T(128)S(1)} %pad_add_fusion.index_ref, s32[3,16]{1,0:T(4,128)S(1)} %copy-done.3, s32[32,32]{1,0:T(8,128)S(1)} %copy-done.1, s32[32,32]{1,0:T(8,128)S(1)} %copy-done.2, f32[24,32,128]{2,1,0:T(8,128)S(1)} %pad_maximum_fusion.near_ref, ...), custom_call_target="tpu_custom_call" | custom-call | flops 6000000000 | bytes 2000000 | tf_op jit(solution)/shard_map/record_scales/pallas_call | solution.py:242
  26.3 10.3 %all-to-all-done.waves_hbm = bf16[32,64,128]{2,1,0:T(8,128)(2,1)S(1)} async-done(((bf16[32,64,128]{2,1,0:T(8,128)(2,1)}), bf16[32,64,128]{2,1,0:T(8,128)(2,1)S(1)}, u32[]{:S(2)}, u32[]{:S(2)}) %all-to-all-start) | async-done | bytes 524320 | tf_op jit(solution)/shard_map/all_to_all | solution.py:307
  36.5 5.7 %stack_picks.1 = bf16[128,384]{1,0:T(8,128)(2,1)S(1)} custom-call(s32[137]{0:T(256)S(1)} %get-tuple-element.7.entries, s32[2]{0:T(128)S(1)} %pad_add_fusion.index_ref, f32[24,32,128]{2,1,0:T(8,128)S(1)} %pad_maximum_fusion.near_ref, f32[24,32,128]{2,1,0:T(8,128)S(1)} %collective-permute-done.3.far_ref, f32[48,32,128]{2,1,0:T(8,128)S(1)} %get-tuple-element.8.scales_hbm, ...), custom_call_target="tpu_custom_call" | custom-call | flops 200000000 | bytes 8000000 | tf_op jit(solution)/shard_map/stack_picks/pallas_call | solution.py:267
  42.3 15.1 %all_to_all.14 = bf16[32,4,384]{2,1,0:T(4,128)(2,1)S(1)} all-to-all(bf16[32,4,384]{2,1,0:T(4,128)(2,1)S(1)} %all_to_all.10), channel_id=1, replica_groups=mesh['sta'=32,'tpl'=8] {'sta'}, dimensions={0} | all-to-all | bytes 196608 | tf_op jit(solution)/shard_map/all_to_all | solution.py:311
  57.4 0.1 convert_reduce_fusion
  57.4 0.1 reshape.19
  57.5 0.7 %copy.8 = f32[48,32]{0,1:T(8,128)} copy(f32[48,32]{1,0:T(8,128)S(1)} %reshape.19) | data formatting | bytes 12288 | tf_op jit(solution)/shard_map/reshape | solution.py:313
  (7 shorter events, 0.1 us)
Async XLA Ops:
  1.2 5.0 %copy-start = (bf16[32,1,3,640]{3,0,2,1:T(8,128)(2,1)S(1)}, bf16[32,1,3,640]{3,0,2,1:T(8,128)(2,1)}, u32[]{:S(2)}) copy-start(bf16[32,1,3,640]{3,0,2,1:T(8,128)(2,1)} %param.7) | copy-start | bytes 368644
  1.2 4.9 %copy-start.1 = (s32[32,32]{1,0:T(8,128)S(1)}, s32[32,32]{1,0:T(8,128)}, u32[]{:S(2)}) copy-start(s32[32,32]{1,0:T(8,128)} %station_ref.3) | copy-start | bytes 12292
  1.2 18.8 %collective-permute-start.2 = (f32[6,32,128]{2,1,0:T(8,128)S(1)}, f32[6,32,128]{2,1,0:T(8,128)S(1)}, u32[]{:S(2)}, u32[]{:S(2)}) collective-permute-start(f32[6,32,128]{2,1,0:T(8,128)S(1)} %bitcast.9), channel_id=1, source_target_pairs={{0,6},{1,7},{2,0},{3,1},{4,2},{5,3},{6,4},{7,5},{8,14},{9,15},{10,... | collective-permute-start | bytes 294920 | tf_op jit(solution)/shard_map/ppermute | solution.py:301
  3.6 16.5 %collective-permute-start.1 = (f32[6,32,128]{2,1,0:T(8,128)S(1)}, f32[6,32,128]{2,1,0:T(8,128)S(1)}, u32[]{:S(2)}, u32[]{:S(2)}) collective-permute-start(f32[6,32,128]{2,1,0:T(8,128)S(1)} %bitcast.10), channel_id=1, source_target_pairs={{0,4},{1,5},{2,6},{3,7},{4,0},{5,1},{6,2},{7,3},{8,12},{9,13},{10,... | collective-permute-start | bytes 294920 | tf_op jit(solution)/shard_map/ppermute | solution.py:301
  4.3 15.8 %collective-permute-start = (f32[6,32,128]{2,1,0:T(8,128)S(1)}, f32[6,32,128]{2,1,0:T(8,128)S(1)}, u32[]{:S(2)}, u32[]{:S(2)}) collective-permute-start(f32[6,32,128]{2,1,0:T(8,128)S(1)} %bitcast.11), channel_id=1, source_target_pairs={{0,2},{1,3},{2,4},{3,5},{4,6},{5,7},{6,0},{7,1},{8,10},{9,11},{10,... | collective-permute-start | bytes 294920 | tf_op jit(solution)/shard_map/ppermute | solution.py:301
  8.5 28.0 %all-to-all-start = ((bf16[32,64,128]{2,1,0:T(8,128)(2,1)}), bf16[32,64,128]{2,1,0:T(8,128)(2,1)S(1)}, u32[]{:S(2)}, u32[]{:S(2)}) async-start(bf16[32,64,128]{2,1,0:T(8,128)(2,1)} %select_waves.1), calls=%async_computation | async-start | bytes 1048576 | tf_op jit(solution)/shard_map/all_to_all | solution.py:307
  20.0 1.9 %copy-start.2 = (s32[32,32]{1,0:T(8,128)S(1)}, s32[32,32]{1,0:T(8,128)}, u32[]{:S(2)}) copy-start(s32[32,32]{1,0:T(8,128)} %lag_ref.1) | copy-start | bytes 12292
  20.0 1.9 %copy-start.3 = (s32[3,16]{1,0:T(4,128)S(1)}, s32[3,16]{1,0:T(4,128)}, u32[]{:S(2)}) copy-start(s32[3,16]{1,0:T(4,128)} %mask_hbm.1) | copy-start | bytes 580
  20.1 1.8 %collective-permute-start.3 = (f32[24,32,128]{2,1,0:T(8,128)S(1)}, f32[24,32,128]{2,1,0:T(8,128)S(1)}, u32[]{:S(2)}, u32[]{:S(2)}) collective-permute-start(f32[24,32,128]{2,1,0:T(8,128)S(1)} %pad_maximum_fusion.near_ref), channel_id=1, source_target_pairs={{0,1},{1,0},{2,3},{3,2},{4,5},{5,4},{6,7},{7,6},{8,9},{9,8},{10,11... | collective-permute-start | bytes 1179656 | tf_op jit(solution)/shard_map/ppermute | solution.py:303

commit v9 on v8

--- a/solution.py
+++ b/solution.py
@@ -68,23 +68,23 @@
     place = jnp.sum(same.astype(jnp.int32), axis=0, keepdims=True)
     slot = across * CAP + place
     peers = out_ref.shape[0]
-    peer = lax.broadcasted_iota(jnp.int32, (peers, group_size), 0)
-    selects = [(peer * CAP + k == slot).astype(jnp.float32).astype(jnp.bfloat16) for k in range(CAP)]
-    select = jnp.concatenate(selects, axis=0)
+    line = lax.broadcasted_iota(jnp.int32, (2 * CAP * peers, group_size), 0)
+    wanted = (line >> 3) * CAP + (line & (CAP - 1)) == slot
+    selects = [wanted & ((line >> 2) & 1 == half) for half in range(2)]
+    select = jnp.concatenate([part.astype(jnp.float32) for part in selects], axis=1).astype(jnp.bfloat16)
+    pieces = []
     for c in range(3):
         values = waves_ref[c].astype(jnp.float32)
         centred = values - jnp.mean(values, axis=-1, keepdims=True)
         power = jnp.mean(centred * centred, axis=-1, keepdims=True)
         unit = (centred / jnp.sqrt(power + EPSILON)).astype(jnp.bfloat16)
-        picked = jnp.dot(select, unit, preferred_element_type=jnp.float32)
-        for tile in range(TILES):
-            columns = slice(tile * LANES, (tile + 1) * LANES)
-            for k in range(CAP):
-                at = (c * TILES + tile) * CAP + k
-                staged[pl.ds(at, peers, stride=SLOT_ROWS), :] = picked[k * peers:(k + 1) * peers, columns]
-    for at in range(3 * TILES * CAP, SLOT_ROWS):
-        staged[pl.ds(at, peers, stride=SLOT_ROWS), :] = jnp.zeros((peers, LANES), jnp.float32)
-    out_ref[...] = staged[...].astype(jnp.bfloat16).reshape(out_ref.shape)
+        pieces += [unit[:, tile * LANES:(tile + 1) * LANES] for tile in range(TILES)]
+    pieces.append(jnp.zeros((group_size, LANES), jnp.bfloat16))
+    for pair in range(len(pieces) // 2):
+        both = jnp.concatenate(pieces[2 * pair:2 * pair + 2], axis=0)
+        picked = jnp.dot(select, both, preferred_element_type=jnp.float32)
+        staged[:, 2 * CAP * pair:2 * CAP * (pair + 1), :] = picked.reshape(peers, 2 * CAP, LANES)
+    out_ref[...] = staged[...].astype(jnp.bfloat16)
 
 
 def owner_of(here, core, hop, hops):
@@ -138,33 +138,24 @@
     entries[total + UNROLL] = count
 
 
-def stack_kernel(entries, index_ref, near_ref, far_ref, scales_hbm, waves_hbm, out_ref,
-                 waves_ref, tiles, scales, frames, units, acc, twice, dense, sems):
+def stack_kernel(entries, index_ref, near_ref, far_ref, scales, waves_ref, out_ref,
+                 frames, units, acc, twice, dense):
     here = index_ref[1]
     hops = near_ref.shape[0] // RECORDS
-    row_copies = [pltpu.make_async_copy(row_ref, tiles.at[core], sems.at[core])
-                  for core, row_ref in enumerate((near_ref, far_ref))]
-    waves_copy = pltpu.make_async_copy(waves_hbm, waves_ref, sems.at[2])
-    scales_copy = pltpu.make_async_copy(scales_hbm, scales, sems.at[3])
-    for copy in row_copies + [waves_copy, scales_copy]:
-        copy.start()
     count = entries[entries.shape[0] - 1]
     acc[...] = jnp.zeros_like(acc)
-
-    for core, copy in enumerate(row_copies):
-        copy.wait()
+    units[...] = waves_ref[...].reshape(units.shape).astype(jnp.float32)
+
+    for core, tile_ref in enumerate((near_ref, far_ref)):
         for hop in range(hops):
             first = owner_of(here, core, hop, hops) * RECORDS
             at = RECORDS * hop
-            values = tiles[core, at:at + RECORDS].reshape(RECORDS * STEP, LANES).astype(jnp.bfloat16)
+            values = tile_ref[at:at + RECORDS].reshape(RECORDS * STEP, LANES).astype(jnp.bfloat16)
             for turn in range(TURNS):
                 rolled = values if turn == 0 else pltpu.roll(values, LANES - turn, 1)
                 frames[pl.ds(first, RECORDS), turn * STEP:(turn + 1) * STEP, :] = (
                     rolled.reshape(RECORDS, STEP, LANES)
                 )
-    waves_copy.wait()
-    units[...] = waves_ref[...].reshape(units.shape).astype(jnp.float32)
-    scales_copy.wait()
     row = lax.broadcasted_iota(jnp.int32, (STEP, LANES), 0)
     lane = lax.broadcasted_iota(jnp.int32, (STEP, LANES), 1)
     own = lane >= row
@@ -220,7 +211,6 @@
 
 SMEM = pl.BlockSpec(memory_space=pltpu.SMEM)
 VMEM = pl.BlockSpec(memory_space=pltpu.VMEM)
-ANY = pl.BlockSpec(memory_space=pl.ANY)
 HBM = pl.BlockSpec(memory_space=pltpu.HBM)
 
 
@@ -230,7 +220,7 @@
         out_shape=jax.ShapeDtypeStruct((peers, SLOT_ROWS, LANES), jnp.bfloat16),
         in_specs=[SMEM, VMEM, VMEM],
         out_specs=VMEM,
-        scratch_shapes=[pltpu.VMEM((peers * SLOT_ROWS, LANES), jnp.float32)],
+        scratch_shapes=[pltpu.VMEM((peers, SLOT_ROWS, LANES), jnp.float32)],
         compiler_params=pltpu.CompilerParams(vmem_limit_bytes=4 * 1024 * 1024),
         cost_estimate=pl.CostEstimate(flops=16_000_000, transcendentals=100, bytes_accessed=620_000),
         name="select_waves",
@@ -267,18 +257,14 @@
     return pl.pallas_call(
         stack_kernel,
         out_shape=jax.ShapeDtypeStruct((slot_count, lines * LANES // slot_count), jnp.bfloat16),
-        in_specs=[SMEM, SMEM, ANY, ANY, ANY, ANY],
+        in_specs=[SMEM, SMEM, VMEM, VMEM, VMEM, VMEM],
         out_specs=VMEM,
         scratch_shapes=[
-            pltpu.VMEM(received.shape, jnp.bfloat16),
-            pltpu.VMEM((2,) + rows[0].shape, jnp.float32),
-            pltpu.VMEM(scales.shape, jnp.float32),
             pltpu.VMEM((records, TURNS * STEP, LANES), jnp.bfloat16),
             pltpu.VMEM((peers * SLOT_ROWS, LANES), jnp.float32),
             pltpu.VMEM(((group_size + 1) * STEP, LANES), jnp.float32),
             pltpu.VMEM((UNROLL, 2 * STEP, LANES), jnp.float32),
             pltpu.VMEM((lines, LANES), jnp.float32),
-            pltpu.SemaphoreType.DMA((4,)),
         ],
         compiler_params=pltpu.CompilerParams(vmem_limit_bytes=16 * 1024 * 1024),
         cost_estimate=pl.CostEstimate(flops=200_000_000, transcendentals=0, bytes_accessed=8_000_000),

time: 58.5 us -> 57.3 us (0.979)
  Pallas kernels: 12.4 us -> 11.3 us
    pallas_call x1, Pallas kernels: 5.67 us -> 5.05 us  [partial_stack(): pl.pallas_call(stack_kernel, out_shape=jax.ShapeDtypeStruct((slot_count,...]
  transfers between devices with their start and end apart: 5 -> 5, of which waited for: 2 -> 2; matrix products, arithmetic and copies ran while one was open for 0% -> 0% of each run, Pallas kernels for 12% -> 11%
where the time goes in v9:
time: 57.3 us; the launch traced here: 57.1 us
  starting transfers between devices  16.4 us (29%)
  blocking collectives  15.1 us (26%)
  waiting for transfers between devices  12 us (21%)
  Pallas kernels  11.3 us (20%)
  local copies, waits for them, and re-layouts  2.01 us (4%)
    all_to_all x1, blocking collectives, body(): lax.all_to_all(partial_sums, 'sta', split_axis=0, concat_axis=0, tiled=True)  15.1 us
    all_to_all x1, starting transfers between devices, body(): lax.all_to_all(outgoing, 'sta', split_axis=0, concat_axis=0, tiled=True)  11.5 us
    all_to_all x1, waiting for transfers between devices, body(): lax.all_to_all(outgoing, 'sta', split_axis=0, concat_axis=0, tiled=True)  10.3 us
    pallas_call x1, Pallas kernels, partial_stack(): pl.pallas_call(stack_kernel, out_shape=jax.ShapeDtypeStruct((slot_count,...  5.05 us
    ppermute x3, starting transfers between devices, body(): lax.ppermute(own, 'tpl', [(i, (i + hop) % tpl_size) for i in range(tpl_si...  4.83 us
    pallas_call x1, Pallas kernels, scales_and_entries(): pl.pallas_call(scales_kernel, out_shape=(jax.ShapeDtypeStruct((2 * rows[0...  4.36 us
    pallas_call x1, Pallas kernels, slot_waves(): pl.pallas_call(select_kernel, out_shape=jax.ShapeDtypeStruct((peers, SLOT...  1.84 us
    ppermute x1, waiting for transfers between devices, body(): lax.ppermute(near, 'tpl', [(i, i ^ 1) for i in range(tpl_size)])  1.71 us
  transfers between devices with their start and end apart: 5, of which 2 were waited for; matrix products, arithmetic and copies ran while one was open for 0% of the time, Pallas kernels for 11%

profile of v9, /device:TPU:2, one launch (start us, length us, event | category | flops | bytes accessed | tf_op | source)
XLA Modules:
  0.0 57.1 jit_solution(9200971547967011827)
XLA Ops:
  0.0 1.0 %reshape.16 = f32[3,2,100,32]{3,2,1,0:T(8,128)S(1)} reshape(f32[3,2,3200]{2,1,0:T(2,128)} %param.5) | data formatting | bytes 153600 | tf_op jit(solution)/shard_map/reshape | solution.py:282
  1.1 0.1 copy.9
  1.2 0.0 copy-start.1
  1.2 2.3 %collective-permute-start.2 = (f32[6,32,128]{2,1,0:T(8,128)S(1)}, f32[6,32,128]{2,1,0:T(8,128)S(1)}, u32[]{:S(2)}, u32[]{:S(2)}) collective-permute-start(f32[6,32,128]{2,1,0:T(8,128)S(1)} %bitcast.9), channel_id=1, source_target_pairs={{0,6},{1,7},{2,0},{3,1},{4,2},{5,3},{6,4},{7,5},{8,14},{9,15},{10,... | collective-permute-start | bytes 294920 | tf_op jit(solution)/shard_map/ppermute | solution.py:287
  3.6 0.7 %collective-permute-start.1 = (f32[6,32,128]{2,1,0:T(8,128)S(1)}, f32[6,32,128]{2,1,0:T(8,128)S(1)}, u32[]{:S(2)}, u32[]{:S(2)}) collective-permute-start(f32[6,32,128]{2,1,0:T(8,128)S(1)} %bitcast.10), channel_id=1, source_target_pairs={{0,4},{1,5},{2,6},{3,7},{4,0},{5,1},{6,2},{7,3},{8,12},{9,13},{10,... | collective-permute-start | bytes 294920 | tf_op jit(solution)/shard_map/ppermute | solution.py:287
  4.3 1.8 %collective-permute-start = (f32[6,32,128]{2,1,0:T(8,128)S(1)}, f32[6,32,128]{2,1,0:T(8,128)S(1)}, u32[]{:S(2)}, u32[]{:S(2)}) collective-permute-start(f32[6,32,128]{2,1,0:T(8,128)S(1)} %bitcast.11), channel_id=1, source_target_pairs={{0,2},{1,3},{2,4},{3,5},{4,6},{5,7},{6,0},{7,1},{8,10},{9,11},{10,... | collective-permute-start | bytes 294920 | tf_op jit(solution)/shard_map/ppermute | solution.py:287
  6.1 0.1 pad_add_fusion.index_ref
  6.1 0.0 copy-done
  6.1 1.8 %select_waves.1 = bf16[32,64,128]{2,1,0:T(8,128)(2,1)} custom-call(s32[2]{0:T(128)S(1)} %pad_add_fusion.index_ref, s32[32,32]{1,0:T(8,128)S(1)} %copy-done.1, bf16[3,32,640]{2,1,0:T(8,128)(2,1)S(1)} %bitcast.7), custom_call_target="tpu_custom_call" | custom-call | flops 16000000 | bytes 620000 | tf_op jit(solution)/shard_map/select_waves/pallas_call | solution.py:218
  8.0 11.5 %all-to-all-start = ((bf16[32,64,128]{2,1,0:T(8,128)(2,1)}), bf16[32,64,128]{2,1,0:T(8,128)(2,1)S(1)}, u32[]{:S(2)}, u32[]{:S(2)}) async-start(bf16[32,64,128]{2,1,0:T(8,128)(2,1)} %select_waves.1), calls=%async_computation | async-start | bytes 1048576 | tf_op jit(solution)/shard_map/all_to_all | solution.py:293
  19.5 0.0 copy-start.2
  19.5 0.0 copy-start.3
  19.5 0.0 collective-permute-done.2
  19.5 0.0 collective-permute-done.1
  19.5 0.0 collective-permute-done
  19.6 0.1 collective-permute-start.3
  19.7 1.7 %collective-permute-done.3.far_ref = f32[24,32,128]{2,1,0:T(8,128)S(1)} collective-permute-done((f32[24,32,128]{2,1,0:T(8,128)S(1)}, f32[24,32,128]{2,1,0:T(8,128)S(1)}, u32[]{:S(2)}, u32[]{:S(2)}) %collective-permute-start.3) | collective-permute-done | bytes 393248 | tf_op jit(solution)/shard_map/ppermute | solution.py:289
  21.4 4.4 %record_scales.1 = (f32[48,32,128]{2,1,0:T(8,128)S(1)}, s32[137]{0:T(256)S(1)}) custom-call(s32[2]{0:T(128)S(1)} %pad_add_fusion.index_ref, s32[3,16]{1,0:T(4,128)S(1)} %copy-done.3, s32[32,32]{1,0:T(8,128)S(1)} %copy-done.1, s32[32,32]{1,0:T(8,128)S(1)} %copy-done.2, f32[24,32,128]{2,1,0:T(8,128)S(1)} %pad_maximum_fusion.near_ref, ...), custom_call_target="tpu_custom_call" | custom-call | flops 6000000000 | bytes 2000000 | tf_op jit(solution)/shard_map/record_scales/pallas_call | solution.py:232
  25.8 10.3 %all-to-all-done.waves_ref = bf16[32,64,128]{2,1,0:T(8,128)(2,1)S(1)} async-done(((bf16[32,64,128]{2,1,0:T(8,128)(2,1)}), bf16[32,64,128]{2,1,0:T(8,128)(2,1)S(1)}, u32[]{:S(2)}, u32[]{:S(2)}) %all-to-all-start) | async-done | bytes 524320 | tf_op jit(solution)/shard_map/all_to_all | solution.py:293
  36.0 5.1 %stack_picks.1 = bf16[128,384]{1,0:T(8,128)(2,1)S(1)} custom-call(s32[137]{0:T(256)S(1)} %get-tuple-element.7.entries, s32[2]{0:T(128)S(1)} %pad_add_fusion.index_ref, f32[24,32,128]{2,1,0:T(8,128)S(1)} %pad_maximum_fusion.near_ref, f32[24,32,128]{2,1,0:T(8,128)S(1)} %collective-permute-done.3.far_ref, f32[48,32,128]{2,1,0:T(8,128)S(1)} %get-tuple-element.8.scales, ...), custom_call_target="tpu_custom_call" | custom-call | flops 200000000 | bytes 8000000 | tf_op jit(solution)/shard_map/stack_picks/pallas_call | solution.py:257
  41.1 15.1 %all_to_all.14 = bf16[32,4,384]{2,1,0:T(4,128)(2,1)S(1)} all-to-all(bf16[32,4,384]{2,1,0:T(4,128)(2,1)S(1)} %all_to_all.10), channel_id=1, replica_groups=mesh['sta'=32,'tpl'=8] {'sta'}, dimensions={0} | all-to-all | bytes 196608 | tf_op jit(solution)/shard_map/all_to_all | solution.py:297
  56.2 0.1 convert_reduce_fusion
  56.3 0.1 reshape.19
  56.4 0.7 %copy.8 = f32[48,32]{0,1:T(8,128)} copy(f32[48,32]{1,0:T(8,128)S(1)} %reshape.19) | data formatting | bytes 12288 | tf_op jit(solution)/shard_map/reshape | solution.py:299
  (7 shorter events, 0.1 us)
Async XLA Ops:
  1.2 5.0 %copy-start = (bf16[32,1,3,640]{3,0,2,1:T(8,128)(2,1)S(1)}, bf16[32,1,3,640]{3,0,2,1:T(8,128)(2,1)}, u32[]{:S(2)}) copy-start(bf16[32,1,3,640]{3,0,2,1:T(8,128)(2,1)} %param.7) | copy-start | bytes 368644
  1.2 4.9 %copy-start.1 = (s32[32,32]{1,0:T(8,128)S(1)}, s32[32,32]{1,0:T(8,128)}, u32[]{:S(2)}) copy-start(s32[32,32]{1,0:T(8,128)} %station_ref.3) | copy-start | bytes 12292
  1.2 18.3 %collective-permute-start.2 = (f32[6,32,128]{2,1,0:T(8,128)S(1)}, f32[6,32,128]{2,1,0:T(8,128)S(1)}, u32[]{:S(2)}, u32[]{:S(2)}) collective-permute-start(f32[6,32,128]{2,1,0:T(8,128)S(1)} %bitcast.9), channel_id=1, source_target_pairs={{0,6},{1,7},{2,0},{3,1},{4,2},{5,3},{6,4},{7,5},{8,14},{9,15},{10,... | collective-permute-start | bytes 294920 | tf_op jit(solution)/shard_map/ppermute | solution.py:287
  3.6 15.9 %collective-permute-start.1 = (f32[6,32,128]{2,1,0:T(8,128)S(1)}, f32[6,32,128]{2,1,0:T(8,128)S(1)}, u32[]{:S(2)}, u32[]{:S(2)}) collective-permute-start(f32[6,32,128]{2,1,0:T(8,128)S(1)} %bitcast.10), channel_id=1, source_target_pairs={{0,4},{1,5},{2,6},{3,7},{4,0},{5,1},{6,2},{7,3},{8,12},{9,13},{10,... | collective-permute-start | bytes 294920 | tf_op jit(solution)/shard_map/ppermute | solution.py:287
  4.3 15.3 %collective-permute-start = (f32[6,32,128]{2,1,0:T(8,128)S(1)}, f32[6,32,128]{2,1,0:T(8,128)S(1)}, u32[]{:S(2)}, u32[]{:S(2)}) collective-permute-start(f32[6,32,128]{2,1,0:T(8,128)S(1)} %bitcast.11), channel_id=1, source_target_pairs={{0,2},{1,3},{2,4},{3,5},{4,6},{5,7},{6,0},{7,1},{8,10},{9,11},{10,... | collective-permute-start | bytes 294920 | tf_op jit(solution)/shard_map/ppermute | solution.py:287
  8.0 28.0 %all-to-all-start = ((bf16[32,64,128]{2,1,0:T(8,128)(2,1)}), bf16[32,64,128]{2,1,0:T(8,128)(2,1)S(1)}, u32[]{:S(2)}, u32[]{:S(2)}) async-start(bf16[32,64,128]{2,1,0:T(8,128)(2,1)} %select_waves.1), calls=%async_computation | async-start | bytes 1048576 | tf_op jit(solution)/shard_map/all_to_all | solution.py:293
  19.5 1.9 %copy-start.2 = (s32[32,32]{1,0:T(8,128)S(1)}, s32[32,32]{1,0:T(8,128)}, u32[]{:S(2)}) copy-start(s32[32,32]{1,0:T(8,128)} %lag_ref.1) | copy-start | bytes 12292
  19.5 1.9 %copy-start.3 = (s32[3,16]{1,0:T(4,128)S(1)}, s32[3,16]{1,0:T(4,128)}, u32[]{:S(2)}) copy-start(s32[3,16]{1,0:T(4,128)} %mask_hbm.1) | copy-start | bytes 580
  19.6 1.8 %collective-permute-start.3 = (f32[24,32,128]{2,1,0:T(8,128)S(1)}, f32[24,32,128]{2,1,0:T(8,128)S(1)}, u32[]{:S(2)}, u32[]{:S(2)}) collective-permute-start(f32[24,32,128]{2,1,0:T(8,128)S(1)} %pad_maximum_fusion.near_ref), channel_id=1, source_target_pairs={{0,1},{1,0},{2,3},{3,2},{4,5},{5,4},{6,7},{7,6},{8,9},{9,8},{10,11... | collective-permute-start | bytes 1179656 | tf_op jit(solution)/shard_map/ppermute | solution.py:289

commit v10 on v9

--- a/solution.py
+++ b/solution.py
@@ -16,7 +16,7 @@
 OUT_BLOCKS = NT // STEP
 TILES = L // LANES
 TURNS = 8
-UNROLL = 8
+UNROLL = 16
 SLOT_ROWS = 64
 RECORDS = 6
 STATION_BITS = 4

time: 57.3 us -> 61.8 us (1.079)
  Pallas kernels: 11.3 us -> 15.8 us
    pallas_call x1, Pallas kernels: 5.05 us -> 9.55 us  [partial_stack(): pl.pallas_call(stack_kernel, out_shape=jax.ShapeDtypeStruct((slot_count,...]
  transfers between devices with their start and end apart: 5 -> 5, of which waited for: 2 -> 2; matrix products, arithmetic and copies ran while one was open for 0% -> 0% of each run, Pallas kernels for 11% -> 10%
where the time goes in v10:
time: 61.8 us; the launch traced here: 61.5 us
  starting transfers between devices  16.4 us (27%)
  Pallas kernels  15.8 us (26%)
  blocking collectives  15.1 us (24%)
  waiting for transfers between devices  12 us (19%)
  local copies, waits for them, and re-layouts  2.01 us (3%)
    all_to_all x1, blocking collectives, body(): lax.all_to_all(partial_sums, 'sta', split_axis=0, concat_axis=0, tiled=True)  15.1 us
    all_to_all x1, starting transfers between devices, body(): lax.all_to_all(outgoing, 'sta', split_axis=0, concat_axis=0, tiled=True)  11.5 us
    all_to_all x1, waiting for transfers between devices, body(): lax.all_to_all(outgoing, 'sta', split_axis=0, concat_axis=0, tiled=True)  10.3 us
    pallas_call x1, Pallas kernels, partial_stack(): pl.pallas_call(stack_kernel, out_shape=jax.ShapeDtypeStruct((slot_count,...  9.55 us
    ppermute x3, starting transfers between devices, body(): lax.ppermute(own, 'tpl', [(i, (i + hop) % tpl_size) for i in range(tpl_si...  4.83 us
    pallas_call x1, Pallas kernels, scales_and_entries(): pl.pallas_call(scales_kernel, out_shape=(jax.ShapeDtypeStruct((2 * rows[0...  4.37 us
    pallas_call x1, Pallas kernels, slot_waves(): pl.pallas_call(select_kernel, out_shape=jax.ShapeDtypeStruct((peers, SLOT...  1.84 us
    ppermute x1, waiting for transfers between devices, body(): lax.ppermute(near, 'tpl', [(i, i ^ 1) for i in range(tpl_size)])  1.71 us
  transfers between devices with their start and end apart: 5, of which 2 were waited for; matrix products, arithmetic and copies ran while one was open for 0% of the time, Pallas kernels for 10%

profile of v10, /device:TPU:2, one launch (start us, length us, event | category | flops | bytes accessed | tf_op | source)
XLA Modules:
  0.0 61.5 jit_solution(11226841056886864037)
XLA Ops:
  0.0 1.0 %reshape.16 = f32[3,2,100,32]{3,2,1,0:T(8,128)S(1)} reshape(f32[3,2,3200]{2,1,0:T(2,128)} %param.5) | data formatting | bytes 153600 | tf_op jit(solution)/shard_map/reshape | solution.py:282
  1.1 0.1 copy.9
  1.2 0.0 copy-start.1
  1.2 2.3 %collective-permute-start.2 = (f32[6,32,128]{2,1,0:T(8,128)S(1)}, f32[6,32,128]{2,1,0:T(8,128)S(1)}, u32[]{:S(2)}, u32[]{:S(2)}) collective-permute-start(f32[6,32,128]{2,1,0:T(8,128)S(1)} %bitcast.9), channel_id=1, source_target_pairs={{0,6},{1,7},{2,0},{3,1},{4,2},{5,3},{6,4},{7,5},{8,14},{9,15},{10,... | collective-permute-start | bytes 294920 | tf_op jit(solution)/shard_map/ppermute | solution.py:287
  3.6 0.7 %collective-permute-start.1 = (f32[6,32,128]{2,1,0:T(8,128)S(1)}, f32[6,32,128]{2,1,0:T(8,128)S(1)}, u32[]{:S(2)}, u32[]{:S(2)}) collective-permute-start(f32[6,32,128]{2,1,0:T(8,128)S(1)} %bitcast.10), channel_id=1, source_target_pairs={{0,4},{1,5},{2,6},{3,7},{4,0},{5,1},{6,2},{7,3},{8,12},{9,13},{10,... | collective-permute-start | bytes 294920 | tf_op jit(solution)/shard_map/ppermute | solution.py:287
  4.3 1.8 %collective-permute-start = (f32[6,32,128]{2,1,0:T(8,128)S(1)}, f32[6,32,128]{2,1,0:T(8,128)S(1)}, u32[]{:S(2)}, u32[]{:S(2)}) collective-permute-start(f32[6,32,128]{2,1,0:T(8,128)S(1)} %bitcast.11), channel_id=1, source_target_pairs={{0,2},{1,3},{2,4},{3,5},{4,6},{5,7},{6,0},{7,1},{8,10},{9,11},{10,... | collective-permute-start | bytes 294920 | tf_op jit(solution)/shard_map/ppermute | solution.py:287
  6.1 0.1 pad_add_fusion.index_ref
  6.1 0.0 copy-done
  6.1 1.8 %select_waves.1 = bf16[32,64,128]{2,1,0:T(8,128)(2,1)} custom-call(s32[2]{0:T(128)S(1)} %pad_add_fusion.index_ref, s32[32,32]{1,0:T(8,128)S(1)} %copy-done.1, bf16[3,32,640]{2,1,0:T(8,128)(2,1)S(1)} %bitcast.7), custom_call_target="tpu_custom_call" | custom-call | flops 16000000 | bytes 620000 | tf_op jit(solution)/shard_map/select_waves/pallas_call | solution.py:218
  8.0 11.5 %all-to-all-start = ((bf16[32,64,128]{2,1,0:T(8,128)(2,1)}), bf16[32,64,128]{2,1,0:T(8,128)(2,1)S(1)}, u32[]{:S(2)}, u32[]{:S(2)}) async-start(bf16[32,64,128]{2,1,0:T(8,128)(2,1)} %select_waves.1), calls=%async_computation | async-start | bytes 1048576 | tf_op jit(solution)/shard_map/all_to_all | solution.py:293
  19.5 0.0 copy-start.2
  19.5 0.0 copy-start.3
  19.5 0.0 collective-permute-done.2
  19.5 0.0 collective-permute-done.1
  19.5 0.0 collective-permute-done
  19.6 0.1 collective-permute-start.3
  19.7 1.7 %collective-permute-done.3.far_ref = f32[24,32,128]{2,1,0:T(8,128)S(1)} collective-permute-done((f32[24,32,128]{2,1,0:T(8,128)S(1)}, f32[24,32,128]{2,1,0:T(8,128)S(1)}, u32[]{:S(2)}, u32[]{:S(2)}) %collective-permute-start.3) | collective-permute-done | bytes 393248 | tf_op jit(solution)/shard_map/ppermute | solution.py:289
  21.4 4.4 %record_scales.1 = (f32[48,32,128]{2,1,0:T(8,128)S(1)}, s32[145]{0:T(256)S(1)}) custom-call(s32[2]{0:T(128)S(1)} %pad_add_fusion.index_ref, s32[3,16]{1,0:T(4,128)S(1)} %copy-done.3, s32[32,32]{1,0:T(8,128)S(1)} %copy-done.1, s32[32,32]{1,0:T(8,128)S(1)} %copy-done.2, f32[24,32,128]{2,1,0:T(8,128)S(1)} %pad_maximum_fusion.near_ref, ...), custom_call_target="tpu_custom_call" | custom-call | flops 6000000000 | bytes 2000000 | tf_op jit(solution)/shard_map/record_scales/pallas_call | solution.py:232
  25.8 10.3 %all-to-all-done.waves_ref = bf16[32,64,128]{2,1,0:T(8,128)(2,1)S(1)} async-done(((bf16[32,64,128]{2,1,0:T(8,128)(2,1)}), bf16[32,64,128]{2,1,0:T(8,128)(2,1)S(1)}, u32[]{:S(2)}, u32[]{:S(2)}) %all-to-all-start) | async-done | bytes 524320 | tf_op jit(solution)/shard_map/all_to_all | solution.py:293
  36.0 9.5 %stack_picks.1 = bf16[128,384]{1,0:T(8,128)(2,1)S(1)} custom-call(s32[145]{0:T(256)S(1)} %get-tuple-element.7.entries, s32[2]{0:T(128)S(1)} %pad_add_fusion.index_ref, f32[24,32,128]{2,1,0:T(8,128)S(1)} %pad_maximum_fusion.near_ref, f32[24,32,128]{2,1,0:T(8,128)S(1)} %collective-permute-done.3.far_ref, f32[48,32,128]{2,1,0:T(8,128)S(1)} %get-tuple-element.8.scales, ...), custom_call_target="tpu_custom_call" | custom-call | flops 200000000 | bytes 8000000 | tf_op jit(solution)/shard_map/stack_picks/pallas_call | solution.py:257
  45.6 15.1 %all_to_all.14 = bf16[32,4,384]{2,1,0:T(4,128)(2,1)S(1)} all-to-all(bf16[32,4,384]{2,1,0:T(4,128)(2,1)S(1)} %all_to_all.10), channel_id=1, replica_groups=mesh['sta'=32,'tpl'=8] {'sta'}, dimensions={0} | all-to-all | bytes 196608 | tf_op jit(solution)/shard_map/all_to_all | solution.py:297
  60.7 0.1 convert_reduce_fusion
  60.8 0.1 reshape.19
  60.8 0.7 %copy.8 = f32[48,32]{0,1:T(8,128)} copy(f32[48,32]{1,0:T(8,128)S(1)} %reshape.19) | data formatting | bytes 12288 | tf_op jit(solution)/shard_map/reshape | solution.py:299
  (7 shorter events, 0.1 us)
Async XLA Ops:
  1.2 5.0 %copy-start = (bf16[32,1,3,640]{3,0,2,1:T(8,128)(2,1)S(1)}, bf16[32,1,3,640]{3,0,2,1:T(8,128)(2,1)}, u32[]{:S(2)}) copy-start(bf16[32,1,3,640]{3,0,2,1:T(8,128)(2,1)} %param.7) | copy-start | bytes 368644
  1.2 4.9 %copy-start.1 = (s32[32,32]{1,0:T(8,128)S(1)}, s32[32,32]{1,0:T(8,128)}, u32[]{:S(2)}) copy-start(s32[32,32]{1,0:T(8,128)} %station_ref.3) | copy-start | bytes 12292
  1.2 18.3 %collective-permute-start.2 = (f32[6,32,128]{2,1,0:T(8,128)S(1)}, f32[6,32,128]{2,1,0:T(8,128)S(1)}, u32[]{:S(2)}, u32[]{:S(2)}) collective-permute-start(f32[6,32,128]{2,1,0:T(8,128)S(1)} %bitcast.9), channel_id=1, source_target_pairs={{0,6},{1,7},{2,0},{3,1},{4,2},{5,3},{6,4},{7,5},{8,14},{9,15},{10,... | collective-permute-start | bytes 294920 | tf_op jit(solution)/shard_map/ppermute | solution.py:287
  3.6 15.9 %collective-permute-start.1 = (f32[6,32,128]{2,1,0:T(8,128)S(1)}, f32[6,32,128]{2,1,0:T(8,128)S(1)}, u32[]{:S(2)}, u32[]{:S(2)}) collective-permute-start(f32[6,32,128]{2,1,0:T(8,128)S(1)} %bitcast.10), channel_id=1, source_target_pairs={{0,4},{1,5},{2,6},{3,7},{4,0},{5,1},{6,2},{7,3},{8,12},{9,13},{10,... | collective-permute-start | bytes 294920 | tf_op jit(solution)/shard_map/ppermute | solution.py:287
  4.3 15.3 %collective-permute-start = (f32[6,32,128]{2,1,0:T(8,128)S(1)}, f32[6,32,128]{2,1,0:T(8,128)S(1)}, u32[]{:S(2)}, u32[]{:S(2)}) collective-permute-start(f32[6,32,128]{2,1,0:T(8,128)S(1)} %bitcast.11), channel_id=1, source_target_pairs={{0,2},{1,3},{2,4},{3,5},{4,6},{5,7},{6,0},{7,1},{8,10},{9,11},{10,... | collective-permute-start | bytes 294920 | tf_op jit(solution)/shard_map/ppermute | solution.py:287
  8.0 28.0 %all-to-all-start = ((bf16[32,64,128]{2,1,0:T(8,128)(2,1)}), bf16[32,64,128]{2,1,0:T(8,128)(2,1)S(1)}, u32[]{:S(2)}, u32[]{:S(2)}) async-start(bf16[32,64,128]{2,1,0:T(8,128)(2,1)} %select_waves.1), calls=%async_computation | async-start | bytes 1048576 | tf_op jit(solution)/shard_map/all_to_all | solution.py:293
  19.5 1.9 %copy-start.2 = (s32[32,32]{1,0:T(8,128)S(1)}, s32[32,32]{1,0:T(8,128)}, u32[]{:S(2)}) copy-start(s32[32,32]{1,0:T(8,128)} %lag_ref.1) | copy-start | bytes 12292
  19.5 1.9 %copy-start.3 = (s32[3,16]{1,0:T(4,128)S(1)}, s32[3,16]{1,0:T(4,128)}, u32[]{:S(2)}) copy-start(s32[3,16]{1,0:T(4,128)} %mask_hbm.1) | copy-start | bytes 580
  19.6 1.8 %collective-permute-start.3 = (f32[24,32,128]{2,1,0:T(8,128)S(1)}, f32[24,32,128]{2,1,0:T(8,128)S(1)}, u32[]{:S(2)}, u32[]{:S(2)}) collective-permute-start(f32[24,32,128]{2,1,0:T(8,128)S(1)} %pad_maximum_fusion.near_ref), channel_id=1, source_target_pairs={{0,1},{1,0},{2,3},{3,2},{4,5},{5,4},{6,7},{7,6},{8,9},{9,8},{10,11... | collective-permute-start | bytes 1179656 | tf_op jit(solution)/shard_map/ppermute | solution.py:289

commit v11 on v9

--- a/solution.py
+++ b/solution.py
@@ -16,6 +16,7 @@
 OUT_BLOCKS = NT // STEP
 TILES = L // LANES
 TURNS = 8
+EARLY = 5
 UNROLL = 8
 SLOT_ROWS = 64
 RECORDS = 6
@@ -91,7 +92,7 @@
     return ((here - 2 * hop) & (2 * hops - 1)) ^ core
 
 
-def scales_kernel(index_ref, mask_hbm, station_ref, lag_ref, near_ref, far_ref, scales, entries,
+def scales_kernel(index_ref, mask_hbm, station_ref, lag_ref, near_ref, far_ref, scales, early, entries,
                   meta_vmem, meta, mask_ref, sems):
     mask_copy = pltpu.make_async_copy(mask_hbm, mask_ref, sems.at[0])
     mask_copy.start()
@@ -116,13 +117,18 @@
     for core, tile_ref in enumerate((near_ref, far_ref)):
         for hop in range(hops):
             owner = owner_of(here, core, hop, hops)
+            first = owner * RECORDS
             values = tile_ref[hop * RECORDS:(hop + 1) * RECORDS].reshape(RECORDS * STEP, LANES)
+            rounded = values.astype(jnp.bfloat16)
+            for turn in range(EARLY):
+                rolled = rounded if turn == 0 else pltpu.roll(rounded, LANES - turn, 1)
+                early[pl.ds(first, RECORDS), turn * STEP:(turn + 1) * STEP, :] = rolled.reshape(RECORDS, STEP, LANES)
             mean_one = window_sums(values) * (1.0 / L)
             mean_two = window_sums(values * values) * (1.0 / L)
             factor = lax.rsqrt(mean_two - mean_one * mean_one + EPSILON)
             for record in range(RECORDS):
                 weight = mask_ref[record >> 1, owner * 2 + (record & 1)].astype(jnp.float32) * (1.0 / L)
-                scales[owner * RECORDS + record] = factor[record] * weight
+                scales[first + record] = factor[record] * weight
 
     meta_copy.wait()
 
@@ -138,24 +144,16 @@
     entries[total + UNROLL] = count
 
 
-def stack_kernel(entries, index_ref, near_ref, far_ref, scales, waves_ref, out_ref,
-                 frames, units, acc, twice, dense):
-    here = index_ref[1]
-    hops = near_ref.shape[0] // RECORDS
+def stack_kernel(entries, early, scales, waves_ref, out_ref, late, units, acc, twice, dense):
     count = entries[entries.shape[0] - 1]
     acc[...] = jnp.zeros_like(acc)
     units[...] = waves_ref[...].reshape(units.shape).astype(jnp.float32)
 
-    for core, tile_ref in enumerate((near_ref, far_ref)):
-        for hop in range(hops):
-            first = owner_of(here, core, hop, hops) * RECORDS
-            at = RECORDS * hop
-            values = tile_ref[at:at + RECORDS].reshape(RECORDS * STEP, LANES).astype(jnp.bfloat16)
-            for turn in range(TURNS):
-                rolled = values if turn == 0 else pltpu.roll(values, LANES - turn, 1)
-                frames[pl.ds(first, RECORDS), turn * STEP:(turn + 1) * STEP, :] = (
-                    rolled.reshape(RECORDS, STEP, LANES)
-                )
+    for first in range(0, early.shape[0], RECORDS):
+        values = early[first:first + RECORDS, :STEP, :].reshape(RECORDS * STEP, LANES)
+        for turn in range(EARLY, TURNS):
+            rolled = pltpu.roll(values, LANES - turn, 1).reshape(RECORDS, STEP, LANES)
+            late[first:first + RECORDS, (turn - EARLY) * STEP:(turn - EARLY + 1) * STEP, :] = rolled
     row = lax.broadcasted_iota(jnp.int32, (STEP, LANES), 0)
     lane = lax.broadcasted_iota(jnp.int32, (STEP, LANES), 1)
     own = lane >= row
@@ -182,7 +180,8 @@
             left = jnp.concatenate(
                 [jnp.concatenate(columns[i:i + 2], axis=1) for i in range(0, TILES + 1, 2)], axis=0
             )
-            product = jnp.dot(left, frames[record], preferred_element_type=jnp.float32)
+            frames = jnp.concatenate([early[record], late[record]], axis=0)
+            product = jnp.dot(left, frames, preferred_element_type=jnp.float32)
             summed = product[:STEP]
             for part in range(1, (TILES + 1) // 2):
                 later = product[part * STEP:(part + 1) * STEP]
@@ -233,10 +232,11 @@
         scales_kernel,
         out_shape=(
             jax.ShapeDtypeStruct((2 * rows[0].shape[0], STEP, LANES), jnp.float32),
+            jax.ShapeDtypeStruct((2 * rows[0].shape[0], EARLY * STEP, LANES), jnp.bfloat16),
             jax.ShapeDtypeStruct((slot_count + UNROLL + 1,), jnp.int32),
         ),
         in_specs=[SMEM, HBM, VMEM, VMEM, VMEM, VMEM],
-        out_specs=(VMEM, SMEM),
+        out_specs=(VMEM, VMEM, SMEM),
         scratch_shapes=[
             pltpu.VMEM((CAP, pick_station.shape[1]), jnp.int32),
             pltpu.SMEM((CAP, pick_station.shape[1]), jnp.int32),
@@ -249,7 +249,7 @@
     )(index, channel_mask, pick_station, pick_lag, *rows)
 
 
-def partial_stack(entries, index, rows, scales, received, group_size):
+def partial_stack(entries, early, scales, received, group_size):
     peers = received.shape[0]
     slot_count = peers * CAP
     lines = NT * group_size // LANES
@@ -257,10 +257,10 @@
     return pl.pallas_call(
         stack_kernel,
         out_shape=jax.ShapeDtypeStruct((slot_count, lines * LANES // slot_count), jnp.bfloat16),
-        in_specs=[SMEM, SMEM, VMEM, VMEM, VMEM, VMEM],
+        in_specs=[SMEM, VMEM, VMEM, VMEM],
         out_specs=VMEM,
         scratch_shapes=[
-            pltpu.VMEM((records, TURNS * STEP, LANES), jnp.bfloat16),
+            pltpu.VMEM((records, (TURNS - EARLY) * STEP, LANES), jnp.bfloat16),
             pltpu.VMEM((peers * SLOT_ROWS, LANES), jnp.float32),
             pltpu.VMEM(((group_size + 1) * STEP, LANES), jnp.float32),
             pltpu.VMEM((UNROLL, 2 * STEP, LANES), jnp.float32),
@@ -269,7 +269,7 @@
         compiler_params=pltpu.CompilerParams(vmem_limit_bytes=16 * 1024 * 1024),
         cost_estimate=pl.CostEstimate(flops=200_000_000, transcendentals=0, bytes_accessed=8_000_000),
         name="stack_picks",
-    )(entries, index, *rows, scales, received)
+    )(entries, early, scales, received)
 
 
 def body(station_data, channel_mask, template_waves, pick_station, pick_lag):
@@ -292,8 +292,8 @@
     outgoing = slot_waves(index, pick_station, waves, sta_size)
     received = lax.all_to_all(outgoing, "sta", split_axis=0, concat_axis=0, tiled=True)
 
-    scales, entries = scales_and_entries(index, channel_mask, pick_station, pick_lag, rows)
-    partial_sums = partial_stack(entries, index, rows, scales, received, group_size)
+    scales, early, entries = scales_and_entries(index, channel_mask, pick_station, pick_lag, rows)
+    partial_sums = partial_stack(entries, early, scales, received, group_size)
     arrived = lax.all_to_all(partial_sums, "sta", split_axis=0, concat_axis=0, tiled=True)
     arrived = arrived.reshape(sta_size, CAP, -1).astype(jnp.float32)
     return jnp.sum(arrived, axis=0).reshape(NT // sta_size, group_size)

time: 57.3 us -> 58.6 us (1.023)
  local copies, waits for them, and re-layouts: 2.01 us -> 3.66 us
  waiting for transfers between devices: 12 us -> 10.8 us
  Pallas kernels: 11.3 us -> 12 us
    unnamed x9 -> x11, local copies, waits for them, and re-layouts: 0.14 us -> 1.75 us
    pallas_call x1, Pallas kernels: 4.36 us -> 5.59 us  [scales_and_entries(): pl.pallas_call(scales_kernel, out_shape=(jax.ShapeDtypeStruct((2 * rows[0...]
    all_to_all x1, waiting for transfers between devices: 10.3 us -> 9.05 us  [body(): lax.all_to_all(outgoing, 'sta', split_axis=0, concat_axis=0, tiled=True)]
  transfers between devices with their start and end apart: 5 -> 5, of which waited for: 2 -> 2; matrix products, arithmetic and copies ran while one was open for 0% -> 0% of each run, Pallas kernels for 11% -> 13%
where the time goes in v11:
time: 58.6 us; the launch traced here: 58.3 us
  starting transfers between devices  16.4 us (28%)
  blocking collectives  15.2 us (26%)
  Pallas kernels  12 us (20%)
  waiting for transfers between devices  10.8 us (18%)
  local copies, waits for them, and re-layouts  3.66 us (6%)
    all_to_all x1, blocking collectives, body(): lax.all_to_all(partial_sums, 'sta', split_axis=0, concat_axis=0, tiled=True)  15.2 us
    all_to_all x1, starting transfers between devices, body(): lax.all_to_all(outgoing, 'sta', split_axis=0, concat_axis=0, tiled=True)  11.5 us
    all_to_all x1, waiting for transfers between devices, body(): lax.all_to_all(outgoing, 'sta', split_axis=0, concat_axis=0, tiled=True)  9.05 us
    pallas_call x1, Pallas kernels, scales_and_entries(): pl.pallas_call(scales_kernel, out_shape=(jax.ShapeDtypeStruct((2 * rows[0...  5.59 us
    ppermute x3, starting transfers between devices, body(): lax.ppermute(own, 'tpl', [(i, (i + hop) % tpl_size) for i in range(tpl_si...  4.83 us
    pallas_call x1, Pallas kernels, partial_stack(): pl.pallas_call(stack_kernel, out_shape=jax.ShapeDtypeStruct((slot_count,...  4.62 us
    pallas_call x1, Pallas kernels, slot_waves(): pl.pallas_call(select_kernel, out_shape=jax.ShapeDtypeStruct((peers, SLOT...  1.83 us
    unnamed x11, local copies, waits for them, and re-layouts  1.75 us
  transfers between devices with their start and end apart: 5, of which 2 were waited for; matrix products, arithmetic and copies ran while one was open for 0% of the time, Pallas kernels for 13%

profile of v11, /device:TPU:2, one launch (start us, length us, event | category | flops | bytes accessed | tf_op | source)
XLA Modules:
  0.0 58.3 jit_solution(16139282451856843207)
XLA Ops:
  0.0 1.1 %reshape.16 = f32[3,2,100,32]{3,2,1,0:T(8,128)S(1)} reshape(f32[3,2,3200]{2,1,0:T(2,128)} %param.5) | data formatting | bytes 153600 | tf_op jit(solution)/shard_map/reshape | solution.py:282
  1.1 0.1 copy.9
  1.3 1.6 %collective-permute-start = (f32[6,32,128]{2,1,0:T(8,128)S(1)}, f32[6,32,128]{2,1,0:T(8,128)S(1)}, u32[]{:S(2)}, u32[]{:S(2)}) collective-permute-start(f32[6,32,128]{2,1,0:T(8,128)S(1)} %bitcast.9), channel_id=1, source_target_pairs={{0,2},{1,3},{2,4},{3,5},{4,6},{5,7},{6,0},{7,1},{8,10},{9,11},{10,... | collective-permute-start | bytes 294920 | tf_op jit(solution)/shard_map/ppermute | solution.py:287
  2.8 2.8 %collective-permute-start.1 = (f32[6,32,128]{2,1,0:T(8,128)S(1)}, f32[6,32,128]{2,1,0:T(8,128)S(1)}, u32[]{:S(2)}, u32[]{:S(2)}) collective-permute-start(f32[6,32,128]{2,1,0:T(8,128)S(1)} %bitcast.10), channel_id=1, source_target_pairs={{0,4},{1,5},{2,6},{3,7},{4,0},{5,1},{6,2},{7,3},{8,12},{9,13},{10,... | collective-permute-start | bytes 294920 | tf_op jit(solution)/shard_map/ppermute | solution.py:287
  5.7 0.4 collective-permute-start.2
  6.1 0.1 pad_add_fusion.index_ref
  6.2 0.9 %copy-done = bf16[32,1,3,640]{3,0,2,1:T(8,128)(2,1)S(1)} copy-done((bf16[32,1,3,640]{3,0,2,1:T(8,128)(2,1)S(1)}, bf16[32,1,3,640]{3,0,2,1:T(8,128)(2,1)}, u32[]{:S(2)}) %copy-start) | copy-done | bytes 122904
  7.1 0.7 %copy-done.1 = s32[32,32]{1,0:T(8,128)S(1)} copy-done((s32[32,32]{1,0:T(8,128)S(1)}, s32[32,32]{1,0:T(8,128)}, u32[]{:S(2)}) %copy-start.1) | copy-done | bytes 4120
  7.8 1.8 %select_waves.1 = bf16[32,64,128]{2,1,0:T(8,128)(2,1)} custom-call(s32[2]{0:T(128)S(1)} %pad_add_fusion.index_ref, s32[32,32]{1,0:T(8,128)S(1)} %copy-done.1, bf16[3,32,640]{2,1,0:T(8,128)(2,1)S(1)} %bitcast.7), custom_call_target="tpu_custom_call" | custom-call | flops 16000000 | bytes 620000 | tf_op jit(solution)/shard_map/select_waves/pallas_call | solution.py:217
  9.6 11.5 %all-to-all-start = ((bf16[32,64,128]{2,1,0:T(8,128)(2,1)}), bf16[32,64,128]{2,1,0:T(8,128)(2,1)S(1)}, u32[]{:S(2)}, u32[]{:S(2)}) async-start(bf16[32,64,128]{2,1,0:T(8,128)(2,1)} %select_waves.1), calls=%async_computation | async-start | bytes 1048576 | tf_op jit(solution)/shard_map/all_to_all | solution.py:293
  21.1 0.0 collective-permute-done
  21.1 0.0 collective-permute-done.1
  21.1 0.0 collective-permute-done.2
  21.2 0.1 collective-permute-start.3
  21.3 1.7 %collective-permute-done.3.far_ref = f32[24,32,128]{2,1,0:T(8,128)S(1)} collective-permute-done((f32[24,32,128]{2,1,0:T(8,128)S(1)}, f32[24,32,128]{2,1,0:T(8,128)S(1)}, u32[]{:S(2)}, u32[]{:S(2)}) %collective-permute-start.3) | collective-permute-done | bytes 393248 | tf_op jit(solution)/shard_map/ppermute | solution.py:289
  23.0 0.0 copy-done.2
  23.0 0.0 copy-done.4
  23.0 5.6 %record_scales.1 = (f32[48,32,128]{2,1,0:T(8,128)S(1)}, bf16[48,160,128]{2,1,0:T(8,128)(2,1)S(1)}, s32[137]{0:T(256)S(1)}) custom-call(s32[2]{0:T(128)S(1)} %pad_add_fusion.index_ref, s32[3,16]{1,0:T(4,128)S(1)} %copy-done.4, s32[32,32]{1,0:T(8,128)S(1)} %copy-done.2, s32[32,32]{1,0:T(8,128)S(1)} %copy-done.3, f32[24,32,128]{2,1,0:T(8,128)S(1)} %pad_maximum_fusion.near_ref, ...), custom_call_target="tpu_custom_call" | custom-call | flops 6000000000 | bytes 2000000 | tf_op jit(solution)/shard_map/record_scales/pallas_call | solution.py:231
  28.6 9.1 %all-to-all-done.waves_ref = bf16[32,64,128]{2,1,0:T(8,128)(2,1)S(1)} async-done(((bf16[32,64,128]{2,1,0:T(8,128)(2,1)}), bf16[32,64,128]{2,1,0:T(8,128)(2,1)S(1)}, u32[]{:S(2)}, u32[]{:S(2)}) %all-to-all-start) | async-done | bytes 524320 | tf_op jit(solution)/shard_map/all_to_all | solution.py:293
  37.7 4.6 %stack_picks.1 = bf16[128,384]{1,0:T(8,128)(2,1)S(1)} custom-call(s32[137]{0:T(256)S(1)} %get-tuple-element.8.entries, bf16[48,160,128]{2,1,0:T(8,128)(2,1)S(1)} %get-tuple-element.9.early, f32[48,32,128]{2,1,0:T(8,128)S(1)} %get-tuple-element.10.scales, bf16[32,64,128]{2,1,0:T(8,128)(2,1)S(1)} %all-to-all-done.waves_ref), custom_call_target="tpu_custom_call" | custom-call | flops 200000000 | bytes 8000000 | tf_op jit(solution)/shard_map/stack_picks/pallas_call | solution.py:257
  42.3 15.2 %all_to_all.14 = bf16[32,4,384]{2,1,0:T(4,128)(2,1)S(1)} all-to-all(bf16[32,4,384]{2,1,0:T(4,128)(2,1)S(1)} %all_to_all.10), channel_id=1, replica_groups=mesh['sta'=32,'tpl'=8] {'sta'}, dimensions={0} | all-to-all | bytes 196608 | tf_op jit(solution)/shard_map/all_to_all | solution.py:297
  57.5 0.1 convert_reduce_fusion
  57.5 0.1 reshape.19
  57.6 0.7 %copy.8 = f32[48,32]{0,1:T(8,128)} copy(f32[48,32]{1,0:T(8,128)S(1)} %reshape.19) | data formatting | bytes 12288 | tf_op jit(solution)/shard_map/reshape | solution.py:299
  (9 shorter events, 0.1 us)
Async XLA Ops:
  0.0 23.0 %copy-start.2 = (s32[32,32]{1,0:T(8,128)S(1)}, s32[32,32]{1,0:T(8,128)}, u32[]{:S(2)}) copy-start(s32[32,32]{1,0:T(8,128)} %station_ref.3) | copy-start | bytes 12292
  0.0 23.0 %copy-start.4 = (s32[3,16]{1,0:T(4,128)S(1)}, s32[3,16]{1,0:T(4,128)}, u32[]{:S(2)}) copy-start(s32[3,16]{1,0:T(4,128)} %mask_hbm.1) | copy-start | bytes 580
  0.0 23.0 %copy-start.3 = (s32[32,32]{1,0:T(8,128)S(1)}, s32[32,32]{1,0:T(8,128)}, u32[]{:S(2)}) copy-start(s32[32,32]{1,0:T(8,128)} %lag_ref.1) | copy-start | bytes 12292
  1.3 19.9 %collective-permute-start = (f32[6,32,128]{2,1,0:T(8,128)S(1)}, f32[6,32,128]{2,1,0:T(8,128)S(1)}, u32[]{:S(2)}, u32[]{:S(2)}) collective-permute-start(f32[6,32,128]{2,1,0:T(8,128)S(1)} %bitcast.9), channel_id=1, source_target_pairs={{0,2},{1,3},{2,4},{3,5},{4,6},{5,7},{6,0},{7,1},{8,10},{9,11},{10,... | collective-permute-start | bytes 294920 | tf_op jit(solution)/shard_map/ppermute | solution.py:287
  2.8 18.3 %collective-permute-start.1 = (f32[6,32,128]{2,1,0:T(8,128)S(1)}, f32[6,32,128]{2,1,0:T(8,128)S(1)}, u32[]{:S(2)}, u32[]{:S(2)}) collective-permute-start(f32[6,32,128]{2,1,0:T(8,128)S(1)} %bitcast.10), channel_id=1, source_target_pairs={{0,4},{1,5},{2,6},{3,7},{4,0},{5,1},{6,2},{7,3},{8,12},{9,13},{10,... | collective-permute-start | bytes 294920 | tf_op jit(solution)/shard_map/ppermute | solution.py:287
  5.7 15.5 %collective-permute-start.2 = (f32[6,32,128]{2,1,0:T(8,128)S(1)}, f32[6,32,128]{2,1,0:T(8,128)S(1)}, u32[]{:S(2)}, u32[]{:S(2)}) collective-permute-start(f32[6,32,128]{2,1,0:T(8,128)S(1)} %bitcast.11), channel_id=1, source_target_pairs={{0,6},{1,7},{2,0},{3,1},{4,2},{5,3},{6,4},{7,5},{8,14},{9,15},{10,... | collective-permute-start | bytes 294920 | tf_op jit(solution)/shard_map/ppermute | solution.py:287
  6.2 0.9 %copy-start = (bf16[32,1,3,640]{3,0,2,1:T(8,128)(2,1)S(1)}, bf16[32,1,3,640]{3,0,2,1:T(8,128)(2,1)}, u32[]{:S(2)}) copy-start(bf16[32,1,3,640]{3,0,2,1:T(8,128)(2,1)} %param.7) | copy-start | bytes 368644
  7.1 0.7 %copy-start.1 = (s32[32,32]{1,0:T(8,128)S(1)}, s32[32,32]{1,0:T(8,128)}, u32[]{:S(2)}) copy-start(s32[32,32]{1,0:T(8,128)} %station_ref.3) | copy-start | bytes 12292
  9.6 28.0 %all-to-all-start = ((bf16[32,64,128]{2,1,0:T(8,128)(2,1)}), bf16[32,64,128]{2,1,0:T(8,128)(2,1)S(1)}, u32[]{:S(2)}, u32[]{:S(2)}) async-start(bf16[32,64,128]{2,1,0:T(8,128)(2,1)} %select_waves.1), calls=%async_computation | async-start | bytes 1048576 | tf_op jit(solution)/shard_map/all_to_all | solution.py:293
  21.2 1.8 %collective-permute-start.3 = (f32[24,32,128]{2,1,0:T(8,128)S(1)}, f32[24,32,128]{2,1,0:T(8,128)S(1)}, u32[]{:S(2)}, u32[]{:S(2)}) collective-permute-start(f32[24,32,128]{2,1,0:T(8,128)S(1)} %pad_maximum_fusion.near_ref), channel_id=1, source_target_pairs={{0,1},{1,0},{2,3},{3,2},{4,5},{5,4},{6,7},{7,6},{8,9},{9,8},{10,11... | collective-permute-start | bytes 1179656 | tf_op jit(solution)/shard_map/ppermute | solution.py:289

commit v12 on v11

--- a/solution.py
+++ b/solution.py
@@ -16,7 +16,7 @@
 OUT_BLOCKS = NT // STEP
 TILES = L // LANES
 TURNS = 8
-EARLY = 5
+EARLY = 3
 UNROLL = 8
 SLOT_ROWS = 64
 RECORDS = 6
@@ -220,7 +220,7 @@
         in_specs=[SMEM, VMEM, VMEM],
         out_specs=VMEM,
         scratch_shapes=[pltpu.VMEM((peers, SLOT_ROWS, LANES), jnp.float32)],
-        compiler_params=pltpu.CompilerParams(vmem_limit_bytes=4 * 1024 * 1024),
+        compiler_params=pltpu.CompilerParams(vmem_limit_bytes=60 * 10260 * 1024),
         cost_estimate=pl.CostEstimate(flops=16_000_000, transcendentals=100, bytes_accessed=620_000),
         name="select_waves",
     )(index, pick_station, template_waves)

time: 58.6 us -> 58.8 us (level)
  other arithmetic: 0.17 us -> 1.71 us
  local copies, waits for them, and re-layouts: 3.66 us -> 2.64 us
  waiting for transfers between devices: 10.8 us -> 10.1 us
    unnamed x11 -> x9, local copies, waits for them, and re-layouts: 1.75 us -> 0.13 us
    concatenate x1, other arithmetic: 0.03 us -> 1.06 us  [body(): near = jnp.concatenate(near, axis=0)]
    all_to_all x1, waiting for transfers between devices: 9.05 us -> 8.35 us  [body(): lax.all_to_all(outgoing, 'sta', split_axis=0, concat_axis=0, tiled=True)]
    pad x1, local copies, waits for them, and re-layouts: 0.03 us -> 0.67 us  [body(): tiles = jnp.pad(tiles, ((0, 0), (0, 0), (0, 0), (0, LANES - BLOCKS)))]
  transfers between devices with their start and end apart: 5 -> 5, of which waited for: 2 -> 2; matrix products, arithmetic and copies ran while one was open for 0% -> 3% of each run, Pallas kernels for 13% -> 13%
where the time goes in v12:
time: 58.8 us; the launch traced here: 58.5 us
  starting transfers between devices  16.5 us (28%)
  blocking collectives  15.1 us (26%)
  Pallas kernels  12.3 us (21%)
  waiting for transfers between devices  10.1 us (17%)
  local copies, waits for them, and re-layouts  2.64 us (4%)
  other arithmetic  1.71 us (3%)
    all_to_all x1, blocking collectives, body(): lax.all_to_all(partial_sums, 'sta', split_axis=0, concat_axis=0, tiled=True)  15.1 us
    all_to_all x1, starting transfers between devices, body(): lax.all_to_all(outgoing, 'sta', split_axis=0, concat_axis=0, tiled=True)  11.6 us
    all_to_all x1, waiting for transfers between devices, body(): lax.all_to_all(outgoing, 'sta', split_axis=0, concat_axis=0, tiled=True)  8.35 us
    pallas_call x1, Pallas kernels, scales_and_entries(): pl.pallas_call(scales_kernel, out_shape=(jax.ShapeDtypeStruct((2 * rows[0...  5.23 us
    pallas_call x1, Pallas kernels, partial_stack(): pl.pallas_call(stack_kernel, out_shape=jax.ShapeDtypeStruct((slot_count,...  4.89 us
    ppermute x3, starting transfers between devices, body(): lax.ppermute(own, 'tpl', [(i, (i + hop) % tpl_size) for i in range(tpl_si...  4.76 us
    pallas_call x1, Pallas kernels, slot_waves(): pl.pallas_call(select_kernel, out_shape=jax.ShapeDtypeStruct((peers, SLOT...  2.23 us
    ppermute x1, waiting for transfers between devices, body(): lax.ppermute(near, 'tpl', [(i, i ^ 1) for i in range(tpl_size)])  1.71 us
  transfers between devices with their start and end apart: 5, of which 2 were waited for; matrix products, arithmetic and copies ran while one was open for 3% of the time, Pallas kernels for 13%

profile of v12, /device:TPU:2, one launch (start us, length us, event | category | flops | bytes accessed | tf_op | source)
XLA Modules:
  0.0 58.5 jit_solution(13012658772902438554)
XLA Ops:
  0.0 1.0 %reshape.16 = f32[3,2,100,32]{3,2,1,0:T(8,128)S(1)} reshape(f32[3,2,3200]{2,1,0:T(2,128)} %param.5) | data formatting | bytes 153600 | tf_op jit(solution)/shard_map/reshape | solution.py:282
  1.1 0.1 copy.9
  1.2 0.7 %pad.4.clone = f32[3,2,32,128]{3,2,1,0:T(8,128)} pad(f32[3,2,32,100]{3,2,1,0:T(8,128)S(1)} %copy.9, f32[]{:T(128)} %constant.12.clone.1), padding=0_0x0_0x0_0x0_28 | pad | bytes 175108 | tf_op jit(solution)/shard_map/jit(_pad)/pad | solution.py:283
  1.8 1.5 %collective-permute-start = (f32[6,32,128]{2,1,0:T(8,128)}, f32[6,32,128]{2,1,0:T(8,128)}, u32[]{:S(2)}, u32[]{:S(2)}) collective-permute-start(f32[6,32,128]{2,1,0:T(8,128)} %bitcast.3), channel_id=1, source_target_pairs={{0,2},{1,3},{2,4},{3,5},{4,6},{5,7},{6,0},{7,1},{8,10},{9,11},{10,... | collective-permute-start | bytes 294920 | tf_op jit(solution)/shard_map/ppermute | solution.py:287
  3.3 2.8 %collective-permute-start.1 = (f32[6,32,128]{2,1,0:T(8,128)}, f32[6,32,128]{2,1,0:T(8,128)}, u32[]{:S(2)}, u32[]{:S(2)}) collective-permute-start(f32[6,32,128]{2,1,0:T(8,128)} %bitcast.3), channel_id=1, source_target_pairs={{0,4},{1,5},{2,6},{3,7},{4,0},{5,1},{6,2},{7,3},{8,12},{9,13},{10,... | collective-permute-start | bytes 294920 | tf_op jit(solution)/shard_map/ppermute | solution.py:287
  6.2 0.4 collective-permute-start.2
  6.6 0.6 pad_add_fusion.index_ref
  7.2 2.2 %select_waves.1 = bf16[32,64,128]{2,1,0:T(8,128)(2,1)} custom-call(s32[2]{0:T(128)} %pad_add_fusion.index_ref, s32[32,32]{1,0:T(8,128)} %station_ref.3, bf16[3,32,640]{2,1,0:T(8,128)(2,1)} %bitcast.8), custom_call_target="tpu_custom_call" | custom-call | flops 16000000 | bytes 620000 | tf_op jit(solution)/shard_map/select_waves/pallas_call | solution.py:217
  9.4 11.6 %all-to-all-start = ((bf16[32,64,128]{2,1,0:T(8,128)(2,1)}), bf16[32,64,128]{2,1,0:T(8,128)(2,1)S(1)}, u32[]{:S(2)}, u32[]{:S(2)}) async-start(bf16[32,64,128]{2,1,0:T(8,128)(2,1)} %select_waves.1), calls=%async_computation | async-start | bytes 1048576 | tf_op jit(solution)/shard_map/all_to_all | solution.py:293
  21.1 0.0 collective-permute-done
  21.1 0.0 collective-permute-done.1
  21.1 0.0 collective-permute-done.2
  21.1 1.1 %pad_maximum_fusion.near_ref = f32[24,32,128]{2,1,0:T(8,128)S(1)} fusion(f32[6,32,128]{2,1,0:T(8,128)} %collective-permute-done.2, f32[6,32,128]{2,1,0:T(8,128)} %collective-permute-done.1, f32[6,32,128]{2,1,0:T(8,128)} %collective-permute-done, f32[6,32,128]{2,1,0:T(8,128)} %bitcast.3), kind=kLoop, calls=%fused_computation | loop fusion | flops 294912 | bytes 786432 | tf_op jit(solution)/shard_map/concatenate | solution.py:288
  22.2 0.1 collective-permute-start.3
  22.3 1.7 %collective-permute-done.3.far_ref = f32[24,32,128]{2,1,0:T(8,128)S(1)} collective-permute-done((f32[24,32,128]{2,1,0:T(8,128)S(1)}, f32[24,32,128]{2,1,0:T(8,128)S(1)}, u32[]{:S(2)}, u32[]{:S(2)}) %collective-permute-start.3) | collective-permute-done | bytes 393248 | tf_op jit(solution)/shard_map/ppermute | solution.py:289
  24.0 0.0 copy-done
  24.0 0.0 copy-done.1
  24.0 5.2 %record_scales.1 = (f32[48,32,128]{2,1,0:T(8,128)S(1)}, bf16[48,96,128]{2,1,0:T(8,128)(2,1)S(1)}, s32[137]{0:T(256)S(1)}) custom-call(s32[2]{0:T(128)S(1)} %copy-done.1, s32[3,16]{1,0:T(4,128)S(1)} %copy-done.3, s32[32,32]{1,0:T(8,128)S(1)} %copy-done, s32[32,32]{1,0:T(8,128)S(1)} %copy-done.2, f32[24,32,128]{2,1,0:T(8,128)S(1)} %pad_maximum_fusion.near_ref, ...), custom_call_target="tpu_custom_call" | custom-call | flops 6000000000 | bytes 2000000 | tf_op jit(solution)/shard_map/record_scales/pallas_call | solution.py:231
  29.2 8.3 %all-to-all-done.waves_ref = bf16[32,64,128]{2,1,0:T(8,128)(2,1)S(1)} async-done(((bf16[32,64,128]{2,1,0:T(8,128)(2,1)}), bf16[32,64,128]{2,1,0:T(8,128)(2,1)S(1)}, u32[]{:S(2)}, u32[]{:S(2)}) %all-to-all-start) | async-done | bytes 524320 | tf_op jit(solution)/shard_map/all_to_all | solution.py:293
  37.6 4.9 %stack_picks.1 = bf16[128,384]{1,0:T(8,128)(2,1)S(1)} custom-call(s32[137]{0:T(256)S(1)} %get-tuple-element.8.entries, bf16[48,96,128]{2,1,0:T(8,128)(2,1)S(1)} %get-tuple-element.9.early, f32[48,32,128]{2,1,0:T(8,128)S(1)} %get-tuple-element.10.scales, bf16[32,64,128]{2,1,0:T(8,128)(2,1)S(1)} %all-to-all-done.waves_ref), custom_call_target="tpu_custom_call" | custom-call | flops 200000000 | bytes 8000000 | tf_op jit(solution)/shard_map/stack_picks/pallas_call | solution.py:257
  42.5 15.1 %all_to_all.14 = bf16[32,4,384]{2,1,0:T(4,128)(2,1)S(1)} all-to-all(bf16[32,4,384]{2,1,0:T(4,128)(2,1)S(1)} %all_to_all.10), channel_id=1, replica_groups=mesh['sta'=32,'tpl'=8] {'sta'}, dimensions={0} | all-to-all | bytes 196608 | tf_op jit(solution)/shard_map/all_to_all | solution.py:297
  57.6 0.1 convert_reduce_fusion
  57.7 0.1 reshape.19
  57.8 0.7 %copy.8 = f32[48,32]{0,1:T(8,128)} copy(f32[48,32]{1,0:T(8,128)S(1)} %reshape.19) | data formatting | bytes 12288 | tf_op jit(solution)/shard_map/reshape | solution.py:299
  (7 shorter events, 0.0 us)
Async XLA Ops:
  1.8 19.2 %collective-permute-start = (f32[6,32,128]{2,1,0:T(8,128)}, f32[6,32,128]{2,1,0:T(8,128)}, u32[]{:S(2)}, u32[]{:S(2)}) collective-permute-start(f32[6,32,128]{2,1,0:T(8,128)} %bitcast.3), channel_id=1, source_target_pairs={{0,2},{1,3},{2,4},{3,5},{4,6},{5,7},{6,0},{7,1},{8,10},{9,11},{10,... | collective-permute-start | bytes 294920 | tf_op jit(solution)/shard_map/ppermute | solution.py:287
  3.3 17.7 %collective-permute-start.1 = (f32[6,32,128]{2,1,0:T(8,128)}, f32[6,32,128]{2,1,0:T(8,128)}, u32[]{:S(2)}, u32[]{:S(2)}) collective-permute-start(f32[6,32,128]{2,1,0:T(8,128)} %bitcast.3), channel_id=1, source_target_pairs={{0,4},{1,5},{2,6},{3,7},{4,0},{5,1},{6,2},{7,3},{8,12},{9,13},{10,... | collective-permute-start | bytes 294920 | tf_op jit(solution)/shard_map/ppermute | solution.py:287
  6.2 14.9 %collective-permute-start.2 = (f32[6,32,128]{2,1,0:T(8,128)}, f32[6,32,128]{2,1,0:T(8,128)}, u32[]{:S(2)}, u32[]{:S(2)}) collective-permute-start(f32[6,32,128]{2,1,0:T(8,128)} %bitcast.3), channel_id=1, source_target_pairs={{0,6},{1,7},{2,0},{3,1},{4,2},{5,3},{6,4},{7,5},{8,14},{9,15},{10,... | collective-permute-start | bytes 294920 | tf_op jit(solution)/shard_map/ppermute | solution.py:287
  9.4 14.6 %copy-start = (s32[32,32]{1,0:T(8,128)S(1)}, s32[32,32]{1,0:T(8,128)}, u32[]{:S(2)}) copy-start(s32[32,32]{1,0:T(8,128)} %station_ref.3) | copy-start | bytes 12292
  9.4 14.6 %copy-start.1 = (s32[2]{0:T(128)S(1)}, s32[2]{0:T(128)}, u32[]{:S(2)}) copy-start(s32[2]{0:T(128)} %pad_add_fusion.index_ref) | copy-start | bytes 28
  9.4 14.6 %copy-start.2 = (s32[32,32]{1,0:T(8,128)S(1)}, s32[32,32]{1,0:T(8,128)}, u32[]{:S(2)}) copy-start(s32[32,32]{1,0:T(8,128)} %lag_ref.1) | copy-start | bytes 12292
  9.4 14.6 %copy-start.3 = (s32[3,16]{1,0:T(4,128)S(1)}, s32[3,16]{1,0:T(4,128)}, u32[]{:S(2)}) copy-start(s32[3,16]{1,0:T(4,128)} %mask_hbm.1) | copy-start | bytes 580
  9.4 28.2 %all-to-all-start = ((bf16[32,64,128]{2,1,0:T(8,128)(2,1)}), bf16[32,64,128]{2,1,0:T(8,128)(2,1)S(1)}, u32[]{:S(2)}, u32[]{:S(2)}) async-start(bf16[32,64,128]{2,1,0:T(8,128)(2,1)} %select_waves.1), calls=%async_computation | async-start | bytes 1048576 | tf_op jit(solution)/shard_map/all_to_all | solution.py:293
  22.2 1.8 %collective-permute-start.3 = (f32[24,32,128]{2,1,0:T(8,128)S(1)}, f32[24,32,128]{2,1,0:T(8,128)S(1)}, u32[]{:S(2)}, u32[]{:S(2)}) collective-permute-start(f32[24,32,128]{2,1,0:T(8,128)S(1)} %pad_maximum_fusion.near_ref), channel_id=1, source_target_pairs={{0,1},{1,0},{2,3},{3,2},{4,5},{5,4},{6,7},{7,6},{8,9},{9,8},{10,11... | collective-permute-start | bytes 1179656 | tf_op jit(solution)/shard_map/ppermute | solution.py:289

commit v13 on v11

--- a/solution.py
+++ b/solution.py
@@ -16,7 +16,7 @@
 OUT_BLOCKS = NT // STEP
 TILES = L // LANES
 TURNS = 8
-EARLY = 5
+EARLY = 2
 UNROLL = 8
 SLOT_ROWS = 64
 RECORDS = 6

time: 58.6 us -> 57.2 us (0.976)
  local copies, waits for them, and re-layouts: 3.66 us -> 2.01 us
  waiting for transfers between devices: 10.8 us -> 11.5 us
    unnamed x11 -> x9, local copies, waits for them, and re-layouts: 1.75 us -> 0.14 us
    pallas_call x1, Pallas kernels: 5.59 us -> 4.86 us  [scales_and_entries(): pl.pallas_call(scales_kernel, out_shape=(jax.ShapeDtypeStruct((2 * rows[0...]
    all_to_all x1, waiting for transfers between devices: 9.05 us -> 9.76 us  [body(): lax.all_to_all(outgoing, 'sta', split_axis=0, concat_axis=0, tiled=True)]
  transfers between devices with their start and end apart: 5 -> 5, of which waited for: 2 -> 2; matrix products, arithmetic and copies ran while one was open for 0% -> 0% of each run, Pallas kernels for 13% -> 12%
where the time goes in v13:
time: 57.2 us; the launch traced here: 56.9 us
  starting transfers between devices  16.4 us (29%)
  blocking collectives  15.1 us (26%)
  Pallas kernels  11.6 us (20%)
  waiting for transfers between devices  11.5 us (20%)
  local copies, waits for them, and re-layouts  2.01 us (4%)
    all_to_all x1, blocking collectives, body(): lax.all_to_all(partial_sums, 'sta', split_axis=0, concat_axis=0, tiled=True)  15.1 us
    all_to_all x1, starting transfers between devices, body(): lax.all_to_all(outgoing, 'sta', split_axis=0, concat_axis=0, tiled=True)  11.5 us
    all_to_all x1, waiting for transfers between devices, body(): lax.all_to_all(outgoing, 'sta', split_axis=0, concat_axis=0, tiled=True)  9.76 us
    pallas_call x1, Pallas kernels, partial_stack(): pl.pallas_call(stack_kernel, out_shape=jax.ShapeDtypeStruct((slot_count,...  4.93 us
    pallas_call x1, Pallas kernels, scales_and_entries(): pl.pallas_call(scales_kernel, out_shape=(jax.ShapeDtypeStruct((2 * rows[0...  4.86 us
    ppermute x3, starting transfers between devices, body(): lax.ppermute(own, 'tpl', [(i, (i + hop) % tpl_size) for i in range(tpl_si...  4.83 us
    pallas_call x1, Pallas kernels, slot_waves(): pl.pallas_call(select_kernel, out_shape=jax.ShapeDtypeStruct((peers, SLOT...  1.84 us
    ppermute x1, waiting for transfers between devices, body(): lax.ppermute(near, 'tpl', [(i, i ^ 1) for i in range(tpl_size)])  1.71 us
  transfers between devices with their start and end apart: 5, of which 2 were waited for; matrix products, arithmetic and copies ran while one was open for 0% of the time, Pallas kernels for 12%

profile of v13, /device:TPU:2, one launch (start us, length us, event | category | flops | bytes accessed | tf_op | source)
XLA Modules:
  0.0 56.9 jit_solution(13292713802542837905)
XLA Ops:
  0.0 1.0 %reshape.16 = f32[3,2,100,32]{3,2,1,0:T(8,128)S(1)} reshape(f32[3,2,3200]{2,1,0:T(2,128)} %param.5) | data formatting | bytes 153600 | tf_op jit(solution)/shard_map/reshape | solution.py:282
  1.1 0.1 copy.9
  1.2 0.0 copy-start.1
  1.2 1.6 %collective-permute-start = (f32[6,32,128]{2,1,0:T(8,128)S(1)}, f32[6,32,128]{2,1,0:T(8,128)S(1)}, u32[]{:S(2)}, u32[]{:S(2)}) collective-permute-start(f32[6,32,128]{2,1,0:T(8,128)S(1)} %bitcast.9), channel_id=1, source_target_pairs={{0,2},{1,3},{2,4},{3,5},{4,6},{5,7},{6,0},{7,1},{8,10},{9,11},{10,... | collective-permute-start | bytes 294920 | tf_op jit(solution)/shard_map/ppermute | solution.py:287
  2.8 2.8 %collective-permute-start.1 = (f32[6,32,128]{2,1,0:T(8,128)S(1)}, f32[6,32,128]{2,1,0:T(8,128)S(1)}, u32[]{:S(2)}, u32[]{:S(2)}) collective-permute-start(f32[6,32,128]{2,1,0:T(8,128)S(1)} %bitcast.10), channel_id=1, source_target_pairs={{0,4},{1,5},{2,6},{3,7},{4,0},{5,1},{6,2},{7,3},{8,12},{9,13},{10,... | collective-permute-start | bytes 294920 | tf_op jit(solution)/shard_map/ppermute | solution.py:287
  5.6 0.4 collective-permute-start.2
  6.1 0.1 pad_add_fusion.index_ref
  6.1 0.0 copy-done
  6.1 1.8 %select_waves.1 = bf16[32,64,128]{2,1,0:T(8,128)(2,1)} custom-call(s32[2]{0:T(128)S(1)} %pad_add_fusion.index_ref, s32[32,32]{1,0:T(8,128)S(1)} %copy-done.1, bf16[3,32,640]{2,1,0:T(8,128)(2,1)S(1)} %bitcast.7), custom_call_target="tpu_custom_call" | custom-call | flops 16000000 | bytes 620000 | tf_op jit(solution)/shard_map/select_waves/pallas_call | solution.py:217
  8.0 11.5 %all-to-all-start = ((bf16[32,64,128]{2,1,0:T(8,128)(2,1)}), bf16[32,64,128]{2,1,0:T(8,128)(2,1)S(1)}, u32[]{:S(2)}, u32[]{:S(2)}) async-start(bf16[32,64,128]{2,1,0:T(8,128)(2,1)} %select_waves.1), calls=%async_computation | async-start | bytes 1048576 | tf_op jit(solution)/shard_map/all_to_all | solution.py:293
  19.5 0.0 copy-start.2
  19.5 0.0 copy-start.3
  19.5 0.0 collective-permute-done
  19.5 0.0 collective-permute-done.1
  19.5 0.0 collective-permute-done.2
  19.6 0.1 collective-permute-start.3
  19.7 1.7 %collective-permute-done.3.far_ref = f32[24,32,128]{2,1,0:T(8,128)S(1)} collective-permute-done((f32[24,32,128]{2,1,0:T(8,128)S(1)}, f32[24,32,128]{2,1,0:T(8,128)S(1)}, u32[]{:S(2)}, u32[]{:S(2)}) %collective-permute-start.3) | collective-permute-done | bytes 393248 | tf_op jit(solution)/shard_map/ppermute | solution.py:289
  21.4 4.9 %record_scales.1 = (f32[48,32,128]{2,1,0:T(8,128)S(1)}, bf16[48,64,128]{2,1,0:T(8,128)(2,1)S(1)}, s32[137]{0:T(256)S(1)}) custom-call(s32[2]{0:T(128)S(1)} %pad_add_fusion.index_ref, s32[3,16]{1,0:T(4,128)S(1)} %copy-done.3, s32[32,32]{1,0:T(8,128)S(1)} %copy-done.1, s32[32,32]{1,0:T(8,128)S(1)} %copy-done.2, f32[24,32,128]{2,1,0:T(8,128)S(1)} %pad_maximum_fusion.near_ref, ...), custom_call_target="tpu_custom_call" | custom-call | flops 6000000000 | bytes 2000000 | tf_op jit(solution)/shard_map/record_scales/pallas_call | solution.py:231
  26.3 9.8 %all-to-all-done.waves_ref = bf16[32,64,128]{2,1,0:T(8,128)(2,1)S(1)} async-done(((bf16[32,64,128]{2,1,0:T(8,128)(2,1)}), bf16[32,64,128]{2,1,0:T(8,128)(2,1)S(1)}, u32[]{:S(2)}, u32[]{:S(2)}) %all-to-all-start) | async-done | bytes 524320 | tf_op jit(solution)/shard_map/all_to_all | solution.py:293
  36.0 4.9 %stack_picks.1 = bf16[128,384]{1,0:T(8,128)(2,1)S(1)} custom-call(s32[137]{0:T(256)S(1)} %get-tuple-element.8.entries, bf16[48,64,128]{2,1,0:T(8,128)(2,1)S(1)} %get-tuple-element.9.early, f32[48,32,128]{2,1,0:T(8,128)S(1)} %get-tuple-element.10.scales, bf16[32,64,128]{2,1,0:T(8,128)(2,1)S(1)} %all-to-all-done.waves_ref), custom_call_target="tpu_custom_call" | custom-call | flops 200000000 | bytes 8000000 | tf_op jit(solution)/shard_map/stack_picks/pallas_call | solution.py:257
  41.0 15.1 %all_to_all.14 = bf16[32,4,384]{2,1,0:T(4,128)(2,1)S(1)} all-to-all(bf16[32,4,384]{2,1,0:T(4,128)(2,1)S(1)} %all_to_all.10), channel_id=1, replica_groups=mesh['sta'=32,'tpl'=8] {'sta'}, dimensions={0} | all-to-all | bytes 196608 | tf_op jit(solution)/shard_map/all_to_all | solution.py:297
  56.1 0.1 convert_reduce_fusion
  56.2 0.1 reshape.19
  56.2 0.7 %copy.8 = f32[48,32]{0,1:T(8,128)} copy(f32[48,32]{1,0:T(8,128)S(1)} %reshape.19) | data formatting | bytes 12288 | tf_op jit(solution)/shard_map/reshape | solution.py:299
  (7 shorter events, 0.1 us)
Async XLA Ops:
  1.2 5.0 %copy-start = (bf16[32,1,3,640]{3,0,2,1:T(8,128)(2,1)S(1)}, bf16[32,1,3,640]{3,0,2,1:T(8,128)(2,1)}, u32[]{:S(2)}) copy-start(bf16[32,1,3,640]{3,0,2,1:T(8,128)(2,1)} %param.7) | copy-start | bytes 368644
  1.2 4.9 %copy-start.1 = (s32[32,32]{1,0:T(8,128)S(1)}, s32[32,32]{1,0:T(8,128)}, u32[]{:S(2)}) copy-start(s32[32,32]{1,0:T(8,128)} %station_ref.3) | copy-start | bytes 12292
  1.2 18.3 %collective-permute-start = (f32[6,32,128]{2,1,0:T(8,128)S(1)}, f32[6,32,128]{2,1,0:T(8,128)S(1)}, u32[]{:S(2)}, u32[]{:S(2)}) collective-permute-start(f32[6,32,128]{2,1,0:T(8,128)S(1)} %bitcast.9), channel_id=1, source_target_pairs={{0,2},{1,3},{2,4},{3,5},{4,6},{5,7},{6,0},{7,1},{8,10},{9,11},{10,... | collective-permute-start | bytes 294920 | tf_op jit(solution)/shard_map/ppermute | solution.py:287
  2.8 16.7 %collective-permute-start.1 = (f32[6,32,128]{2,1,0:T(8,128)S(1)}, f32[6,32,128]{2,1,0:T(8,128)S(1)}, u32[]{:S(2)}, u32[]{:S(2)}) collective-permute-start(f32[6,32,128]{2,1,0:T(8,128)S(1)} %bitcast.10), channel_id=1, source_target_pairs={{0,4},{1,5},{2,6},{3,7},{4,0},{5,1},{6,2},{7,3},{8,12},{9,13},{10,... | collective-permute-start | bytes 294920 | tf_op jit(solution)/shard_map/ppermute | solution.py:287
  5.6 13.9 %collective-permute-start.2 = (f32[6,32,128]{2,1,0:T(8,128)S(1)}, f32[6,32,128]{2,1,0:T(8,128)S(1)}, u32[]{:S(2)}, u32[]{:S(2)}) collective-permute-start(f32[6,32,128]{2,1,0:T(8,128)S(1)} %bitcast.11), channel_id=1, source_target_pairs={{0,6},{1,7},{2,0},{3,1},{4,2},{5,3},{6,4},{7,5},{8,14},{9,15},{10,... | collective-permute-start | bytes 294920 | tf_op jit(solution)/shard_map/ppermute | solution.py:287
  8.0 28.0 %all-to-all-start = ((bf16[32,64,128]{2,1,0:T(8,128)(2,1)}), bf16[32,64,128]{2,1,0:T(8,128)(2,1)S(1)}, u32[]{:S(2)}, u32[]{:S(2)}) async-start(bf16[32,64,128]{2,1,0:T(8,128)(2,1)} %select_waves.1), calls=%async_computation | async-start | bytes 1048576 | tf_op jit(solution)/shard_map/all_to_all | solution.py:293
  19.5 1.9 %copy-start.2 = (s32[32,32]{1,0:T(8,128)S(1)}, s32[32,32]{1,0:T(8,128)}, u32[]{:S(2)}) copy-start(s32[32,32]{1,0:T(8,128)} %lag_ref.1) | copy-start | bytes 12292
  19.5 1.9 %copy-start.3 = (s32[3,16]{1,0:T(4,128)S(1)}, s32[3,16]{1,0:T(4,128)}, u32[]{:S(2)}) copy-start(s32[3,16]{1,0:T(4,128)} %mask_hbm.1) | copy-start | bytes 580
  19.6 1.8 %collective-permute-start.3 = (f32[24,32,128]{2,1,0:T(8,128)S(1)}, f32[24,32,128]{2,1,0:T(8,128)S(1)}, u32[]{:S(2)}, u32[]{:S(2)}) collective-permute-start(f32[24,32,128]{2,1,0:T(8,128)S(1)} %pad_maximum_fusion.near_ref), channel_id=1, source_target_pairs={{0,1},{1,0},{2,3},{3,2},{4,5},{5,4},{6,7},{7,6},{8,9},{9,8},{10,11... | collective-permute-start | bytes 1179656 | tf_op jit(solution)/shard_map/ppermute | solution.py:289

commit v14 on v10

--- a/solution.py
+++ b/solution.py
@@ -16,7 +16,7 @@
 OUT_BLOCKS = NT // STEP
 TILES = L // LANES
 TURNS = 8
-UNROLL = 16
+UNROLL = 6
 SLOT_ROWS = 64
 RECORDS = 6
 STATION_BITS = 4

time: 61.8 us -> 58.1 us (0.940)
  Pallas kernels: 15.8 us -> 12 us
    pallas_call x1, Pallas kernels: 9.55 us -> 5.81 us  [partial_stack(): pl.pallas_call(stack_kernel, out_shape=jax.ShapeDtypeStruct((slot_count,...]
  transfers between devices with their start and end apart: 5 -> 5, of which waited for: 2 -> 2; matrix products, arithmetic and copies ran while one was open for 0% -> 0% of each run, Pallas kernels for 10% -> 11%
where the time goes in v14:
time: 58.1 us; the launch traced here: 57.8 us
  starting transfers between devices  16.4 us (28%)
  blocking collectives  15.1 us (26%)
  Pallas kernels  12 us (21%)
  waiting for transfers between devices  12 us (21%)
  local copies, waits for them, and re-layouts  2.01 us (3%)
    all_to_all x1, blocking collectives, body(): lax.all_to_all(partial_sums, 'sta', split_axis=0, concat_axis=0, tiled=True)  15.1 us
    all_to_all x1, starting transfers between devices, body(): lax.all_to_all(outgoing, 'sta', split_axis=0, concat_axis=0, tiled=True)  11.5 us
    all_to_all x1, waiting for transfers between devices, body(): lax.all_to_all(outgoing, 'sta', split_axis=0, concat_axis=0, tiled=True)  10.3 us
    pallas_call x1, Pallas kernels, partial_stack(): pl.pallas_call(stack_kernel, out_shape=jax.ShapeDtypeStruct((slot_count,...  5.81 us
    ppermute x3, starting transfers between devices, body(): lax.ppermute(own, 'tpl', [(i, (i + hop) % tpl_size) for i in range(tpl_si...  4.83 us
    pallas_call x1, Pallas kernels, scales_and_entries(): pl.pallas_call(scales_kernel, out_shape=(jax.ShapeDtypeStruct((2 * rows[0...  4.36 us
    pallas_call x1, Pallas kernels, slot_waves(): pl.pallas_call(select_kernel, out_shape=jax.ShapeDtypeStruct((peers, SLOT...  1.84 us
    ppermute x1, waiting for transfers between devices, body(): lax.ppermute(near, 'tpl', [(i, i ^ 1) for i in range(tpl_size)])  1.71 us
  transfers between devices with their start and end apart: 5, of which 2 were waited for; matrix products, arithmetic and copies ran while one was open for 0% of the time, Pallas kernels for 11%

profile of v14, /device:TPU:2, one launch (start us, length us, event | category | flops | bytes accessed | tf_op | source)
XLA Modules:
  0.0 57.8 jit_solution(12587250982019812408)
XLA Ops:
  0.0 1.0 %reshape.16 = f32[3,2,100,32]{3,2,1,0:T(8,128)S(1)} reshape(f32[3,2,3200]{2,1,0:T(2,128)} %param.5) | data formatting | bytes 153600 | tf_op jit(solution)/shard_map/reshape | solution.py:282
  1.1 0.1 copy.9
  1.2 0.0 copy-start.1
  1.2 2.3 %collective-permute-start.2 = (f32[6,32,128]{2,1,0:T(8,128)S(1)}, f32[6,32,128]{2,1,0:T(8,128)S(1)}, u32[]{:S(2)}, u32[]{:S(2)}) collective-permute-start(f32[6,32,128]{2,1,0:T(8,128)S(1)} %bitcast.9), channel_id=1, source_target_pairs={{0,6},{1,7},{2,0},{3,1},{4,2},{5,3},{6,4},{7,5},{8,14},{9,15},{10,... | collective-permute-start | bytes 294920 | tf_op jit(solution)/shard_map/ppermute | solution.py:287
  3.6 0.7 %collective-permute-start.1 = (f32[6,32,128]{2,1,0:T(8,128)S(1)}, f32[6,32,128]{2,1,0:T(8,128)S(1)}, u32[]{:S(2)}, u32[]{:S(2)}) collective-permute-start(f32[6,32,128]{2,1,0:T(8,128)S(1)} %bitcast.10), channel_id=1, source_target_pairs={{0,4},{1,5},{2,6},{3,7},{4,0},{5,1},{6,2},{7,3},{8,12},{9,13},{10,... | collective-permute-start | bytes 294920 | tf_op jit(solution)/shard_map/ppermute | solution.py:287
  4.3 1.8 %collective-permute-start = (f32[6,32,128]{2,1,0:T(8,128)S(1)}, f32[6,32,128]{2,1,0:T(8,128)S(1)}, u32[]{:S(2)}, u32[]{:S(2)}) collective-permute-start(f32[6,32,128]{2,1,0:T(8,128)S(1)} %bitcast.11), channel_id=1, source_target_pairs={{0,2},{1,3},{2,4},{3,5},{4,6},{5,7},{6,0},{7,1},{8,10},{9,11},{10,... | collective-permute-start | bytes 294920 | tf_op jit(solution)/shard_map/ppermute | solution.py:287
  6.1 0.1 pad_add_fusion.index_ref
  6.1 0.0 copy-done
  6.1 1.8 %select_waves.1 = bf16[32,64,128]{2,1,0:T(8,128)(2,1)} custom-call(s32[2]{0:T(128)S(1)} %pad_add_fusion.index_ref, s32[32,32]{1,0:T(8,128)S(1)} %copy-done.1, bf16[3,32,640]{2,1,0:T(8,128)(2,1)S(1)} %bitcast.7), custom_call_target="tpu_custom_call" | custom-call | flops 16000000 | bytes 620000 | tf_op jit(solution)/shard_map/select_waves/pallas_call | solution.py:218
  8.0 11.5 %all-to-all-start = ((bf16[32,64,128]{2,1,0:T(8,128)(2,1)}), bf16[32,64,128]{2,1,0:T(8,128)(2,1)S(1)}, u32[]{:S(2)}, u32[]{:S(2)}) async-start(bf16[32,64,128]{2,1,0:T(8,128)(2,1)} %select_waves.1), calls=%async_computation | async-start | bytes 1048576 | tf_op jit(solution)/shard_map/all_to_all | solution.py:293
  19.5 0.0 copy-start.2
  19.5 0.0 copy-start.3
  19.5 0.0 collective-permute-done.2
  19.5 0.0 collective-permute-done.1
  19.5 0.0 collective-permute-done
  19.6 0.1 collective-permute-start.3
  19.7 1.7 %collective-permute-done.3.far_ref = f32[24,32,128]{2,1,0:T(8,128)S(1)} collective-permute-done((f32[24,32,128]{2,1,0:T(8,128)S(1)}, f32[24,32,128]{2,1,0:T(8,128)S(1)}, u32[]{:S(2)}, u32[]{:S(2)}) %collective-permute-start.3) | collective-permute-done | bytes 393248 | tf_op jit(solution)/shard_map/ppermute | solution.py:289
  21.4 4.4 %record_scales.1 = (f32[48,32,128]{2,1,0:T(8,128)S(1)}, s32[135]{0:T(256)S(1)}) custom-call(s32[2]{0:T(128)S(1)} %pad_add_fusion.index_ref, s32[3,16]{1,0:T(4,128)S(1)} %copy-done.3, s32[32,32]{1,0:T(8,128)S(1)} %copy-done.1, s32[32,32]{1,0:T(8,128)S(1)} %copy-done.2, f32[24,32,128]{2,1,0:T(8,128)S(1)} %pad_maximum_fusion.near_ref, ...), custom_call_target="tpu_custom_call" | custom-call | flops 6000000000 | bytes 2000000 | tf_op jit(solution)/shard_map/record_scales/pallas_call | solution.py:232
  25.8 10.3 %all-to-all-done.waves_ref = bf16[32,64,128]{2,1,0:T(8,128)(2,1)S(1)} async-done(((bf16[32,64,128]{2,1,0:T(8,128)(2,1)}), bf16[32,64,128]{2,1,0:T(8,128)(2,1)S(1)}, u32[]{:S(2)}, u32[]{:S(2)}) %all-to-all-start) | async-done | bytes 524320 | tf_op jit(solution)/shard_map/all_to_all | solution.py:293
  36.0 5.8 %stack_picks.1 = bf16[128,384]{1,0:T(8,128)(2,1)S(1)} custom-call(s32[135]{0:T(256)S(1)} %get-tuple-element.7.entries, s32[2]{0:T(128)S(1)} %pad_add_fusion.index_ref, f32[24,32,128]{2,1,0:T(8,128)S(1)} %pad_maximum_fusion.near_ref, f32[24,32,128]{2,1,0:T(8,128)S(1)} %collective-permute-done.3.far_ref, f32[48,32,128]{2,1,0:T(8,128)S(1)} %get-tuple-element.8.scales, ...), custom_call_target="tpu_custom_call" | custom-call | flops 200000000 | bytes 8000000 | tf_op jit(solution)/shard_map/stack_picks/pallas_call | solution.py:257
  41.9 15.1 %all_to_all.14 = bf16[32,4,384]{2,1,0:T(4,128)(2,1)S(1)} all-to-all(bf16[32,4,384]{2,1,0:T(4,128)(2,1)S(1)} %all_to_all.10), channel_id=1, replica_groups=mesh['sta'=32,'tpl'=8] {'sta'}, dimensions={0} | all-to-all | bytes 196608 | tf_op jit(solution)/shard_map/all_to_all | solution.py:297
  57.0 0.1 convert_reduce_fusion
  57.0 0.1 reshape.19
  57.1 0.7 %copy.8 = f32[48,32]{0,1:T(8,128)} copy(f32[48,32]{1,0:T(8,128)S(1)} %reshape.19) | data formatting | bytes 12288 | tf_op jit(solution)/shard_map/reshape | solution.py:299
  (7 shorter events, 0.1 us)
Async XLA Ops:
  1.2 5.0 %copy-start = (bf16[32,1,3,640]{3,0,2,1:T(8,128)(2,1)S(1)}, bf16[32,1,3,640]{3,0,2,1:T(8,128)(2,1)}, u32[]{:S(2)}) copy-start(bf16[32,1,3,640]{3,0,2,1:T(8,128)(2,1)} %param.7) | copy-start | bytes 368644
  1.2 4.9 %copy-start.1 = (s32[32,32]{1,0:T(8,128)S(1)}, s32[32,32]{1,0:T(8,128)}, u32[]{:S(2)}) copy-start(s32[32,32]{1,0:T(8,128)} %station_ref.3) | copy-start | bytes 12292
  1.2 18.3 %collective-permute-start.2 = (f32[6,32,128]{2,1,0:T(8,128)S(1)}, f32[6,32,128]{2,1,0:T(8,128)S(1)}, u32[]{:S(2)}, u32[]{:S(2)}) collective-permute-start(f32[6,32,128]{2,1,0:T(8,128)S(1)} %bitcast.9), channel_id=1, source_target_pairs={{0,6},{1,7},{2,0},{3,1},{4,2},{5,3},{6,4},{7,5},{8,14},{9,15},{10,... | collective-permute-start | bytes 294920 | tf_op jit(solution)/shard_map/ppermute | solution.py:287
  3.6 15.9 %collective-permute-start.1 = (f32[6,32,128]{2,1,0:T(8,128)S(1)}, f32[6,32,128]{2,1,0:T(8,128)S(1)}, u32[]{:S(2)}, u32[]{:S(2)}) collective-permute-start(f32[6,32,128]{2,1,0:T(8,128)S(1)} %bitcast.10), channel_id=1, source_target_pairs={{0,4},{1,5},{2,6},{3,7},{4,0},{5,1},{6,2},{7,3},{8,12},{9,13},{10,... | collective-permute-start | bytes 294920 | tf_op jit(solution)/shard_map/ppermute | solution.py:287
  4.3 15.3 %collective-permute-start = (f32[6,32,128]{2,1,0:T(8,128)S(1)}, f32[6,32,128]{2,1,0:T(8,128)S(1)}, u32[]{:S(2)}, u32[]{:S(2)}) collective-permute-start(f32[6,32,128]{2,1,0:T(8,128)S(1)} %bitcast.11), channel_id=1, source_target_pairs={{0,2},{1,3},{2,4},{3,5},{4,6},{5,7},{6,0},{7,1},{8,10},{9,11},{10,... | collective-permute-start | bytes 294920 | tf_op jit(solution)/shard_map/ppermute | solution.py:287
  8.0 28.0 %all-to-all-start = ((bf16[32,64,128]{2,1,0:T(8,128)(2,1)}), bf16[32,64,128]{2,1,0:T(8,128)(2,1)S(1)}, u32[]{:S(2)}, u32[]{:S(2)}) async-start(bf16[32,64,128]{2,1,0:T(8,128)(2,1)} %select_waves.1), calls=%async_computation | async-start | bytes 1048576 | tf_op jit(solution)/shard_map/all_to_all | solution.py:293
  19.5 1.9 %copy-start.2 = (s32[32,32]{1,0:T(8,128)S(1)}, s32[32,32]{1,0:T(8,128)}, u32[]{:S(2)}) copy-start(s32[32,32]{1,0:T(8,128)} %lag_ref.1) | copy-start | bytes 12292
  19.5 1.9 %copy-start.3 = (s32[3,16]{1,0:T(4,128)S(1)}, s32[3,16]{1,0:T(4,128)}, u32[]{:S(2)}) copy-start(s32[3,16]{1,0:T(4,128)} %mask_hbm.1) | copy-start | bytes 580
  19.6 1.8 %collective-permute-start.3 = (f32[24,32,128]{2,1,0:T(8,128)S(1)}, f32[24,32,128]{2,1,0:T(8,128)S(1)}, u32[]{:S(2)}, u32[]{:S(2)}) collective-permute-start(f32[24,32,128]{2,1,0:T(8,128)S(1)} %pad_maximum_fusion.near_ref), channel_id=1, source_target_pairs={{0,1},{1,0},{2,3},{3,2},{4,5},{5,4},{6,7},{7,6},{8,9},{9,8},{10,11... | collective-permute-start | bytes 1179656 | tf_op jit(solution)/shard_map/ppermute | solution.py:289
